TPU v7x, 256 devices: a whole 4x4x8 slice. The times are simulated.
256 devices in a mesh: set: 8 (over y_hi, x), exp: 4 (over y_lo, core), seq: 8 (over z).
Axes of the slice: x: 4, y: 4 (y_hi: 2, y_lo: 2; y = y_hi * 2 + y_lo), z: 8, core: 2. Of those that a mesh axis runs over, the one named last changes fastest.
Arguments:
- tokens: bfloat16 [12288, 2560], P(('set', 'exp', 'seq')), parts along dimension 0, may hold values from -6 to 6
- expert_ids: int32 [12288, 2], P(('set', 'exp', 'seq')), parts along dimension 0, may hold values from 0 to 3, as said below
- gate_nums: int32 [12288, 2], P(('set', 'exp', 'seq')), parts along dimension 0, may hold values from 1 to 8
- moe_gain: float32 [2560], replicated, may hold values from 0.1 to 1.9
- w_gate_up: bfloat16 [4, 2560, 2, 3584], P('exp', None, None, 'seq'), may hold values from -0.125 to 0.125
- w_down: bfloat16 [4, 3584, 2560], P('exp', 'seq'), may hold values from -0.09375 to 0.09375
- attn_gain: float32 [2560], replicated, may hold values from 0.1 to 1.9
- w_qkv: bfloat16 [2560, 3, 2048], P(None, None, 'seq'), may hold values from -0.125 to 0.125
- q_gain: float32 [128], replicated, may hold values from 1.2 to 2.2
- k_gain: float32 [128], replicated, may hold values from 1.2 to 2.2
- w_out: bfloat16 [2048, 2560], P('seq'), may hold values from -0.125 to 0.125
Outputs:
- mixed: bfloat16 [12288, 2560], P(('set', 'exp', 'seq')), parts along dimension 0
- attended: bfloat16 [12288, 2560], P(('set', 'exp', 'seq')), parts along dimension 0
There are 8 independent parts, one for each index of `set`. A program takes and returns all parts, laid end to end along the dimension named above; an argument that names none is the same for every part. Nothing has to cross between parts.
Inputs may be any that keep to these rules, and one draw needn't show every extreme that they name: `expert_ids`: the two ids of a row differ. In the rows of one device no expert is named by more than 36 rows, and one expert, the same for all devices of a set, is named by exactly 36 of them.
All inputs are finite; a program needn't handle non-finite values.
Results may differ from a plain program's by a relative error of at most 0.014.
Values may be sent and summed in bfloat16 or wider, within the bound.
No kernel may reach another device: no remote copies, remote signals or barrier semaphores. Data moves between devices by JAX's collectives and lax.ppermute only.
A program may use at most 64 MiB of HBM per device.

v0:
```python
import math

import jax
import jax.numpy as jnp
from jax import lax
from jax.experimental import pallas as pl
from jax.experimental.pallas import tpu as pltpu
from jax.sharding import Mesh
from jax.sharding import PartitionSpec as P


LANES = 128
EXP = ("exp_0", "exp_1")
SET_EXP_SEQ = ("set", "exp_0", "exp_1", "seq")


def swap(value, axis):
    return lax.ppermute(value, axis, [(0, 1), (1, 0)])


def shift(value, step):
    n = lax.axis_size("seq")
    return lax.ppermute(value, "seq", [(i, (i + step) % n) for i in range(n)])


def wide(value):
    return value.astype(jnp.float32)


def added(*values):
    total = wide(values[0])
    for v in values[1:]:
        total = total + wide(v)
    return total.astype(jnp.bfloat16)


def tied(first, second):
    return lax.optimization_barrier((first, second))


def rms_scale(values, gain):
    return values * lax.rsqrt(jnp.mean(values * values, axis=-1, keepdims=True) + 1e-06) * gain


def ring_scatter(above, below, rows):
    blank = jnp.zeros((rows, above.shape[1]), jnp.bfloat16)

    def step(i, carry):
        up, down = carry
        at_up = lax.dynamic_slice_in_dim(above, i * rows, rows)
        at_down = lax.dynamic_slice_in_dim(below, i * rows, rows)
        return shift(added(at_up, up), 1), shift(added(at_down, down), -1)

    return lax.fori_loop(0, above.shape[0] // rows, step, (blank, blank))


ANY = pl.BlockSpec(memory_space=pl.ANY)


TRANS = (((1,), (1,)), ((), ()))


def expert_call(mine, other, w_gate_up, w_down, me):
    n = len(mine)
    plane = mine[0].shape[0]
    half = plane // 2
    _, fb, dim = w_gate_up.shape
    ff = 2 * fb
    cols = mine[0].shape[1]
    m1 = n * plane
    m = 2 * m1
    kc = 512
    nk = dim // kc

    def kernel(me_ref, *refs):
        xs, (ox, wgu, wd, out_mine, out_other) = refs[:n], refs[n : n + 5]
        x_s, wgu_s, wd_s, acc, h_s, sh_s, sx, sg, sd = refs[n + 5 :]

        def w_copy(k):
            return pltpu.make_async_copy(wgu.at[k], wgu_s.at[k], sg.at[k])

        copies = []
        for i in range(n):
            for b in range(2):
                src = pl.ds(b * half, half)
                dst = (b * n + i) * half
                copies.append(
                    pltpu.make_async_copy(
                        xs[i].at[src], x_s.at[pl.ds(dst, half)], sx.at[0, 2 * i + b]
                    )
                )
                src = pl.ds(i * plane + b * half, half)
                copies.append(
                    pltpu.make_async_copy(
                        ox.at[src], x_s.at[pl.ds(m1 + dst, half)], sx.at[1, 2 * i + b]
                    )
                )
        d_copy = pltpu.make_async_copy(wd, wd_s, sd)
        for c in copies:
            c.start()
        for k in range(4):
            w_copy(k).start()
        d_copy.start()
        for c in copies:
            c.wait()
        nums = x_s[:, dim:].astype(jnp.float32)
        here = lax.broadcasted_iota(jnp.int32, nums.shape, 1) == me_ref[0]
        share = jnp.sum(jnp.where(here, nums, 0.0), axis=1, keepdims=True) / jnp.sum(
            nums, axis=1, keepdims=True
        )
        sh_s[...] = jnp.broadcast_to(share, sh_s.shape)

        def step(k, carry):
            w_copy(k).wait()
            acc[k] = lax.dot_general(
                x_s[:, :dim], wgu_s[k], TRANS, preferred_element_type=jnp.float32
            )
            return carry

        lax.fori_loop(0, 4, step, 0)
        for b in range(2):
            gate = acc[b]
            h_s[b] = (gate / (1.0 + jnp.exp(-gate)) * acc[2 + b]).astype(jnp.bfloat16)
        d_copy.wait()

        def down(k, carry):
            at = pl.ds(pl.multiple_of(k * kc, kc), kc)
            y = jnp.dot(h_s[0], wd_s[0, :, at], preferred_element_type=jnp.float32) + jnp.dot(
                h_s[1], wd_s[1, :, at], preferred_element_type=jnp.float32
            )
            y = (y * sh_s[:, :1]).astype(jnp.bfloat16)
            out_mine[:, at] = y[:m1]
            out_other[:, at] = y[m1:]
            return carry

        lax.fori_loop(0, nk, down, 0)

    return pl.pallas_call(
        kernel,
        out_shape=[jax.ShapeDtypeStruct((m1, dim), jnp.bfloat16)] * 2,
        in_specs=[pl.BlockSpec(memory_space=pltpu.SMEM)] + [ANY] * (n + 3),
        out_specs=[pl.BlockSpec(memory_space=pltpu.VMEM)] * 2,
        scratch_shapes=[
            pltpu.VMEM((m, cols), jnp.bfloat16),
            pltpu.VMEM((4, fb, dim), jnp.bfloat16),
            pltpu.VMEM((2, fb, dim), jnp.bfloat16),
            pltpu.VMEM((4, m, fb), jnp.float32),
            pltpu.VMEM((2, m, fb), jnp.bfloat16),
            pltpu.VMEM((m, LANES), jnp.float32),
            pltpu.SemaphoreType.DMA((2, 2 * n)),
            pltpu.SemaphoreType.DMA((4,)),
            pltpu.SemaphoreType.DMA,
        ],
        compiler_params=pltpu.CompilerParams(vmem_limit_bytes=(10 + 5 * n) * 2**20),
        cost_estimate=pl.CostEstimate(
            flops=6 * m * dim * ff, bytes_accessed=6 * dim * ff + 4 * m * dim, transcendentals=m * ff
        ),
        name="expert",
    )(me, *mine, other, w_gate_up, w_down)


def project_call(parts, w, q_gain, k_gain, heads):
    n = len(parts)
    sizes = [p.shape[0] for p in parts]
    m = sum(sizes)
    cols, dim = w.shape
    width = cols // 3
    head = width // heads
    kc = 512
    nk = dim // kc

    def kernel(*refs):
        xs, (w_ref, qg, kg, q_out, kv_out, x_s, w_s, acc, sx, sw) = refs[:n], refs[n:]

        def x_copy(i):
            return pltpu.make_async_copy(
                xs[i], x_s.at[pl.ds(sum(sizes[:i]), sizes[i])], sx.at[i]
            )

        def w_copy(k):
            at = pl.ds(pl.multiple_of(k * kc, kc), kc)
            return pltpu.make_async_copy(w_ref.at[:, at], w_s.at[:, at], sw.at[k])

        for i in range(n):
            x_copy(i).start()
        for k in range(nk):
            w_copy(k).start()
        acc[...] = jnp.zeros_like(acc)
        for i in range(n):
            x_copy(i).wait()

        def step(k, carry):
            at = pl.ds(pl.multiple_of(k * kc, kc), kc)
            w_copy(k).wait()
            acc[...] += lax.dot_general(
                x_s[:, at], w_s[:, at], TRANS, preferred_element_type=jnp.float32
            )
            return carry

        lax.fori_loop(0, nk, step, 0)
        for i in range(heads):
            at = slice(i * head, (i + 1) * head)
            q_out[:, at] = rms_scale(acc[:, at], qg[...]).astype(jnp.bfloat16)
            at_k = slice(width + i * head, width + (i + 1) * head)
            kv_out[:, at] = rms_scale(acc[:, at_k], kg[...]).astype(jnp.bfloat16)
        kv_out[:, width:] = acc[:, 2 * width :].astype(jnp.bfloat16)

    vmem = pl.BlockSpec(memory_space=pltpu.VMEM)
    return pl.pallas_call(
        kernel,
        out_shape=[
            jax.ShapeDtypeStruct((m, width), jnp.bfloat16),
            jax.ShapeDtypeStruct((m, 2 * width), jnp.bfloat16),
        ],
        in_specs=[ANY] * (n + 1) + [vmem, vmem],
        out_specs=[vmem, vmem],
        scratch_shapes=[
            pltpu.VMEM((m, dim), jnp.bfloat16),
            pltpu.VMEM((cols, dim), jnp.bfloat16),
            pltpu.VMEM((m, cols), jnp.float32),
            pltpu.SemaphoreType.DMA((n,)),
            pltpu.SemaphoreType.DMA((nk,)),
        ],
        compiler_params=pltpu.CompilerParams(vmem_limit_bytes=16 * 2**20),
        cost_estimate=pl.CostEstimate(
            flops=2 * m * dim * cols, bytes_accessed=2 * dim * cols + 2 * m * dim, transcendentals=0
        ),
        name="project",
    )(*parts, w, q_gain.reshape(1, -1), k_gain.reshape(1, -1))


def attend_call(queries, kvs, w_out, heads, rows):
    nq, nv = len(queries), len(kvs)
    m = sum(q.shape[0] for q in queries)
    t = sum(k.shape[0] for k in kvs)
    width = queries[0].shape[1]
    head = width // heads
    dim = w_out.shape[1]
    planes = m // rows
    scale_factor = 1.0 / math.sqrt(head)

    def kernel(*refs):
        qs, ks, w_ref = refs[:nq], refs[nq : nq + nv], refs[nq + nv]
        outs = refs[nq + nv + 1 : nq + nv + 1 + planes]
        q_s, kv_s, w_s, o_s, sq, sk, sw = refs[nq + nv + 1 + planes :]
        copies = []
        at = 0
        for i, k in enumerate(ks):
            copies.append(pltpu.make_async_copy(k, kv_s.at[pl.ds(at, k.shape[0])], sk.at[i]))
            at += k.shape[0]
        at = 0
        for i, q in enumerate(qs):
            copies.append(pltpu.make_async_copy(q, q_s.at[pl.ds(at, q.shape[0])], sq.at[i]))
            at += q.shape[0]
        w_copy = pltpu.make_async_copy(w_ref, w_s, sw)
        for c in copies:
            c.start()
        w_copy.start()
        for c in copies:
            c.wait()
        block = 128

        def rows_step(b, carry):
            r = pl.ds(pl.multiple_of(b * block, block), block)
            for i in range(heads):
                at = slice(i * head, (i + 1) * head)
                scores = (
                    lax.dot_general(
                        q_s[r, at], kv_s[:, at], TRANS, preferred_element_type=jnp.float32
                    )
                    * scale_factor
                )
                probs = jnp.exp(scores)
                denom = jnp.sum(probs, axis=1, keepdims=True)
                num = jnp.dot(
                    probs.astype(jnp.bfloat16),
                    kv_s[:, width + i * head : width + (i + 1) * head],
                    preferred_element_type=jnp.float32,
                )
                o_s[r, at] = (num / denom).astype(jnp.bfloat16)
            return carry

        lax.fori_loop(0, m // block, rows_step, 0)
        w_copy.wait()
        kc = 512

        def out_step(k, carry):
            cols = pl.ds(pl.multiple_of(k * kc, kc), kc)
            y = jnp.dot(o_s[...], w_s[:, cols], preferred_element_type=jnp.float32)
            y = y.astype(jnp.bfloat16)
            for i in range(planes):
                outs[i][:, cols] = y[i * rows : (i + 1) * rows]
            return carry

        lax.fori_loop(0, dim // kc, out_step, 0)

    return pl.pallas_call(
        kernel,
        out_shape=[jax.ShapeDtypeStruct((rows, dim), jnp.bfloat16)] * planes,
        in_specs=[ANY] * (nq + nv + 1),
        out_specs=[pl.BlockSpec(memory_space=pltpu.VMEM)] * planes,
        scratch_shapes=[
            pltpu.VMEM((m, width), jnp.bfloat16),
            pltpu.VMEM((t, 2 * width), jnp.bfloat16),
            pltpu.VMEM(w_out.shape, jnp.bfloat16),
            pltpu.VMEM((m, width), jnp.bfloat16),
            pltpu.SemaphoreType.DMA((nq,)),
            pltpu.SemaphoreType.DMA((nv,)),
            pltpu.SemaphoreType.DMA,
        ],
        compiler_params=pltpu.CompilerParams(vmem_limit_bytes=32 * 2**20),
        cost_estimate=pl.CostEstimate(
            flops=4 * m * t * width + 2 * m * width * dim,
            bytes_accessed=2 * (t * 2 * width + width * dim + m * dim),
            transcendentals=m * t * heads,
        ),
        name="attend",
    )(*queries, *kvs, w_out)


def shards(
    tokens,
    expert_ids,
    gate_nums,
    moe_gain,
    w_gate_up,
    w_down,
    attn_gain,
    w_qkv,
    q_gain,
    k_gain,
    w_out,
):
    rows, dim = tokens.shape
    me = (lax.axis_index("exp_0") * 2 + lax.axis_index("exp_1")).reshape(1).astype(jnp.int32)
    w_down0 = w_down[0].reshape(2, -1, dim)

    tokens_wide = wide(tokens)
    normed = rms_scale(tokens_wide, moe_gain).astype(jnp.bfloat16)
    lane = lax.broadcasted_iota(jnp.int32, (rows, LANES), 1)
    numer = jnp.where(expert_ids[:, :1] == lane, gate_nums[:, :1], 0) + jnp.where(
        expert_ids[:, 1:] == lane, gate_nums[:, 1:], 0
    )
    packed = jnp.concatenate([normed, numer.astype(jnp.bfloat16)], axis=1)

    column = jnp.concatenate([packed, swap(packed, "exp_0")], 0)
    w_gu = w_gate_up[0].transpose(1, 2, 0).reshape(4, -1, dim)
    w_qkv2 = w_qkv.transpose(1, 2, 0).reshape(-1, dim)

    def experts(planes):
        other = swap(jnp.concatenate(planes, 0) if len(planes) > 1 else planes[0], "exp_1")
        mine, theirs = expert_call(planes, other, w_gu, w_down0, me)
        chip = added(mine, swap(theirs, "exp_1"))
        cut = rows * len(planes)
        across = swap(chip[cut:], "exp_0")
        return [
            (chip[i * rows : (i + 1) * rows], across[i * rows : (i + 1) * rows])
            for i in range(len(planes))
        ]

    up1, down1 = shift(column, 1), shift(column, -1)
    (up1, down1), (w_gu, w_qkv2) = tied((up1, down1), (w_gu, w_qkv2))
    up2, down2 = shift(up1, 1), shift(down1, -1)
    own_terms, b1, a1 = experts([column, up1, down1])
    up3, down3 = shift(up2, 1), shift(down2, -1)
    b2, a2 = experts([up2, down2])
    far_up, far_down = shift(up3[:rows], 1), shift(down3[rows:], -1)
    b3, a3 = experts([up3, down3])
    (far_terms,) = experts([jnp.concatenate([far_up, far_down], 0)])
    above = jnp.concatenate([added(*t) for t in (far_terms, a3, a2, a1)], 0)
    blank = jnp.zeros((rows, dim), jnp.bfloat16)
    below = jnp.concatenate([blank, *(added(*t) for t in (b3, b2, b1))], 0)
    from_below, from_above = ring_scatter(above, below, rows)
    moe_total = wide(own_terms[0]) + wide(own_terms[1]) + wide(from_below) + wide(from_above)
    mixed = (tokens_wide + moe_total).astype(jnp.bfloat16)

    mixed_wide = wide(mixed)
    attn_in = rms_scale(mixed_wide, attn_gain).astype(jnp.bfloat16)
    head = q_gain.shape[0]
    heads = w_qkv.shape[2] // head

    def project(parts):
        q, kv = project_call(parts, w_qkv2, q_gain, k_gain, heads)
        beside = swap(kv, "exp_0")
        return q, jnp.concatenate([kv, beside], 0)

    half = rows // 2
    up1, down1 = shift(attn_in, 1), shift(attn_in, -1)
    up2, down2 = shift(up1, 1), shift(down1, -1)
    up3, down3 = shift(up2, 1), shift(down2, -1)
    q_a, kv_a = project([attn_in, up1, down1, up2, down2])
    far = (shift(up3[:half], 1), shift(down3[half:], -1))
    kv_a = lax.all_gather(kv_a, "exp_1", axis=0, tiled=True)
    far, kv_a = tied(far, kv_a)
    q_b, kv_b = project([up3, down3, jnp.concatenate(far, 0)])
    kvs = [kv_a, kv_b, swap(kv_b, "exp_1")]
    piece = attend_call([q_a, q_b], kvs, w_out, heads, rows)
    from_below, from_above = ring_scatter(
        jnp.concatenate([piece[7], *piece[6:1:-2]], 0),
        jnp.concatenate([blank, *piece[5:0:-2]], 0),
        rows,
    )
    attended = (
        mixed_wide + (wide(piece[0]) + wide(from_below) + wide(from_above))
    ).astype(jnp.bfloat16)
    return (mixed, attended)


def solution(mesh):
    torus = Mesh(
        mesh.devices.reshape(mesh.shape["set"], 2, 2, mesh.shape["seq"]),
        ("set", "exp_0", "exp_1", "seq"),
    )
    in_specs = (
        P(SET_EXP_SEQ, None),
        P(SET_EXP_SEQ, None),
        P(SET_EXP_SEQ, None),
        P(),
        P(EXP, None, None, "seq"),
        P(EXP, "seq", None),
        P(),
        P(None, None, "seq"),
        P(),
        P(),
        P("seq", None),
    )
    out_specs = (P(SET_EXP_SEQ, None), P(SET_EXP_SEQ, None))

    return jax.shard_map(shards, mesh=torus, in_specs=in_specs, out_specs=out_specs, check_vma=False)
```

profile of v0, /device:TPU:1, one launch (start us, length us, event | category | flops | bytes accessed | tf_op | source)
XLA Modules:
  0.0 275.0 jit_solution(8825946471679856192)
XLA Ops:
  3.7 2.2 collective-permute-start.4
  5.9 4.8 %collective-permute-done.4 = bf16[48,2688]{1,0:T(8,128)(2,1)S(1)} collective-permute-done((bf16[48,2688]{1,0:T(8,128)(2,1)S(1)}, bf16[48,2688]{1,0:T(8,128)(2,1)S(1)}, u32[]{:S(2)}, u32[]{:S(2)}) %collective-permute-start.4) | collective-permute-done | bytes 258080 | tf_op jit(solution)/shard_map/ppermute | solution.py:18
  10.7 2.8 %collective-permute-start.5 = (bf16[96,2688]{1,0:T(8,128)(2,1)S(1)}, bf16[96,2688]{1,0:T(8,128)(2,1)S(1)}, u32[]{:S(2)}, u32[]{:S(2)}) collective-permute-start(bf16[96,2688]{1,0:T(8,128)(2,1)S(1)} %pad_maximum_fusion.7.refs_0_), channel_id=1, source_target_pairs={{0,1},{1,2},{2,3},{3,4},{4,5},{5,6},{6,7},{7,0},{8,9},{9,10},{10,1... | collective-permute-start | bytes 1548296 | tf_op jit(solution)/shard_map/ppermute | solution.py:23
  13.5 4.0 %collective-permute-start.6 = (bf16[96,2688]{1,0:T(8,128)(2,1)S(1)}, bf16[96,2688]{1,0:T(8,128)(2,1)S(1)}, u32[]{:S(2)}, u32[]{:S(2)}) collective-permute-start(bf16[96,2688]{1,0:T(8,128)(2,1)S(1)} %pad_maximum_fusion.7.refs_0_), channel_id=1, source_target_pairs={{0,7},{1,0},{2,1},{3,2},{4,3},{5,4},{6,5},{7,6},{8,15},{9,8},{10,9... | collective-permute-start | bytes 1548296 | tf_op jit(solution)/shard_map/ppermute | solution.py:23
  17.5 6.3 %copy.13 = bf16[3,256,2560]{2,1,0:T(8,128)(2,1)} copy(bf16[3,256,2560]{1,2,0:T(8,128)(2,1)} %bitcast.35) | data formatting | bytes 7864320 | tf_op jit(solution)/shard_map/transpose | solution.py:348
  23.8 4.2 %collective-permute-done.5.refs_1_ = bf16[96,2688]{1,0:T(8,128)(2,1)S(1)} collective-permute-done((bf16[96,2688]{1,0:T(8,128)(2,1)S(1)}, bf16[96,2688]{1,0:T(8,128)(2,1)S(1)}, u32[]{:S(2)}, u32[]{:S(2)}) %collective-permute-start.5) | collective-permute-done | bytes 516128 | tf_op jit(solution)/shard_map/ppermute | solution.py:23
  28.1 2.7 collective-permute-start.13
  30.8 9.7 %collective-permute-done.10.refs_0_ = bf16[96,2688]{1,0:T(8,128)(2,1)S(1)} collective-permute-done((bf16[96,2688]{1,0:T(8,128)(2,1)S(1)}, bf16[96,2688]{1,0:T(8,128)(2,1)S(1)}, u32[]{:S(2)}, u32[]{:S(2)}) %collective-permute-start.10) | collective-permute-done | bytes 516128 | tf_op jit(solution)/shard_map/ppermute | solution.py:23
  40.5 2.7 collective-permute-start.14
  44.5 3.5 %collective-permute-start.7 = (bf16[288,2688]{1,0:T(8,128)(2,1)}, bf16[288,2688]{1,0:T(8,128)(2,1)}, u32[]{:S(2)}, u32[]{:S(2)}) collective-permute-start(bf16[288,2688]{1,0:T(8,128)(2,1)} %pad_maximum_fusion), channel_id=1, source_target_pairs={{0,8},{8,0},{1,9},{9,1},{2,10},{10,2},{3,11},{11,3},{4,12},{12,4},... | collective-permute-start | bytes 4644872 | tf_op jit(solution)/shard_map/ppermute | solution.py:18
  49.0 3.0 %collective-permute-done.11.refs_0_ = bf16[96,2688]{1,0:T(8,128)(2,1)S(1)} collective-permute-done((bf16[96,2688]{1,0:T(8,128)(2,1)S(1)}, bf16[96,2688]{1,0:T(8,128)(2,1)S(1)}, u32[]{:S(2)}, u32[]{:S(2)}) %collective-permute-start.11) | collective-permute-done | bytes 516128 | tf_op jit(solution)/shard_map/ppermute | solution.py:23
  53.4 3.8 %collective-permute-start.19 = (bf16[192,2688]{1,0:T(8,128)(2,1)}, bf16[192,2688]{1,0:T(8,128)(2,1)}, u32[]{:S(2)}, u32[]{:S(2)}) collective-permute-start(bf16[192,2688]{1,0:T(8,128)(2,1)} %pad_maximum_fusion.3), channel_id=1, source_target_pairs={{0,8},{8,0},{1,9},{9,1},{2,10},{10,2},{3,11},{11,3},{4,12},{12,4},... | collective-permute-start | bytes 3096584 | tf_op jit(solution)/shard_map/ppermute | solution.py:18
  57.2 3.0 %collective-permute-start.15 = (bf16[48,2688]{1,0:T(8,128)(2,1)S(1)}, bf16[48,2688]{1,0:T(8,128)(2,1)S(1)}, u32[]{:S(2)}, u32[]{:S(2)}) collective-permute-start(bf16[48,2688]{1,0:T(8,128)(2,1)S(1)} %slice.112), channel_id=1, source_target_pairs={{0,7},{1,0},{2,1},{3,2},{4,3},{5,4},{6,5},{7,6},{8,15},{9,8},{10,9... | collective-permute-start | bytes 774152 | tf_op jit(solution)/shard_map/ppermute | solution.py:23
  60.2 5.5 %collective-permute-done.15 = bf16[48,2688]{1,0:T(8,128)(2,1)S(1)} collective-permute-done((bf16[48,2688]{1,0:T(8,128)(2,1)S(1)}, bf16[48,2688]{1,0:T(8,128)(2,1)S(1)}, u32[]{:S(2)}, u32[]{:S(2)}) %collective-permute-start.15) | collective-permute-done | bytes 258080 | tf_op jit(solution)/shard_map/ppermute | solution.py:23
  66.8 2.3 copy-done.2
  71.1 7.7 %expert.7 = (bf16[192,2560]{1,0:T(8,128)(2,1)S(1)}, bf16[192,2560]{1,0:T(8,128)(2,1)S(1)}) custom-call(s32[1]{0:T(128)} %bitcast.me_ref, bf16[96,2688]{1,0:T(8,128)(2,1)S(1)} %copy-done.11, bf16[96,2688]{1,0:T(8,128)(2,1)S(1)} %copy-done.13, bf16[192,2688]{1,0:T(8,128)(2,1)} %collective-permute-done.22.refs_2_, bf16[4,224,2560]{2,1,0:T(8,128)(2,1)S(1)} %bitcast.21, ...), custom_call_target="tpu_custom_call" | custom-call | flops 2642411520 | bytes 10813440 | tf_op jit(solution)/shard_map/expert/pallas_call | solution.py:138
  79.2 5.5 %expert.5 = (bf16[96,2560]{1,0:T(8,128)(2,1)S(1)}, bf16[96,2560]{1,0:T(8,128)(2,1)S(1)}) custom-call(s32[1]{0:T(128)} %bitcast.me_ref, bf16[96,2688]{1,0:T(8,128)(2,1)S(1)} %constant_dynamic-update-slice_fusion.refs_0_, bf16[96,2688]{1,0:T(8,128)(2,1)} %collective-permute-done.16.refs_1_, bf16[4,224,2560]{2,1,0:T(8,128)(2,1)S(1)} %bitcast.24, ...), custom_call_target="tpu_custom_call" | custom-call | flops 1321205760 | bytes 8847360 | tf_op jit(solution)/shard_map/expert/pallas_call | solution.py:138
  85.3 10.1 %expert.4 = (bf16[288,2560]{1,0:T(8,128)(2,1)S(1)}, bf16[288,2560]{1,0:T(8,128)(2,1)S(1)}) custom-call(s32[1]{0:T(128)} %bitcast.me_ref, bf16[96,2688]{1,0:T(8,128)(2,1)S(1)} %copy-done.9, bf16[96,2688]{1,0:T(8,128)(2,1)S(1)} %copy-done.15, bf16[96,2688]{1,0:T(8,128)(2,1)S(1)} %copy-done.17, bf16[288,2688]{1,0:T(8,128)(2,1)} %collective-permute-done.7.refs_3_, ...), custom_call_target="tpu_custom_call" | custom-call | flops 3963617280 | bytes 12779520 | tf_op jit(solution)/shard_map/expert/pallas_call | solution.py:138
  95.6 7.7 %expert.6 = (bf16[192,2560]{1,0:T(8,128)(2,1)S(1)}, bf16[192,2560]{1,0:T(8,128)(2,1)S(1)}) custom-call(s32[1]{0:T(128)} %bitcast.me_ref, bf16[96,2688]{1,0:T(8,128)(2,1)S(1)} %copy-done.5, bf16[96,2688]{1,0:T(8,128)(2,1)S(1)} %copy-done.7, bf16[192,2688]{1,0:T(8,128)(2,1)} %collective-permute-done.19.refs_2_, bf16[4,224,2560]{2,1,0:T(8,128)(2,1)S(1)} %bitcast.26, ...), custom_call_target="tpu_custom_call" | custom-call | flops 2642411520 | bytes 10813440 | tf_op jit(solution)/shard_map/expert/pallas_call | solution.py:138
  105.8 5.6 %collective-permute-done.18 = bf16[48,2560]{1,0:T(8,128)(2,1)S(1)} collective-permute-done((bf16[48,2560]{1,0:T(8,128)(2,1)S(1)}, bf16[48,2560]{1,0:T(8,128)(2,1)S(1)}, u32[]{:S(2)}, u32[]{:S(2)}) %collective-permute-start.18) | collective-permute-done | bytes 245792 | tf_op jit(solution)/shard_map/ppermute | solution.py:18
  113.9 8.1 %collective-permute-done.24 = bf16[96,2560]{1,0:T(8,128)(2,1)S(1)} collective-permute-done((bf16[96,2560]{1,0:T(8,128)(2,1)S(1)}, bf16[96,2560]{1,0:T(8,128)(2,1)S(1)}, u32[]{:S(2)}, u32[]{:S(2)}) %collective-permute-start.24) | collective-permute-done | bytes 491552 | tf_op jit(solution)/shard_map/ppermute | solution.py:18
  122.1 26.2 %collective-permute-done.21 = bf16[96,2560]{1,0:T(8,128)(2,1)S(1)} collective-permute-done((bf16[96,2560]{1,0:T(8,128)(2,1)S(1)}, bf16[96,2560]{1,0:T(8,128)(2,1)S(1)}, u32[]{:S(2)}, u32[]{:S(2)}) %collective-permute-start.21) | collective-permute-done | bytes 491552 | tf_op jit(solution)/shard_map/ppermute | solution.py:18
  150.5 33.5 %while.30 = (s32[]{:T(128)}, bf16[48,2560]{1,0:T(8,128)(2,1)S(1)}, bf16[48,2560]{1,0:T(8,128)(2,1)S(1)}, bf16[192,2560]{1,0:T(8,128)(2,1)S(1)}, bf16[192,2560]{1...) while((s32[]{:T(128)}, bf16[48,2560]{1,0:T(8,128)(2,1)S(1)}, ...), condition=%wide.region_2.3_spmd, body=%wide.region_1.2_spmd.sunk | while | flops 983046 | bytes 3440867 | solution.py:54
  152.5 2.6 collective-permute-start.1
  155.1 4.3 %collective-permute-done = bf16[48,2560]{1,0:T(8,128)(2,1)S(1)} collective-permute-done((bf16[48,2560]{1,0:T(8,128)(2,1)S(1)}, bf16[48,2560]{1,0:T(8,128)(2,1)S(1)}, u32[]{:S(2)}, u32[]{:S(2)}) %collective-permute-start) | collective-permute-done | bytes 245792 | tf_op jit(solution)/shard_map/while/body/eval_jaxpr/ppermute | solution.py:23
  159.6 2.3 collective-permute-start
  164.2 3.4 %collective-permute-done = bf16[48,2560]{1,0:T(8,128)(2,1)S(1)} collective-permute-done((bf16[48,2560]{1,0:T(8,128)(2,1)S(1)}, bf16[48,2560]{1,0:T(8,128)(2,1)S(1)}, u32[]{:S(2)}, u32[]{:S(2)}) %collective-permute-start) | collective-permute-done | bytes 245792 | tf_op jit(solution)/shard_map/while/body/eval_jaxpr/ppermute | solution.py:23
  172.3 2.5 collective-permute-done
  180.1 2.5 collective-permute-done
  188.3 3.6 %collective-permute-done.25.refs_1_ = bf16[48,2560]{1,0:T(8,128)(2,1)S(1)} collective-permute-done((bf16[48,2560]{1,0:T(8,128)(2,1)S(1)}, bf16[48,2560]{1,0:T(8,128)(2,1)S(1)}, u32[]{:S(2)}, u32[]{:S(2)}) %collective-permute-start.25) | collective-permute-done | bytes 245792 | tf_op jit(solution)/shard_map/ppermute | solution.py:23
  192.4 2.1 collective-permute-start.28
  194.6 5.9 %collective-permute-done.27.refs_3_ = bf16[48,2560]{1,0:T(8,128)(2,1)S(1)} collective-permute-done((bf16[48,2560]{1,0:T(8,128)(2,1)S(1)}, bf16[48,2560]{1,0:T(8,128)(2,1)S(1)}, u32[]{:S(2)}, u32[]{:S(2)}) %collective-permute-start.27) | collective-permute-done | bytes 245792 | tf_op jit(solution)/shard_map/ppermute | solution.py:23
  200.5 3.2 %collective-permute-start.30 = (bf16[48,2560]{1,0:T(8,128)(2,1)S(1)}, bf16[48,2560]{1,0:T(8,128)(2,1)S(1)}, u32[]{:S(2)}, u32[]{:S(2)}) collective-permute-start(bf16[48,2560]{1,0:T(8,128)(2,1)S(1)} %collective-permute-done.28.refs_4_), channel_id=1, source_target_pairs={{0,7},{1,0},{2,1},{3,2},{4,3},{5,4},{6,5},{7,6},{8,15},{9,8},{10,9... | collective-permute-start | bytes 737288 | tf_op jit(solution)/shard_map/ppermute | solution.py:23
  205.8 4.2 %project.2 = (bf16[240,256]{1,0:T(8,128)(2,1)S(1)}, bf16[240,512]{1,0:T(8,128)(2,1)S(1)}) custom-call(bf16[48,2560]{1,0:T(8,128)(2,1)S(1)} %fusion.10.refs_0_, bf16[48,2560]{1,0:T(8,128)(2,1)S(1)} %collective-permute-done.25.refs_1_, bf16[48,2560]{1,0:T(8,128)(2,1)S(1)} %collective-permute-done.26.refs_2_, ...), custom_call_target="tpu_custom_call" | custom-call | flops 943718400 | bytes 5160960 | tf_op jit(solution)/shard_map/project/pallas_call | solution.py:209
  211.5 2.7 collective-permute-start.32
  215.4 12.9 %all_gather.3.refs_2_ = bf16[960,512]{1,0:T(8,128)(2,1)S(1)} all-gather(bf16[480,512]{1,0:T(8,128)(2,1)S(1)} %pad_maximum_fusion.8), channel_id=1, replica_groups=mesh['set'=8,'exp_0'=2,'exp_1'=2,'seq'=8] {'exp_1'}, dimensions={0}, use_global_device_ids=true | all-gather | bytes 1474560 | tf_op jit(solution)/shard_map/all_gather | solution.py:393
  228.3 3.5 %project.3 = (bf16[144,256]{1,0:T(8,128)(2,1)S(1)}, bf16[144,512]{1,0:T(8,128)(2,1)S(1)}) custom-call(bf16[48,2560]{1,0:T(8,128)(2,1)S(1)} %collective-permute-done.29.refs_0_, bf16[48,2560]{1,0:T(8,128)(2,1)S(1)} %collective-permute-done.30.refs_1_, bf16[48,2560]{1,0:T(8,128)(2,1)S(1)} %pad_maximum_fusion.10.refs_2_, bf16[768,2560]{1,0:T(8,128)(2,1)S(1)} %bitcast.20, ...), custom_call_target="tpu_custom_call" | custom-call | flops 566231040 | bytes 4669440 | tf_op jit(solution)/shard_map/project/pallas_call | solution.py:209
  233.2 3.7 %collective-permute-done.34 = bf16[144,512]{1,0:T(8,128)(2,1)S(1)} collective-permute-done((bf16[144,512]{1,0:T(8,128)(2,1)S(1)}, bf16[144,512]{1,0:T(8,128)(2,1)S(1)}, u32[]{:S(2)}, u32[]{:S(2)}) %collective-permute-start.34) | collective-permute-done | bytes 147488 | tf_op jit(solution)/shard_map/ppermute | solution.py:18
  239.5 4.2 %attend.1 = (bf16[48,2560]{1,0:T(8,128)(2,1)S(1)}, bf16[48,2560]{1,0:T(8,128)(2,1)S(1)}, bf16[48,2560]{1,0:T(8,128)(2,1)S(1)}, bf16[48,2560]{1,0:T(8,128)(2,1)S(...) custom-call(bf16[240,256]{1,0:T(8,128)(2,1)S(1)} %get-tuple-element., ...), custom_call_target="tpu_custom_call" | custom-call | flops 1107296256 | bytes 4849664 | tf_op jit(solution)/shard_map/attend/pallas_call | solution.py:297
  244.7 29.5 %while.31 = (s32[]{:T(128)}, bf16[48,2560]{1,0:T(8,128)(2,1)S(1)}, bf16[48,2560]{1,0:T(8,128)(2,1)S(1)}, bf16[192,2560]{1,0:T(8,128)(2,1)S(1)}, bf16[192,2560]{1...) while((s32[]{:T(128)}, bf16[48,2560]{1,0:T(8,128)(2,1)S(1)}, ...), condition=%wide.region_5.6_spmd, body=%wide.region_4.5_spmd.sunk | while | flops 983046 | bytes 3440867 | solution.py:54
  244.9 2.7 collective-permute-start.3
  247.7 5.6 %collective-permute-done.2 = bf16[48,2560]{1,0:T(8,128)(2,1)S(1)} collective-permute-done((bf16[48,2560]{1,0:T(8,128)(2,1)S(1)}, bf16[48,2560]{1,0:T(8,128)(2,1)S(1)}, u32[]{:S(2)}, u32[]{:S(2)}) %collective-permute-start.2) | collective-permute-done | bytes 245792 | tf_op jit(solution)/shard_map/while/body/eval_jaxpr/ppermute | solution.py:23
  253.5 2.7 collective-permute-start.3
  256.2 4.7 %collective-permute-done.2 = bf16[48,2560]{1,0:T(8,128)(2,1)S(1)} collective-permute-done((bf16[48,2560]{1,0:T(8,128)(2,1)S(1)}, bf16[48,2560]{1,0:T(8,128)(2,1)S(1)}, u32[]{:S(2)}, u32[]{:S(2)}) %collective-permute-start.2) | collective-permute-done | bytes 245792 | tf_op jit(solution)/shard_map/while/body/eval_jaxpr/ppermute | solution.py:23
  261.1 2.7 collective-permute-start.3
  263.9 3.9 %collective-permute-done.2 = bf16[48,2560]{1,0:T(8,128)(2,1)S(1)} collective-permute-done((bf16[48,2560]{1,0:T(8,128)(2,1)S(1)}, bf16[48,2560]{1,0:T(8,128)(2,1)S(1)}, u32[]{:S(2)}, u32[]{:S(2)}) %collective-permute-start.2) | collective-permute-done | bytes 245792 | tf_op jit(solution)/shard_map/while/body/eval_jaxpr/ppermute | solution.py:23
  268.0 2.7 collective-permute-start.3
  270.7 3.4 %collective-permute-done.2 = bf16[48,2560]{1,0:T(8,128)(2,1)S(1)} collective-permute-done((bf16[48,2560]{1,0:T(8,128)(2,1)S(1)}, bf16[48,2560]{1,0:T(8,128)(2,1)S(1)}, u32[]{:S(2)}, u32[]{:S(2)}) %collective-permute-start.2) | collective-permute-done | bytes 245792 | tf_op jit(solution)/shard_map/while/body/eval_jaxpr/ppermute | solution.py:23
  (180 shorter events, 50.2 us)
Async XLA Ops:
  3.7 7.0 %collective-permute-start.4 = (bf16[48,2688]{1,0:T(8,128)(2,1)S(1)}, bf16[48,2688]{1,0:T(8,128)(2,1)S(1)}, u32[]{:S(2)}, u32[]{:S(2)}) collective-permute-start(bf16[48,2688]{1,0:T(8,128)(2,1)S(1)} %pad_maximum_fusion.9), channel_id=1, source_target_pairs={{0,16},{16,0},{1,17},{17,1},{2,18},{18,2},{3,19},{19,3},{4,20},{20... | collective-permute-start | bytes 774152 | tf_op jit(solution)/shard_map/ppermute | solution.py:18
  10.7 17.3 %collective-permute-start.5 = (bf16[96,2688]{1,0:T(8,128)(2,1)S(1)}, bf16[96,2688]{1,0:T(8,128)(2,1)S(1)}, u32[]{:S(2)}, u32[]{:S(2)}) collective-permute-start(bf16[96,2688]{1,0:T(8,128)(2,1)S(1)} %pad_maximum_fusion.7.refs_0_), channel_id=1, source_target_pairs={{0,1},{1,2},{2,3},{3,4},{4,5},{5,6},{6,7},{7,0},{8,9},{9,10},{10,1... | collective-permute-start | bytes 1548296 | tf_op jit(solution)/shard_map/ppermute | solution.py:23
  13.5 14.5 %collective-permute-start.6 = (bf16[96,2688]{1,0:T(8,128)(2,1)S(1)}, bf16[96,2688]{1,0:T(8,128)(2,1)S(1)}, u32[]{:S(2)}, u32[]{:S(2)}) collective-permute-start(bf16[96,2688]{1,0:T(8,128)(2,1)S(1)} %pad_maximum_fusion.7.refs_0_), channel_id=1, source_target_pairs={{0,7},{1,0},{2,1},{3,2},{4,3},{5,4},{6,5},{7,6},{8,15},{9,8},{10,9... | collective-permute-start | bytes 1548296 | tf_op jit(solution)/shard_map/ppermute | solution.py:23
  28.0 12.5 %collective-permute-start.10 = (bf16[96,2688]{1,0:T(8,128)(2,1)S(1)}, bf16[96,2688]{1,0:T(8,128)(2,1)S(1)}, u32[]{:S(2)}, u32[]{:S(2)}) collective-permute-start(bf16[96,2688]{1,0:T(8,128)(2,1)S(1)} %collective-permute-done.5.refs_1_), channel_id=1, source_target_pairs={{0,1},{1,2},{2,3},{3,4},{4,5},{5,6},{6,7},{7,0},{8,9},{9,10},{10,1... | collective-permute-start | bytes 1548296 | tf_op jit(solution)/shard_map/ppermute | solution.py:23
  28.1 12.4 %collective-permute-start.13 = (bf16[96,2688]{1,0:T(8,128)(2,1)S(1)}, bf16[96,2688]{1,0:T(8,128)(2,1)S(1)}, u32[]{:S(2)}, u32[]{:S(2)}) collective-permute-start(bf16[96,2688]{1,0:T(8,128)(2,1)S(1)} %collective-permute-done.6.refs_2_), channel_id=1, source_target_pairs={{0,7},{1,0},{2,1},{3,2},{4,3},{5,4},{6,5},{7,6},{8,15},{9,8},{10,9... | collective-permute-start | bytes 1548296 | tf_op jit(solution)/shard_map/ppermute | solution.py:23
  40.5 11.6 %collective-permute-start.11 = (bf16[96,2688]{1,0:T(8,128)(2,1)S(1)}, bf16[96,2688]{1,0:T(8,128)(2,1)S(1)}, u32[]{:S(2)}, u32[]{:S(2)}) collective-permute-start(bf16[96,2688]{1,0:T(8,128)(2,1)S(1)} %collective-permute-done.10.refs_0_), channel_id=1, source_target_pairs={{0,1},{1,2},{2,3},{3,4},{4,5},{5,6},{6,7},{7,0},{8,9},{9,10},{10,1... | collective-permute-start | bytes 1548296 | tf_op jit(solution)/shard_map/ppermute | solution.py:23
  40.5 11.7 %collective-permute-start.14 = (bf16[96,2688]{1,0:T(8,128)(2,1)S(1)}, bf16[96,2688]{1,0:T(8,128)(2,1)S(1)}, u32[]{:S(2)}, u32[]{:S(2)}) collective-permute-start(bf16[96,2688]{1,0:T(8,128)(2,1)S(1)} %collective-permute-done.13.refs_1_), channel_id=1, source_target_pairs={{0,7},{1,0},{2,1},{3,2},{4,3},{5,4},{6,5},{7,6},{8,15},{9,8},{10,9... | collective-permute-start | bytes 1548296 | tf_op jit(solution)/shard_map/ppermute | solution.py:23
  44.5 40.8 %collective-permute-start.7 = (bf16[288,2688]{1,0:T(8,128)(2,1)}, bf16[288,2688]{1,0:T(8,128)(2,1)}, u32[]{:S(2)}, u32[]{:S(2)}) collective-permute-start(bf16[288,2688]{1,0:T(8,128)(2,1)} %pad_maximum_fusion), channel_id=1, source_target_pairs={{0,8},{8,0},{1,9},{9,1},{2,10},{10,2},{3,11},{11,3},{4,12},{12,4},... | collective-permute-start | bytes 4644872 | tf_op jit(solution)/shard_map/ppermute | solution.py:18
  49.0 17.7 %collective-permute-start.22 = (bf16[192,2688]{1,0:T(8,128)(2,1)}, bf16[192,2688]{1,0:T(8,128)(2,1)}, u32[]{:S(2)}, u32[]{:S(2)}) collective-permute-start(bf16[192,2688]{1,0:T(8,128)(2,1)} %pad_maximum_fusion.4), channel_id=1, source_target_pairs={{0,8},{8,0},{1,9},{9,1},{2,10},{10,2},{3,11},{11,3},{4,12},{12,4},... | collective-permute-start | bytes 3096584 | tf_op jit(solution)/shard_map/ppermute | solution.py:18
  52.1 8.1 %collective-permute-start.12 = (bf16[48,2688]{1,0:T(8,128)(2,1)S(1)}, bf16[48,2688]{1,0:T(8,128)(2,1)S(1)}, u32[]{:S(2)}, u32[]{:S(2)}) collective-permute-start(bf16[48,2688]{1,0:T(8,128)(2,1)S(1)} %slice.111), channel_id=1, source_target_pairs={{0,1},{1,2},{2,3},{3,4},{4,5},{5,6},{6,7},{7,0},{8,9},{9,10},{10,1... | collective-permute-start | bytes 774152 | tf_op jit(solution)/shard_map/ppermute | solution.py:23
  53.4 42.2 %collective-permute-start.19 = (bf16[192,2688]{1,0:T(8,128)(2,1)}, bf16[192,2688]{1,0:T(8,128)(2,1)}, u32[]{:S(2)}, u32[]{:S(2)}) collective-permute-start(bf16[192,2688]{1,0:T(8,128)(2,1)} %pad_maximum_fusion.3), channel_id=1, source_target_pairs={{0,8},{8,0},{1,9},{9,1},{2,10},{10,2},{3,11},{11,3},{4,12},{12,4},... | collective-permute-start | bytes 3096584 | tf_op jit(solution)/shard_map/ppermute | solution.py:18
  57.2 8.5 %collective-permute-start.15 = (bf16[48,2688]{1,0:T(8,128)(2,1)S(1)}, bf16[48,2688]{1,0:T(8,128)(2,1)S(1)}, u32[]{:S(2)}, u32[]{:S(2)}) collective-permute-start(bf16[48,2688]{1,0:T(8,128)(2,1)S(1)} %slice.112), channel_id=1, source_target_pairs={{0,7},{1,0},{2,1},{3,2},{4,3},{5,4},{6,5},{7,6},{8,15},{9,8},{10,9... | collective-permute-start | bytes 774152 | tf_op jit(solution)/shard_map/ppermute | solution.py:23
  65.8 13.4 %collective-permute-start.16 = (bf16[96,2688]{1,0:T(8,128)(2,1)S(1)}, bf16[96,2688]{1,0:T(8,128)(2,1)}, u32[]{:S(2)}, u32[]{:S(2)}) collective-permute-start(bf16[96,2688]{1,0:T(8,128)(2,1)S(1)} %constant_dynamic-update-slice_fusion.refs_0_), channel_id=1, source_target_pairs={{0,8},{8,0},{1,9},{9,1},{2,10},{10,2},{3,11},{11,3},{4,12},{12,4},... | collective-permute-start | bytes 1548296 | tf_op jit(solution)/shard_map/ppermute | solution.py:18
  78.8 26.5 %collective-permute-start.23 = (bf16[192,2560]{1,0:T(8,128)(2,1)S(1)}, bf16[192,2560]{1,0:T(8,128)(2,1)S(1)}, u32[]{:S(2)}, u32[]{:S(2)}) collective-permute-start(bf16[192,2560]{1,0:T(8,128)(2,1)S(1)} %get-tuple-element.229), channel_id=1, source_target_pairs={{0,8},{8,0},{1,9},{9,1},{2,10},{10,2},{3,11},{11,3},{4,12},{12,4},... | collective-permute-start | bytes 2949128 | tf_op jit(solution)/shard_map/ppermute | solution.py:18
  84.8 19.0 %collective-permute-start.17 = (bf16[96,2560]{1,0:T(8,128)(2,1)S(1)}, bf16[96,2560]{1,0:T(8,128)(2,1)S(1)}, u32[]{:S(2)}, u32[]{:S(2)}) collective-permute-start(bf16[96,2560]{1,0:T(8,128)(2,1)S(1)} %get-tuple-element.225), channel_id=1, source_target_pairs={{0,8},{8,0},{1,9},{9,1},{2,10},{10,2},{3,11},{11,3},{4,12},{12,4},... | collective-permute-start | bytes 1474568 | tf_op jit(solution)/shard_map/ppermute | solution.py:18
  95.4 16.1 %collective-permute-start.8 = (bf16[288,2560]{1,0:T(8,128)(2,1)S(1)}, bf16[288,2560]{1,0:T(8,128)(2,1)S(1)}, u32[]{:S(2)}, u32[]{:S(2)}) collective-permute-start(bf16[288,2560]{1,0:T(8,128)(2,1)S(1)} %get-tuple-element.223), channel_id=1, source_target_pairs={{0,8},{8,0},{1,9},{9,1},{2,10},{10,2},{3,11},{11,3},{4,12},{12,4},... | collective-permute-start | bytes 4423688 | tf_op jit(solution)/shard_map/ppermute | solution.py:18
  103.2 10.1 %collective-permute-start.20 = (bf16[192,2560]{1,0:T(8,128)(2,1)S(1)}, bf16[192,2560]{1,0:T(8,128)(2,1)S(1)}, u32[]{:S(2)}, u32[]{:S(2)}) collective-permute-start(bf16[192,2560]{1,0:T(8,128)(2,1)S(1)} %get-tuple-element.227), channel_id=1, source_target_pairs={{0,8},{8,0},{1,9},{9,1},{2,10},{10,2},{3,11},{11,3},{4,12},{12,4},... | collective-permute-start | bytes 2949128 | tf_op jit(solution)/shard_map/ppermute | solution.py:18
  103.9 7.5 %collective-permute-start.18 = (bf16[48,2560]{1,0:T(8,128)(2,1)S(1)}, bf16[48,2560]{1,0:T(8,128)(2,1)S(1)}, u32[]{:S(2)}, u32[]{:S(2)}) collective-permute-start(bf16[48,2560]{1,0:T(8,128)(2,1)S(1)} %slice.114), channel_id=1, source_target_pairs={{0,16},{16,0},{1,17},{17,1},{2,18},{18,2},{3,19},{19,3},{4,20},{20... | collective-permute-start | bytes 737288 | tf_op jit(solution)/shard_map/ppermute | solution.py:18
  105.6 16.4 %collective-permute-start.24 = (bf16[96,2560]{1,0:T(8,128)(2,1)S(1)}, bf16[96,2560]{1,0:T(8,128)(2,1)S(1)}, u32[]{:S(2)}, u32[]{:S(2)}) collective-permute-start(bf16[96,2560]{1,0:T(8,128)(2,1)S(1)} %slice.119), channel_id=1, source_target_pairs={{0,16},{16,0},{1,17},{17,1},{2,18},{18,2},{3,19},{19,3},{4,20},{20... | collective-permute-start | bytes 1474568 | tf_op jit(solution)/shard_map/ppermute | solution.py:18
  112.0 36.5 %collective-permute-start.9 = (bf16[144,2560]{1,0:T(8,128)(2,1)S(1)}, bf16[144,2560]{1,0:T(8,128)(2,1)S(1)}, u32[]{:S(2)}, u32[]{:S(2)}) collective-permute-start(bf16[144,2560]{1,0:T(8,128)(2,1)S(1)} %slice.109), channel_id=1, source_target_pairs={{0,16},{16,0},{1,17},{17,1},{2,18},{18,2},{3,19},{19,3},{4,20},{20... | collective-permute-start | bytes 2211848 | tf_op jit(solution)/shard_map/ppermute | solution.py:18
  113.6 34.7 %collective-permute-start.21 = (bf16[96,2560]{1,0:T(8,128)(2,1)S(1)}, bf16[96,2560]{1,0:T(8,128)(2,1)S(1)}, u32[]{:S(2)}, u32[]{:S(2)}) collective-permute-start(bf16[96,2560]{1,0:T(8,128)(2,1)S(1)} %slice.116), channel_id=1, source_target_pairs={{0,16},{16,0},{1,17},{17,1},{2,18},{18,2},{3,19},{19,3},{4,20},{20... | collective-permute-start | bytes 1474568 | tf_op jit(solution)/shard_map/ppermute | solution.py:18
  150.6 8.8 %collective-permute-start = (bf16[48,2560]{1,0:T(8,128)(2,1)S(1)}, bf16[48,2560]{1,0:T(8,128)(2,1)S(1)}, u32[]{:S(2)}, u32[]{:S(2)}) collective-permute-start(bf16[48,2560]{1,0:T(8,128)(2,1)S(1)} %add_convert_fusion.20), channel_id=1, source_target_pairs={{0,1},{1,2},{2,3},{3,4},{4,5},{5,6},{6,7},{7,0},{8,9},{9,10},{10,1... | collective-permute-start | bytes 737288 | tf_op jit(solution)/shard_map/while/body/eval_jaxpr/ppermute | solution.py:23
  152.5 7.0 %collective-permute-start.1 = (bf16[48,2560]{1,0:T(8,128)(2,1)S(1)}, bf16[48,2560]{1,0:T(8,128)(2,1)S(1)}, u32[]{:S(2)}, u32[]{:S(2)}) collective-permute-start(bf16[48,2560]{1,0:T(8,128)(2,1)S(1)} %add_convert_fusion.21), channel_id=1, source_target_pairs={{0,7},{1,0},{2,1},{3,2},{4,3},{5,4},{6,5},{7,6},{8,15},{9,8},{10,9... | collective-permute-start | bytes 737288 | tf_op jit(solution)/shard_map/while/body/eval_jaxpr/ppermute | solution.py:23
  159.6 8.0 %collective-permute-start = (bf16[48,2560]{1,0:T(8,128)(2,1)S(1)}, bf16[48,2560]{1,0:T(8,128)(2,1)S(1)}, u32[]{:S(2)}, u32[]{:S(2)}) collective-permute-start(bf16[48,2560]{1,0:T(8,128)(2,1)S(1)} %add_convert_fusion.20), channel_id=1, source_target_pairs={{0,1},{1,2},{2,3},{3,4},{4,5},{5,6},{6,7},{7,0},{8,9},{9,10},{10,1... | collective-permute-start | bytes 737288 | tf_op jit(solution)/shard_map/while/body/eval_jaxpr/ppermute | solution.py:23
  162.9 5.5 %collective-permute-start.1 = (bf16[48,2560]{1,0:T(8,128)(2,1)S(1)}, bf16[48,2560]{1,0:T(8,128)(2,1)S(1)}, u32[]{:S(2)}, u32[]{:S(2)}) collective-permute-start(bf16[48,2560]{1,0:T(8,128)(2,1)S(1)} %add_convert_fusion.21), channel_id=1, source_target_pairs={{0,7},{1,0},{2,1},{3,2},{4,3},{5,4},{6,5},{7,6},{8,15},{9,8},{10,9... | collective-permute-start | bytes 737288 | tf_op jit(solution)/shard_map/while/body/eval_jaxpr/ppermute | solution.py:23
  168.5 6.3 %collective-permute-start = (bf16[48,2560]{1,0:T(8,128)(2,1)S(1)}, bf16[48,2560]{1,0:T(8,128)(2,1)S(1)}, u32[]{:S(2)}, u32[]{:S(2)}) collective-permute-start(bf16[48,2560]{1,0:T(8,128)(2,1)S(1)} %add_convert_fusion.20), channel_id=1, source_target_pairs={{0,1},{1,2},{2,3},{3,4},{4,5},{5,6},{6,7},{7,0},{8,9},{9,10},{10,1... | collective-permute-start | bytes 737288 | tf_op jit(solution)/shard_map/while/body/eval_jaxpr/ppermute | solution.py:23
  170.7 5.5 %collective-permute-start.1 = (bf16[48,2560]{1,0:T(8,128)(2,1)S(1)}, bf16[48,2560]{1,0:T(8,128)(2,1)S(1)}, u32[]{:S(2)}, u32[]{:S(2)}) collective-permute-start(bf16[48,2560]{1,0:T(8,128)(2,1)S(1)} %add_convert_fusion.21), channel_id=1, source_target_pairs={{0,7},{1,0},{2,1},{3,2},{4,3},{5,4},{6,5},{7,6},{8,15},{9,8},{10,9... | collective-permute-start | bytes 737288 | tf_op jit(solution)/shard_map/while/body/eval_jaxpr/ppermute | solution.py:23
  176.3 6.3 %collective-permute-start = (bf16[48,2560]{1,0:T(8,128)(2,1)S(1)}, bf16[48,2560]{1,0:T(8,128)(2,1)S(1)}, u32[]{:S(2)}, u32[]{:S(2)}) collective-permute-start(bf16[48,2560]{1,0:T(8,128)(2,1)S(1)} %add_convert_fusion.20), channel_id=1, source_target_pairs={{0,1},{1,2},{2,3},{3,4},{4,5},{5,6},{6,7},{7,0},{8,9},{9,10},{10,1... | collective-permute-start | bytes 737288 | tf_op jit(solution)/shard_map/while/body/eval_jaxpr/ppermute | solution.py:23
  178.9 5.1 %collective-permute-start.1 = (bf16[48,2560]{1,0:T(8,128)(2,1)S(1)}, bf16[48,2560]{1,0:T(8,128)(2,1)S(1)}, u32[]{:S(2)}, u32[]{:S(2)}) collective-permute-start(bf16[48,2560]{1,0:T(8,128)(2,1)S(1)} %add_convert_fusion.21), channel_id=1, source_target_pairs={{0,7},{1,0},{2,1},{3,2},{4,3},{5,4},{6,5},{7,6},{8,15},{9,8},{10,9... | collective-permute-start | bytes 737288 | tf_op jit(solution)/shard_map/while/body/eval_jaxpr/ppermute | solution.py:23
  185.5 6.3 %collective-permute-start.25 = (bf16[48,2560]{1,0:T(8,128)(2,1)S(1)}, bf16[48,2560]{1,0:T(8,128)(2,1)S(1)}, u32[]{:S(2)}, u32[]{:S(2)}) collective-permute-start(bf16[48,2560]{1,0:T(8,128)(2,1)S(1)} %fusion.10.refs_0_), channel_id=1, source_target_pairs={{0,1},{1,2},{2,3},{3,4},{4,5},{5,6},{6,7},{7,0},{8,9},{9,10},{10,1... | collective-permute-start | bytes 737288 | tf_op jit(solution)/shard_map/ppermute | solution.py:23
  187.4 5.1 %collective-permute-start.26 = (bf16[48,2560]{1,0:T(8,128)(2,1)S(1)}, bf16[48,2560]{1,0:T(8,128)(2,1)S(1)}, u32[]{:S(2)}, u32[]{:S(2)}) collective-permute-start(bf16[48,2560]{1,0:T(8,128)(2,1)S(1)} %fusion.10.refs_0_), channel_id=1, source_target_pairs={{0,7},{1,0},{2,1},{3,2},{4,3},{5,4},{6,5},{7,6},{8,15},{9,8},{10,9... | collective-permute-start | bytes 737288 | tf_op jit(solution)/shard_map/ppermute | solution.py:23
  191.9 8.6 %collective-permute-start.27 = (bf16[48,2560]{1,0:T(8,128)(2,1)S(1)}, bf16[48,2560]{1,0:T(8,128)(2,1)S(1)}, u32[]{:S(2)}, u32[]{:S(2)}) collective-permute-start(bf16[48,2560]{1,0:T(8,128)(2,1)S(1)} %collective-permute-done.25.refs_1_), channel_id=1, source_target_pairs={{0,1},{1,2},{2,3},{3,4},{4,5},{5,6},{6,7},{7,0},{8,9},{9,10},{10,1... | collective-permute-start | bytes 737288 | tf_op jit(solution)/shard_map/ppermute | solution.py:23
  192.4 8.0 %collective-permute-start.28 = (bf16[48,2560]{1,0:T(8,128)(2,1)S(1)}, bf16[48,2560]{1,0:T(8,128)(2,1)S(1)}, u32[]{:S(2)}, u32[]{:S(2)}) collective-permute-start(bf16[48,2560]{1,0:T(8,128)(2,1)S(1)} %collective-permute-done.26.refs_2_), channel_id=1, source_target_pairs={{0,7},{1,0},{2,1},{3,2},{4,3},{5,4},{6,5},{7,6},{8,15},{9,8},{10,9... | collective-permute-start | bytes 737288 | tf_op jit(solution)/shard_map/ppermute | solution.py:23
  200.5 10.9 %collective-permute-start.29 = (bf16[48,2560]{1,0:T(8,128)(2,1)S(1)}, bf16[48,2560]{1,0:T(8,128)(2,1)S(1)}, u32[]{:S(2)}, u32[]{:S(2)}) collective-permute-start(bf16[48,2560]{1,0:T(8,128)(2,1)S(1)} %collective-permute-done.27.refs_3_), channel_id=1, source_target_pairs={{0,1},{1,2},{2,3},{3,4},{4,5},{5,6},{6,7},{7,0},{8,9},{9,10},{10,1... | collective-permute-start | bytes 737288 | tf_op jit(solution)/shard_map/ppermute | solution.py:23
  200.5 11.0 %collective-permute-start.30 = (bf16[48,2560]{1,0:T(8,128)(2,1)S(1)}, bf16[48,2560]{1,0:T(8,128)(2,1)S(1)}, u32[]{:S(2)}, u32[]{:S(2)}) collective-permute-start(bf16[48,2560]{1,0:T(8,128)(2,1)S(1)} %collective-permute-done.28.refs_4_), channel_id=1, source_target_pairs={{0,7},{1,0},{2,1},{3,2},{4,3},{5,4},{6,5},{7,6},{8,15},{9,8},{10,9... | collective-permute-start | bytes 737288 | tf_op jit(solution)/shard_map/ppermute | solution.py:23
  210.0 5.4 %collective-permute-start.33 = (bf16[240,512]{1,0:T(8,128)(2,1)S(1)}, bf16[240,512]{1,0:T(8,128)(2,1)S(1)}, u32[]{:S(2)}, u32[]{:S(2)}) collective-permute-start(bf16[240,512]{1,0:T(8,128)(2,1)S(1)} %get-tuple-element.234), channel_id=1, source_target_pairs={{0,16},{16,0},{1,17},{17,1},{2,18},{18,2},{3,19},{19,3},{4,20},{20... | collective-permute-start | bytes 737288 | tf_op jit(solution)/shard_map/ppermute | solution.py:18
  211.4 16.9 %collective-permute-start.31 = (bf16[24,2560]{1,0:T(8,128)(2,1)S(1)}, bf16[24,2560]{1,0:T(8,128)(2,1)S(1)}, u32[]{:S(2)}, u32[]{:S(2)}) collective-permute-start(bf16[24,2560]{1,0:T(8,128)(2,1)S(1)} %slice.129), channel_id=1, source_target_pairs={{0,1},{1,2},{2,3},{3,4},{4,5},{5,6},{6,7},{7,0},{8,9},{9,10},{10,1... | collective-permute-start | bytes 368648 | tf_op jit(solution)/shard_map/ppermute | solution.py:23
  211.5 16.8 %collective-permute-start.32 = (bf16[24,2560]{1,0:T(8,128)(2,1)S(1)}, bf16[24,2560]{1,0:T(8,128)(2,1)S(1)}, u32[]{:S(2)}, u32[]{:S(2)}) collective-permute-start(bf16[24,2560]{1,0:T(8,128)(2,1)S(1)} %slice.130), channel_id=1, source_target_pairs={{0,7},{1,0},{2,1},{3,2},{4,3},{5,4},{6,5},{7,6},{8,15},{9,8},{10,9... | collective-permute-start | bytes 368648 | tf_op jit(solution)/shard_map/ppermute | solution.py:23
  231.8 5.1 %collective-permute-start.34 = (bf16[144,512]{1,0:T(8,128)(2,1)S(1)}, bf16[144,512]{1,0:T(8,128)(2,1)S(1)}, u32[]{:S(2)}, u32[]{:S(2)}) collective-permute-start(bf16[144,512]{1,0:T(8,128)(2,1)S(1)} %get-tuple-element.239), channel_id=1, source_target_pairs={{0,16},{16,0},{1,17},{17,1},{2,18},{18,2},{3,19},{19,3},{4,20},{20... | collective-permute-start | bytes 442376 | tf_op jit(solution)/shard_map/ppermute | solution.py:18
  236.9 2.5 collective-permute-start.35
  244.8 8.5 %collective-permute-start.2 = (bf16[48,2560]{1,0:T(8,128)(2,1)S(1)}, bf16[48,2560]{1,0:T(8,128)(2,1)S(1)}, u32[]{:S(2)}, u32[]{:S(2)}) collective-permute-start(bf16[48,2560]{1,0:T(8,128)(2,1)S(1)} %add_convert_fusion.22), channel_id=1, source_target_pairs={{0,1},{1,2},{2,3},{3,4},{4,5},{5,6},{6,7},{7,0},{8,9},{9,10},{10,1... | collective-permute-start | bytes 737288 | tf_op jit(solution)/shard_map/while/body/eval_jaxpr/ppermute | solution.py:23
  244.9 8.3 %collective-permute-start.3 = (bf16[48,2560]{1,0:T(8,128)(2,1)S(1)}, bf16[48,2560]{1,0:T(8,128)(2,1)S(1)}, u32[]{:S(2)}, u32[]{:S(2)}) collective-permute-start(bf16[48,2560]{1,0:T(8,128)(2,1)S(1)} %add_convert_fusion.23), channel_id=1, source_target_pairs={{0,7},{1,0},{2,1},{3,2},{4,3},{5,4},{6,5},{7,6},{8,15},{9,8},{10,9... | collective-permute-start | bytes 737288 | tf_op jit(solution)/shard_map/while/body/eval_jaxpr/ppermute | solution.py:23
  253.3 7.6 %collective-permute-start.2 = (bf16[48,2560]{1,0:T(8,128)(2,1)S(1)}, bf16[48,2560]{1,0:T(8,128)(2,1)S(1)}, u32[]{:S(2)}, u32[]{:S(2)}) collective-permute-start(bf16[48,2560]{1,0:T(8,128)(2,1)S(1)} %add_convert_fusion.22), channel_id=1, source_target_pairs={{0,1},{1,2},{2,3},{3,4},{4,5},{5,6},{6,7},{7,0},{8,9},{9,10},{10,1... | collective-permute-start | bytes 737288 | tf_op jit(solution)/shard_map/while/body/eval_jaxpr/ppermute | solution.py:23
  253.5 7.5 %collective-permute-start.3 = (bf16[48,2560]{1,0:T(8,128)(2,1)S(1)}, bf16[48,2560]{1,0:T(8,128)(2,1)S(1)}, u32[]{:S(2)}, u32[]{:S(2)}) collective-permute-start(bf16[48,2560]{1,0:T(8,128)(2,1)S(1)} %add_convert_fusion.23), channel_id=1, source_target_pairs={{0,7},{1,0},{2,1},{3,2},{4,3},{5,4},{6,5},{7,6},{8,15},{9,8},{10,9... | collective-permute-start | bytes 737288 | tf_op jit(solution)/shard_map/while/body/eval_jaxpr/ppermute | solution.py:23
  261.0 6.8 %collective-permute-start.2 = (bf16[48,2560]{1,0:T(8,128)(2,1)S(1)}, bf16[48,2560]{1,0:T(8,128)(2,1)S(1)}, u32[]{:S(2)}, u32[]{:S(2)}) collective-permute-start(bf16[48,2560]{1,0:T(8,128)(2,1)S(1)} %add_convert_fusion.22), channel_id=1, source_target_pairs={{0,1},{1,2},{2,3},{3,4},{4,5},{5,6},{6,7},{7,0},{8,9},{9,10},{10,1... | collective-permute-start | bytes 737288 | tf_op jit(solution)/shard_map/while/body/eval_jaxpr/ppermute | solution.py:23
  261.1 6.6 %collective-permute-start.3 = (bf16[48,2560]{1,0:T(8,128)(2,1)S(1)}, bf16[48,2560]{1,0:T(8,128)(2,1)S(1)}, u32[]{:S(2)}, u32[]{:S(2)}) collective-permute-start(bf16[48,2560]{1,0:T(8,128)(2,1)S(1)} %add_convert_fusion.23), channel_id=1, source_target_pairs={{0,7},{1,0},{2,1},{3,2},{4,3},{5,4},{6,5},{7,6},{8,15},{9,8},{10,9... | collective-permute-start | bytes 737288 | tf_op jit(solution)/shard_map/while/body/eval_jaxpr/ppermute | solution.py:23
  267.8 6.3 %collective-permute-start.2 = (bf16[48,2560]{1,0:T(8,128)(2,1)S(1)}, bf16[48,2560]{1,0:T(8,128)(2,1)S(1)}, u32[]{:S(2)}, u32[]{:S(2)}) collective-permute-start(bf16[48,2560]{1,0:T(8,128)(2,1)S(1)} %add_convert_fusion.22), channel_id=1, source_target_pairs={{0,1},{1,2},{2,3},{3,4},{4,5},{5,6},{6,7},{7,0},{8,9},{9,10},{10,1... | collective-permute-start | bytes 737288 | tf_op jit(solution)/shard_map/while/body/eval_jaxpr/ppermute | solution.py:23
  268.0 6.1 %collective-permute-start.3 = (bf16[48,2560]{1,0:T(8,128)(2,1)S(1)}, bf16[48,2560]{1,0:T(8,128)(2,1)S(1)}, u32[]{:S(2)}, u32[]{:S(2)}) collective-permute-start(bf16[48,2560]{1,0:T(8,128)(2,1)S(1)} %add_convert_fusion.23), channel_id=1, source_target_pairs={{0,7},{1,0},{2,1},{3,2},{4,3},{5,4},{6,5},{7,6},{8,15},{9,8},{10,9... | collective-permute-start | bytes 737288 | tf_op jit(solution)/shard_map/while/body/eval_jaxpr/ppermute | solution.py:23
  (30 other events, 360.4 us)
where the time goes:
time: 278 us; the launch traced here: 275 us
  waiting for transfers between devices  117 us (42%)
  starting transfers between devices  70.2 us (25%)
  Pallas kernels  42.8 us (15%)
  other arithmetic  15.5 us (6%)
  local copies, waits for them, and re-layouts  15.4 us (6%)
  blocking collectives  12.9 us (5%)
    ppermute x32, waiting for transfers between devices, shift(): return lax.ppermute(value, 'seq', [(i, (i + step) % n) for i in range(n)])  66 us
    ppermute x16, waiting for transfers between devices, swap(): return lax.ppermute(value, axis, [(0, 1), (1, 0)])  50.8 us
    ppermute x32, starting transfers between devices, shift(): return lax.ppermute(value, 'seq', [(i, (i + step) % n) for i in range(n)])  50.8 us
    pallas_call x4, Pallas kernels, expert_call(): pl.pallas_call(kernel, out_shape=[jax.ShapeDtypeStruct((m1, dim), jnp.bfl...  30.9 us
    ppermute x16, starting transfers between devices, swap(): return lax.ppermute(value, axis, [(0, 1), (1, 0)])  19.4 us
    all_gather x1, blocking collectives, shards(): kv_a = lax.all_gather(kv_a, 'exp_1', axis=0, tiled=True)  12.9 us
    unnamed x62, local copies, waits for them, and re-layouts  8.08 us
    pallas_call x2, Pallas kernels, project_call(): pl.pallas_call(kernel, out_shape=[jax.ShapeDtypeStruct((m, width), jnp.bf...  7.64 us
  transfers between devices with their start and end apart: 48, of which 25 were waited for; matrix products, arithmetic and copies ran while one was open for 6% of the time, Pallas kernels for 13%

commit v1 on v0

--- a/solution.py
+++ b/solution.py
@@ -55,6 +55,7 @@
 
 
 ANY = pl.BlockSpec(memory_space=pl.ANY)
+FAR = pl.BlockSpec(memory_space=pltpu.HBM)
 
 
 TRANS = (((1,), (1,)), ((), ()))
@@ -138,7 +139,7 @@
     return pl.pallas_call(
         kernel,
         out_shape=[jax.ShapeDtypeStruct((m1, dim), jnp.bfloat16)] * 2,
-        in_specs=[pl.BlockSpec(memory_space=pltpu.SMEM)] + [ANY] * (n + 3),
+        in_specs=[pl.BlockSpec(memory_space=pltpu.SMEM)] + [ANY] * (n + 1) + [FAR, FAR],
         out_specs=[pl.BlockSpec(memory_space=pltpu.VMEM)] * 2,
         scratch_shapes=[
             pltpu.VMEM((m, cols), jnp.bfloat16),
@@ -151,7 +152,7 @@
             pltpu.SemaphoreType.DMA((4,)),
             pltpu.SemaphoreType.DMA,
         ],
-        compiler_params=pltpu.CompilerParams(vmem_limit_bytes=(10 + 5 * n) * 2**20),
+        compiler_params=pltpu.CompilerParams(vmem_limit_bytes=50 * 2**20),
         cost_estimate=pl.CostEstimate(
             flops=6 * m * dim * ff, bytes_accessed=6 * dim * ff + 4 * m * dim, transcendentals=m * ff
         ),
@@ -163,8 +164,8 @@
     n = len(parts)
     sizes = [p.shape[0] for p in parts]
     m = sum(sizes)
-    cols, dim = w.shape
-    width = cols // 3
+    _, dim, width = w.shape
+    cols = 3 * width
     head = width // heads
     kc = 512
     nk = dim // kc
@@ -192,9 +193,11 @@
         def step(k, carry):
             at = pl.ds(pl.multiple_of(k * kc, kc), kc)
             w_copy(k).wait()
-            acc[...] += lax.dot_general(
-                x_s[:, at], w_s[:, at], TRANS, preferred_element_type=jnp.float32
-            )
+            x = x_s[:, at]
+            for g in range(3):
+                acc[:, g * width : (g + 1) * width] += jnp.dot(
+                    x, w_s[g, at, :], preferred_element_type=jnp.float32
+                )
             return carry
 
         lax.fori_loop(0, nk, step, 0)
@@ -212,16 +215,16 @@
             jax.ShapeDtypeStruct((m, width), jnp.bfloat16),
             jax.ShapeDtypeStruct((m, 2 * width), jnp.bfloat16),
         ],
-        in_specs=[ANY] * (n + 1) + [vmem, vmem],
+        in_specs=[ANY] * n + [FAR, vmem, vmem],
         out_specs=[vmem, vmem],
         scratch_shapes=[
             pltpu.VMEM((m, dim), jnp.bfloat16),
-            pltpu.VMEM((cols, dim), jnp.bfloat16),
+            pltpu.VMEM((3, dim, width), jnp.bfloat16),
             pltpu.VMEM((m, cols), jnp.float32),
             pltpu.SemaphoreType.DMA((n,)),
             pltpu.SemaphoreType.DMA((nk,)),
         ],
-        compiler_params=pltpu.CompilerParams(vmem_limit_bytes=16 * 2**20),
+        compiler_params=pltpu.CompilerParams(vmem_limit_bytes=58 * 2**20),
         cost_estimate=pl.CostEstimate(
             flops=2 * m * dim * cols, bytes_accessed=2 * dim * cols + 2 * m * dim, transcendentals=0
         ),
@@ -297,7 +300,7 @@
     return pl.pallas_call(
         kernel,
         out_shape=[jax.ShapeDtypeStruct((rows, dim), jnp.bfloat16)] * planes,
-        in_specs=[ANY] * (nq + nv + 1),
+        in_specs=[ANY] * (nq + nv) + [FAR],
         out_specs=[pl.BlockSpec(memory_space=pltpu.VMEM)] * planes,
         scratch_shapes=[
             pltpu.VMEM((m, width), jnp.bfloat16),
@@ -343,23 +346,25 @@
     )
     packed = jnp.concatenate([normed, numer.astype(jnp.bfloat16)], axis=1)
 
-    column = jnp.concatenate([packed, swap(packed, "exp_0")], 0)
     w_gu = w_gate_up[0].transpose(1, 2, 0).reshape(4, -1, dim)
-    w_qkv2 = w_qkv.transpose(1, 2, 0).reshape(-1, dim)
+    w_qkv3 = w_qkv.transpose(1, 0, 2)
+    beside = swap(packed, "exp_0")
+    up_a, down_a = shift(packed, 1), shift(packed, -1)
+    up_b, down_b = shift(beside, 1), shift(beside, -1)
+    column = jnp.concatenate([packed, beside], 0)
+    up1, down1 = jnp.concatenate([up_a, up_b], 0), jnp.concatenate([down_a, down_b], 0)
 
     def experts(planes):
         other = swap(jnp.concatenate(planes, 0) if len(planes) > 1 else planes[0], "exp_1")
         mine, theirs = expert_call(planes, other, w_gu, w_down0, me)
-        chip = added(mine, swap(theirs, "exp_1"))
+        got = swap(theirs, "exp_1")
         cut = rows * len(planes)
-        across = swap(chip[cut:], "exp_0")
+        across = swap(added(mine[cut:], got[cut:]), "exp_0")
         return [
-            (chip[i * rows : (i + 1) * rows], across[i * rows : (i + 1) * rows])
+            tuple(t[i * rows : (i + 1) * rows] for t in (mine, got, across))
             for i in range(len(planes))
         ]
 
-    up1, down1 = shift(column, 1), shift(column, -1)
-    (up1, down1), (w_gu, w_qkv2) = tied((up1, down1), (w_gu, w_qkv2))
     up2, down2 = shift(up1, 1), shift(down1, -1)
     own_terms, b1, a1 = experts([column, up1, down1])
     up3, down3 = shift(up2, 1), shift(down2, -1)
@@ -371,7 +376,7 @@
     blank = jnp.zeros((rows, dim), jnp.bfloat16)
     below = jnp.concatenate([blank, *(added(*t) for t in (b3, b2, b1))], 0)
     from_below, from_above = ring_scatter(above, below, rows)
-    moe_total = wide(own_terms[0]) + wide(own_terms[1]) + wide(from_below) + wide(from_above)
+    moe_total = sum(wide(t) for t in (*own_terms, from_below, from_above))
     mixed = (tokens_wide + moe_total).astype(jnp.bfloat16)
 
     mixed_wide = wide(mixed)
@@ -380,7 +385,7 @@
     heads = w_qkv.shape[2] // head
 
     def project(parts):
-        q, kv = project_call(parts, w_qkv2, q_gain, k_gain, heads)
+        q, kv = project_call(parts, w_qkv3, q_gain, k_gain, heads)
         beside = swap(kv, "exp_0")
         return q, jnp.concatenate([kv, beside], 0)
 

time: 278 us -> 282 us (1.014)
  local copies, waits for them, and re-layouts: 15.4 us -> 6.57 us
  Pallas kernels: 42.8 us -> 51.1 us
  starting transfers between devices: 70.2 us -> 76.4 us
  waiting for transfers between devices: 117 us -> 111 us
  other arithmetic: 15.5 us -> 19.2 us
    transpose x1 -> x0, local copies, waits for them, and re-layouts: 6.27 us -> none  [shards(): w_qkv2 = w_qkv.transpose(1, 2, 0).reshape(-1, dim)]
    ppermute x32 -> x34, starting transfers between devices: 50.8 us -> 56.7 us  [shift(): return lax.ppermute(value, 'seq', [(i, (i + step) % n) for i in range(n)])]
    pallas_call x4, Pallas kernels: 30.9 us -> 36 us  [expert_call(): pl.pallas_call(kernel, out_shape=[jax.ShapeDtypeStruct((m1, dim), jnp.bfl...]
    ppermute x16, waiting for transfers between devices: 50.8 us -> 46 us  [swap(): return lax.ppermute(value, axis, [(0, 1), (1, 0)])]
    convert_element_type x24, other arithmetic: 6.13 us -> 9.74 us  [added(): return total.astype(jnp.bfloat16)]
    concatenate x3 -> x2, other arithmetic: 3.46 us -> 0.15 us  [experts(): jnp.concatenate(planes, 0)]
    pallas_call x2, Pallas kernels: 7.64 us -> 10.9 us  [project_call(): pl.pallas_call(kernel, out_shape=[jax.ShapeDtypeStruct((m, width), jnp.bf...]
    unnamed x62 -> x42, local copies, waits for them, and re-layouts: 8.08 us -> 4.89 us
  transfers between devices with their start and end apart: 48 -> 50, of which waited for: 25 -> 26; matrix products, arithmetic and copies ran while one was open for 6% -> 4% of each run, Pallas kernels for 13% -> 15%
where the time goes in v1:
time: 282 us; the launch traced here: 279 us
  waiting for transfers between devices  111 us (39%)
  starting transfers between devices  76.4 us (27%)
  Pallas kernels  51.1 us (18%)
  other arithmetic  19.2 us (7%)
  blocking collectives  12.9 us (5%)
  local copies, waits for them, and re-layouts  6.57 us (2%)
    ppermute x34, waiting for transfers between devices, shift(): return lax.ppermute(value, 'seq', [(i, (i + step) % n) for i in range(n)])  65.3 us
    ppermute x34, starting transfers between devices, shift(): return lax.ppermute(value, 'seq', [(i, (i + step) % n) for i in range(n)])  56.7 us
    ppermute x16, waiting for transfers between devices, swap(): return lax.ppermute(value, axis, [(0, 1), (1, 0)])  46 us
    pallas_call x4, Pallas kernels, expert_call(): pl.pallas_call(kernel, out_shape=[jax.ShapeDtypeStruct((m1, dim), jnp.bfl...  36 us
    ppermute x16, starting transfers between devices, swap(): return lax.ppermute(value, axis, [(0, 1), (1, 0)])  19.7 us
    all_gather x1, blocking collectives, shards(): kv_a = lax.all_gather(kv_a, 'exp_1', axis=0, tiled=True)  12.9 us
    pallas_call x2, Pallas kernels, project_call(): pl.pallas_call(kernel, out_shape=[jax.ShapeDtypeStruct((m, width), jnp.bf...  10.9 us
    convert_element_type x24, other arithmetic, added(): return total.astype(jnp.bfloat16)  9.74 us
  transfers between devices with their start and end apart: 50, of which 26 were waited for; matrix products, arithmetic and copies ran while one was open for 4% of the time, Pallas kernels for 15%

profile of v1, /device:TPU:1, one launch (start us, length us, event | category | flops | bytes accessed | tf_op | source)
XLA Modules:
  0.0 278.6 jit_solution(688848232171327590)
XLA Ops:
  4.4 2.1 collective-permute-start.4
  6.5 1.6 collective-permute-start.5
  8.2 3.9 %collective-permute-start.7 = (bf16[48,2688]{1,0:T(8,128)(2,1)S(1)}, bf16[48,2688]{1,0:T(8,128)(2,1)S(1)}, u32[]{:S(2)}, u32[]{:S(2)}) collective-permute-start(bf16[48,2688]{1,0:T(8,128)(2,1)S(1)} %get-tuple-element.279), channel_id=1, source_target_pairs={{0,7},{1,0},{2,1},{3,2},{4,3},{5,4},{6,5},{7,6},{8,15},{9,8},{10,9... | collective-permute-start | bytes 774152 | tf_op jit(solution)/shard_map/ppermute | solution.py:23
  12.1 1.9 collective-permute-start.6
  14.0 3.9 %collective-permute-start.8 = (bf16[48,2688]{1,0:T(8,128)(2,1)S(1)}, bf16[48,2688]{1,0:T(8,128)(2,1)S(1)}, u32[]{:S(2)}, u32[]{:S(2)}) collective-permute-start(bf16[48,2688]{1,0:T(8,128)(2,1)S(1)} %collective-permute-done.4), channel_id=1, source_target_pairs={{0,7},{1,0},{2,1},{3,2},{4,3},{5,4},{6,5},{7,6},{8,15},{9,8},{10,9... | collective-permute-start | bytes 774152 | tf_op jit(solution)/shard_map/ppermute | solution.py:23
  19.4 3.6 %collective-permute-done.6 = bf16[48,2688]{1,0:T(8,128)(2,1)S(1)} collective-permute-done((bf16[48,2688]{1,0:T(8,128)(2,1)S(1)}, bf16[48,2688]{1,0:T(8,128)(2,1)S(1)}, u32[]{:S(2)}, u32[]{:S(2)}) %collective-permute-start.6) | collective-permute-done | bytes 258080 | tf_op jit(solution)/shard_map/ppermute | solution.py:23
  25.2 2.7 collective-permute-start.15
  27.9 8.3 %collective-permute-done.12.refs_0_ = bf16[96,2688]{1,0:T(8,128)(2,1)S(1)} collective-permute-done((bf16[96,2688]{1,0:T(8,128)(2,1)S(1)}, bf16[96,2688]{1,0:T(8,128)(2,1)S(1)}, u32[]{:S(2)}, u32[]{:S(2)}) %collective-permute-start.12) | collective-permute-done | bytes 516128 | tf_op jit(solution)/shard_map/ppermute | solution.py:23
  36.6 3.4 %collective-permute-start.16 = (bf16[96,2688]{1,0:T(8,128)(2,1)S(1)}, bf16[96,2688]{1,0:T(8,128)(2,1)S(1)}, u32[]{:S(2)}, u32[]{:S(2)}) collective-permute-start(bf16[96,2688]{1,0:T(8,128)(2,1)S(1)} %collective-permute-done.15.refs_1_), channel_id=1, source_target_pairs={{0,7},{1,0},{2,1},{3,2},{4,3},{5,4},{6,5},{7,6},{8,15},{9,8},{10,9... | collective-permute-start | bytes 1548296 | tf_op jit(solution)/shard_map/ppermute | solution.py:23
  40.0 3.5 %collective-permute-start.9 = (bf16[288,2688]{1,0:T(8,128)(2,1)}, bf16[288,2688]{1,0:T(8,128)(2,1)}, u32[]{:S(2)}, u32[]{:S(2)}) collective-permute-start(bf16[288,2688]{1,0:T(8,128)(2,1)} %get-tuple-element.270), channel_id=1, source_target_pairs={{0,8},{8,0},{1,9},{9,1},{2,10},{10,2},{3,11},{11,3},{4,12},{12,4},... | collective-permute-start | bytes 4644872 | tf_op jit(solution)/shard_map/ppermute | solution.py:18
  43.7 4.0 %collective-permute-done.13.refs_0_ = bf16[96,2688]{1,0:T(8,128)(2,1)S(1)} collective-permute-done((bf16[96,2688]{1,0:T(8,128)(2,1)S(1)}, bf16[96,2688]{1,0:T(8,128)(2,1)S(1)}, u32[]{:S(2)}, u32[]{:S(2)}) %collective-permute-start.13) | collective-permute-done | bytes 516128 | tf_op jit(solution)/shard_map/ppermute | solution.py:23
  48.0 4.2 %collective-permute-start.21 = (bf16[192,2688]{1,0:T(8,128)(2,1)S(1)}, bf16[192,2688]{1,0:T(8,128)(2,1)S(1)}, u32[]{:S(2)}, u32[]{:S(2)}) collective-permute-start(bf16[192,2688]{1,0:T(8,128)(2,1)S(1)} %pad_maximum_fusion.2), channel_id=1, source_target_pairs={{0,8},{8,0},{1,9},{9,1},{2,10},{10,2},{3,11},{11,3},{4,12},{12,4},... | collective-permute-start | bytes 3096584 | tf_op jit(solution)/shard_map/ppermute | solution.py:18
  52.2 3.5 %collective-permute-start.17 = (bf16[48,2688]{1,0:T(8,128)(2,1)S(1)}, bf16[48,2688]{1,0:T(8,128)(2,1)S(1)}, u32[]{:S(2)}, u32[]{:S(2)}) collective-permute-start(bf16[48,2688]{1,0:T(8,128)(2,1)S(1)} %slice.160), channel_id=1, source_target_pairs={{0,7},{1,0},{2,1},{3,2},{4,3},{5,4},{6,5},{7,6},{8,15},{9,8},{10,9... | collective-permute-start | bytes 774152 | tf_op jit(solution)/shard_map/ppermute | solution.py:23
  55.7 5.5 %collective-permute-done.17 = bf16[48,2688]{1,0:T(8,128)(2,1)S(1)} collective-permute-done((bf16[48,2688]{1,0:T(8,128)(2,1)S(1)}, bf16[48,2688]{1,0:T(8,128)(2,1)S(1)}, u32[]{:S(2)}, u32[]{:S(2)}) %collective-permute-start.17) | collective-permute-done | bytes 258080 | tf_op jit(solution)/shard_map/ppermute | solution.py:23
  62.4 8.9 %expert.7 = (bf16[192,2560]{1,0:T(8,128)(2,1)S(1)}, bf16[192,2560]{1,0:T(8,128)(2,1)S(1)}) custom-call(s32[1]{0:T(128)} %bitcast.me_ref, bf16[96,2688]{1,0:T(8,128)(2,1)S(1)} %collective-permute-done.12.refs_0_, bf16[96,2688]{1,0:T(8,128)(2,1)S(1)} %collective-permute-done.15.refs_1_, bf16[192,2688]{1,0:T(8,128)(2,1)S(1)} %collective-permute-done.24.refs_2_, ...), custom_call_target="tpu_custom_call" | custom-call | flops 2642411520 | bytes 10813440 | tf_op jit(solution)/shard_map/expert/pallas_call | solution.py:139
  71.4 6.1 %expert.5 = (bf16[96,2560]{1,0:T(8,128)(2,1)S(1)}, bf16[96,2560]{1,0:T(8,128)(2,1)S(1)}) custom-call(s32[1]{0:T(128)} %bitcast.me_ref, bf16[96,2688]{1,0:T(8,128)(2,1)S(1)} %constant_dynamic-update-slice_fusion.10.refs_0_, bf16[96,2688]{1,0:T(8,128)(2,1)S(1)} %collective-permute-done.18.refs_1_, bf16[4,224,2560]{2,1,0:T(8,128)(2,1)} %bitcast.21, ...), custom_call_target="tpu_custom_call" | custom-call | flops 1321205760 | bytes 8847360 | tf_op jit(solution)/shard_map/expert/pallas_call | solution.py:139
  78.1 12.0 %expert.4 = (bf16[288,2560]{1,0:T(8,128)(2,1)S(1)}, bf16[288,2560]{1,0:T(8,128)(2,1)}) custom-call(s32[1]{0:T(128)} %bitcast.me_ref, bf16[96,2688]{1,0:T(8,128)(2,1)S(1)} %pad_maximum_fusion.6.refs_0_, bf16[96,2688]{1,0:T(8,128)(2,1)S(1)} %get-tuple-element.275.refs_1_, bf16[96,2688]{1,0:T(8,128)(2,1)S(1)} %get-tuple-element.271.refs_2_, ...), custom_call_target="tpu_custom_call" | custom-call | flops 3963617280 | bytes 12779520 | tf_op jit(solution)/shard_map/expert/pallas_call | solution.py:139
  90.3 8.9 %expert.6 = (bf16[192,2560]{1,0:T(8,128)(2,1)S(1)}, bf16[192,2560]{1,0:T(8,128)(2,1)S(1)}) custom-call(s32[1]{0:T(128)} %bitcast.me_ref, bf16[96,2688]{1,0:T(8,128)(2,1)S(1)} %collective-permute-done.13.refs_0_, bf16[96,2688]{1,0:T(8,128)(2,1)S(1)} %collective-permute-done.16.refs_1_, bf16[192,2688]{1,0:T(8,128)(2,1)S(1)} %collective-permute-done.21.refs_2_, ...), custom_call_target="tpu_custom_call" | custom-call | flops 2642411520 | bytes 10813440 | tf_op jit(solution)/shard_map/expert/pallas_call | solution.py:139
  101.5 5.7 %collective-permute-done.20 = bf16[48,2560]{1,0:T(8,128)(2,1)S(1)} collective-permute-done((bf16[48,2560]{1,0:T(8,128)(2,1)S(1)}, bf16[48,2560]{1,0:T(8,128)(2,1)S(1)}, u32[]{:S(2)}, u32[]{:S(2)}) %collective-permute-start.20) | collective-permute-done | bytes 245792 | tf_op jit(solution)/shard_map/ppermute | solution.py:18
  109.3 8.5 %collective-permute-done.26 = bf16[96,2560]{1,0:T(8,128)(2,1)S(1)} collective-permute-done((bf16[96,2560]{1,0:T(8,128)(2,1)S(1)}, bf16[96,2560]{1,0:T(8,128)(2,1)S(1)}, u32[]{:S(2)}, u32[]{:S(2)}) %collective-permute-start.26) | collective-permute-done | bytes 491552 | tf_op jit(solution)/shard_map/ppermute | solution.py:18
  118.0 26.1 %collective-permute-done.23 = bf16[96,2560]{1,0:T(8,128)(2,1)S(1)} collective-permute-done((bf16[96,2560]{1,0:T(8,128)(2,1)S(1)}, bf16[96,2560]{1,0:T(8,128)(2,1)S(1)}, u32[]{:S(2)}, u32[]{:S(2)}) %collective-permute-start.23) | collective-permute-done | bytes 491552 | tf_op jit(solution)/shard_map/ppermute | solution.py:18
  146.7 37.3 %while.30 = (s32[]{:T(128)}, bf16[48,2560]{1,0:T(8,128)(2,1)S(1)}, bf16[48,2560]{1,0:T(8,128)(2,1)S(1)}, bf16[192,2560]{1,0:T(8,128)(2,1)}, bf16[192,2560]{1,0:T...) while((s32[]{:T(128)}, bf16[48,2560]{1,0:T(8,128)(2,1)S(1)}, bf16[48,2560]{1,0:T(8,128)(2,1)S(1)}, ...), condition=%wide.region_2.3_spmd, body=%wide.region_1.2_spmd.sunk | while | flops 983046 | bytes 3440867 | solution.py:54
  148.9 3.4 %collective-permute-start.1 = (bf16[48,2560]{1,0:T(8,128)(2,1)S(1)}, bf16[48,2560]{1,0:T(8,128)(2,1)S(1)}, u32[]{:S(2)}, u32[]{:S(2)}) collective-permute-start(bf16[48,2560]{1,0:T(8,128)(2,1)S(1)} %add_convert_fusion.21), channel_id=1, source_target_pairs={{0,7},{1,0},{2,1},{3,2},{4,3},{5,4},{6,5},{7,6},{8,15},{9,8},{10,9... | collective-permute-start | bytes 737288 | tf_op jit(solution)/shard_map/while/body/eval_jaxpr/ppermute | solution.py:23
  152.3 4.2 %collective-permute-done = bf16[48,2560]{1,0:T(8,128)(2,1)S(1)} collective-permute-done((bf16[48,2560]{1,0:T(8,128)(2,1)S(1)}, bf16[48,2560]{1,0:T(8,128)(2,1)S(1)}, u32[]{:S(2)}, u32[]{:S(2)}) %collective-permute-start) | collective-permute-done | bytes 245792 | tf_op jit(solution)/shard_map/while/body/eval_jaxpr/ppermute | solution.py:23
  157.6 2.5 collective-permute-start
  162.2 3.4 %collective-permute-done = bf16[48,2560]{1,0:T(8,128)(2,1)S(1)} collective-permute-done((bf16[48,2560]{1,0:T(8,128)(2,1)S(1)}, bf16[48,2560]{1,0:T(8,128)(2,1)S(1)}, u32[]{:S(2)}, u32[]{:S(2)}) %collective-permute-start) | collective-permute-done | bytes 245792 | tf_op jit(solution)/shard_map/while/body/eval_jaxpr/ppermute | solution.py:23
  171.4 2.5 collective-permute-done
  180.2 2.5 collective-permute-done
  185.6 2.1 collective-permute-start.27
  188.6 3.6 %collective-permute-done.27.refs_1_ = bf16[48,2560]{1,0:T(8,128)(2,1)S(1)} collective-permute-done((bf16[48,2560]{1,0:T(8,128)(2,1)S(1)}, bf16[48,2560]{1,0:T(8,128)(2,1)S(1)}, u32[]{:S(2)}, u32[]{:S(2)}) %collective-permute-start.27) | collective-permute-done | bytes 245792 | tf_op jit(solution)/shard_map/ppermute | solution.py:23
  192.7 2.1 collective-permute-start.30
  194.9 5.9 %collective-permute-done.29.refs_3_ = bf16[48,2560]{1,0:T(8,128)(2,1)S(1)} collective-permute-done((bf16[48,2560]{1,0:T(8,128)(2,1)S(1)}, bf16[48,2560]{1,0:T(8,128)(2,1)S(1)}, u32[]{:S(2)}, u32[]{:S(2)}) %collective-permute-start.29) | collective-permute-done | bytes 245792 | tf_op jit(solution)/shard_map/ppermute | solution.py:23
  200.8 3.2 %collective-permute-start.32 = (bf16[48,2560]{1,0:T(8,128)(2,1)S(1)}, bf16[48,2560]{1,0:T(8,128)(2,1)S(1)}, u32[]{:S(2)}, u32[]{:S(2)}) collective-permute-start(bf16[48,2560]{1,0:T(8,128)(2,1)S(1)} %collective-permute-done.30.refs_4_), channel_id=1, source_target_pairs={{0,7},{1,0},{2,1},{3,2},{4,3},{5,4},{6,5},{7,6},{8,15},{9,8},{10,9... | collective-permute-start | bytes 737288 | tf_op jit(solution)/shard_map/ppermute | solution.py:23
  204.0 5.7 %project.2 = (bf16[240,256]{1,0:T(8,128)(2,1)}, bf16[240,512]{1,0:T(8,128)(2,1)}) custom-call(bf16[48,2560]{1,0:T(8,128)(2,1)} %copy-done.9, bf16[48,2560]{1,0:T(8,128)(2,1)} %copy-done.13, bf16[48,2560]{1,0:T(8,128)(2,1)} %copy-done.14, bf16[48,2560]{1,0:T(8,128)(2,1)} %copy-done.16, bf16[48,2560]{1,0:T(8,128)(2,1)} %copy-done.15, ...), custom_call_target="tpu_custom_call" | custom-call | flops 943718400 | bytes 5160960 | tf_op jit(solution)/shard_map/project/pallas_call | solution.py:212
  211.3 2.7 collective-permute-start.34
  216.4 12.9 %all_gather.3.refs_2_ = bf16[960,512]{1,0:T(8,128)(2,1)S(1)} all-gather(bf16[480,512]{1,0:T(8,128)(2,1)S(1)} %pad_maximum_fusion.7), channel_id=1, replica_groups=mesh['set'=8,'exp_0'=2,'exp_1'=2,'seq'=8] {'exp_1'}, dimensions={0}, use_global_device_ids=true | all-gather | bytes 1474560 | tf_op jit(solution)/shard_map/all_gather | solution.py:398
  230.0 5.2 %project.3 = (bf16[144,256]{1,0:T(8,128)(2,1)}, bf16[144,512]{1,0:T(8,128)(2,1)}) custom-call(bf16[48,2560]{1,0:T(8,128)(2,1)} %copy-done.11, bf16[48,2560]{1,0:T(8,128)(2,1)} %copy-done.12, bf16[48,2560]{1,0:T(8,128)(2,1)} %pad_maximum_fusion.9.refs_2_, bf16[3,2560,256]{2,1,0:T(8,128)(2,1)} %bitcast.19, f32[1,128]{1,0:T(1,128)} %bitcast.29, f32[1,128]{1,0:T(1,128)} %bitcast.31), custom_call_target="tpu_custom_call" | custom-call | flops 566231040 | bytes 4669440 | tf_op jit(solution)/shard_map/project/pallas_call | solution.py:212
  237.5 3.0 %collective-permute-done.36 = bf16[144,512]{1,0:T(8,128)(2,1)S(1)} collective-permute-done((bf16[144,512]{1,0:T(8,128)(2,1)}, bf16[144,512]{1,0:T(8,128)(2,1)S(1)}, u32[]{:S(2)}, u32[]{:S(2)}) %collective-permute-start.36) | collective-permute-done | bytes 147488 | tf_op jit(solution)/shard_map/ppermute | solution.py:18
  243.9 4.3 %attend.1 = (bf16[48,2560]{1,0:T(8,128)(2,1)S(1)}, bf16[48,2560]{1,0:T(8,128)(2,1)S(1)}, bf16[48,2560]{1,0:T(8,128)(2,1)S(1)}, bf16[48,2560]{1,0:T(8,128)(2,1)S(...) custom-call(bf16[240,256]{1,0:T(8,128)(2,1)S(1)} %copy-done.1, ...), custom_call_target="tpu_custom_call" | custom-call | flops 1107296256 | bytes 4849664 | tf_op jit(solution)/shard_map/attend/pallas_call | solution.py:300
  248.3 29.4 %while.31 = (s32[]{:T(128)}, bf16[48,2560]{1,0:T(8,128)(2,1)S(1)}, bf16[48,2560]{1,0:T(8,128)(2,1)S(1)}, bf16[192,2560]{1,0:T(8,128)(2,1)S(1)}, bf16[192,2560]{1...) while((s32[]{:T(128)}, bf16[48,2560]{1,0:T(8,128)(2,1)S(1)}, ...), condition=%wide.region_5.6_spmd, body=%wide.region_4.5_spmd.sunk | while | flops 983046 | bytes 3440867 | solution.py:54
  248.6 2.7 collective-permute-start.3
  251.3 5.5 %collective-permute-done.2 = bf16[48,2560]{1,0:T(8,128)(2,1)S(1)} collective-permute-done((bf16[48,2560]{1,0:T(8,128)(2,1)S(1)}, bf16[48,2560]{1,0:T(8,128)(2,1)S(1)}, u32[]{:S(2)}, u32[]{:S(2)}) %collective-permute-start.2) | collective-permute-done | bytes 245792 | tf_op jit(solution)/shard_map/while/body/eval_jaxpr/ppermute | solution.py:23
  257.1 2.7 collective-permute-start.3
  259.8 4.7 %collective-permute-done.2 = bf16[48,2560]{1,0:T(8,128)(2,1)S(1)} collective-permute-done((bf16[48,2560]{1,0:T(8,128)(2,1)S(1)}, bf16[48,2560]{1,0:T(8,128)(2,1)S(1)}, u32[]{:S(2)}, u32[]{:S(2)}) %collective-permute-start.2) | collective-permute-done | bytes 245792 | tf_op jit(solution)/shard_map/while/body/eval_jaxpr/ppermute | solution.py:23
  264.8 2.7 collective-permute-start.3
  267.5 3.8 %collective-permute-done.2 = bf16[48,2560]{1,0:T(8,128)(2,1)S(1)} collective-permute-done((bf16[48,2560]{1,0:T(8,128)(2,1)S(1)}, bf16[48,2560]{1,0:T(8,128)(2,1)S(1)}, u32[]{:S(2)}, u32[]{:S(2)}) %collective-permute-start.2) | collective-permute-done | bytes 245792 | tf_op jit(solution)/shard_map/while/body/eval_jaxpr/ppermute | solution.py:23
  271.6 2.7 collective-permute-start.3
  274.3 3.4 %collective-permute-done.2 = bf16[48,2560]{1,0:T(8,128)(2,1)S(1)} collective-permute-done((bf16[48,2560]{1,0:T(8,128)(2,1)S(1)}, bf16[48,2560]{1,0:T(8,128)(2,1)S(1)}, u32[]{:S(2)}, u32[]{:S(2)}) %collective-permute-start.2) | collective-permute-done | bytes 245792 | tf_op jit(solution)/shard_map/while/body/eval_jaxpr/ppermute | solution.py:23
  (158 shorter events, 51.5 us)
Async XLA Ops:
  4.4 7.7 %collective-permute-start.4 = (bf16[48,2688]{1,0:T(8,128)(2,1)S(1)}, bf16[48,2688]{1,0:T(8,128)(2,1)S(1)}, u32[]{:S(2)}, u32[]{:S(2)}) collective-permute-start(bf16[48,2688]{1,0:T(8,128)(2,1)S(1)} %get-tuple-element.279), channel_id=1, source_target_pairs={{0,16},{16,0},{1,17},{17,1},{2,18},{18,2},{3,19},{19,3},{4,20},{20... | collective-permute-start | bytes 774152 | tf_op jit(solution)/shard_map/ppermute | solution.py:18
  6.5 12.1 %collective-permute-start.5 = (bf16[48,2688]{1,0:T(8,128)(2,1)S(1)}, bf16[48,2688]{1,0:T(8,128)(2,1)S(1)}, u32[]{:S(2)}, u32[]{:S(2)}) collective-permute-start(bf16[48,2688]{1,0:T(8,128)(2,1)S(1)} %get-tuple-element.279), channel_id=1, source_target_pairs={{0,1},{1,2},{2,3},{3,4},{4,5},{5,6},{6,7},{7,0},{8,9},{9,10},{10,1... | collective-permute-start | bytes 774152 | tf_op jit(solution)/shard_map/ppermute | solution.py:23
  8.2 15.6 %collective-permute-start.7 = (bf16[48,2688]{1,0:T(8,128)(2,1)S(1)}, bf16[48,2688]{1,0:T(8,128)(2,1)S(1)}, u32[]{:S(2)}, u32[]{:S(2)}) collective-permute-start(bf16[48,2688]{1,0:T(8,128)(2,1)S(1)} %get-tuple-element.279), channel_id=1, source_target_pairs={{0,7},{1,0},{2,1},{3,2},{4,3},{5,4},{6,5},{7,6},{8,15},{9,8},{10,9... | collective-permute-start | bytes 774152 | tf_op jit(solution)/shard_map/ppermute | solution.py:23
  12.1 10.9 %collective-permute-start.6 = (bf16[48,2688]{1,0:T(8,128)(2,1)S(1)}, bf16[48,2688]{1,0:T(8,128)(2,1)S(1)}, u32[]{:S(2)}, u32[]{:S(2)}) collective-permute-start(bf16[48,2688]{1,0:T(8,128)(2,1)S(1)} %collective-permute-done.4), channel_id=1, source_target_pairs={{0,1},{1,2},{2,3},{3,4},{4,5},{5,6},{6,7},{7,0},{8,9},{9,10},{10,1... | collective-permute-start | bytes 774152 | tf_op jit(solution)/shard_map/ppermute | solution.py:23
  14.0 10.5 %collective-permute-start.8 = (bf16[48,2688]{1,0:T(8,128)(2,1)S(1)}, bf16[48,2688]{1,0:T(8,128)(2,1)S(1)}, u32[]{:S(2)}, u32[]{:S(2)}) collective-permute-start(bf16[48,2688]{1,0:T(8,128)(2,1)S(1)} %collective-permute-done.4), channel_id=1, source_target_pairs={{0,7},{1,0},{2,1},{3,2},{4,3},{5,4},{6,5},{7,6},{8,15},{9,8},{10,9... | collective-permute-start | bytes 774152 | tf_op jit(solution)/shard_map/ppermute | solution.py:23
  23.7 12.4 %collective-permute-start.12 = (bf16[96,2688]{1,0:T(8,128)(2,1)S(1)}, bf16[96,2688]{1,0:T(8,128)(2,1)S(1)}, u32[]{:S(2)}, u32[]{:S(2)}) collective-permute-start(bf16[96,2688]{1,0:T(8,128)(2,1)S(1)} %get-tuple-element.275.refs_1_), channel_id=1, source_target_pairs={{0,1},{1,2},{2,3},{3,4},{4,5},{5,6},{6,7},{7,0},{8,9},{9,10},{10,1... | collective-permute-start | bytes 1548296 | tf_op jit(solution)/shard_map/ppermute | solution.py:23
  25.2 11.4 %collective-permute-start.15 = (bf16[96,2688]{1,0:T(8,128)(2,1)S(1)}, bf16[96,2688]{1,0:T(8,128)(2,1)S(1)}, u32[]{:S(2)}, u32[]{:S(2)}) collective-permute-start(bf16[96,2688]{1,0:T(8,128)(2,1)S(1)} %get-tuple-element.271.refs_2_), channel_id=1, source_target_pairs={{0,7},{1,0},{2,1},{3,2},{4,3},{5,4},{6,5},{7,6},{8,15},{9,8},{10,9... | collective-permute-start | bytes 1548296 | tf_op jit(solution)/shard_map/ppermute | solution.py:23
  36.1 11.6 %collective-permute-start.13 = (bf16[96,2688]{1,0:T(8,128)(2,1)S(1)}, bf16[96,2688]{1,0:T(8,128)(2,1)S(1)}, u32[]{:S(2)}, u32[]{:S(2)}) collective-permute-start(bf16[96,2688]{1,0:T(8,128)(2,1)S(1)} %collective-permute-done.12.refs_0_), channel_id=1, source_target_pairs={{0,1},{1,2},{2,3},{3,4},{4,5},{5,6},{6,7},{7,0},{8,9},{9,10},{10,1... | collective-permute-start | bytes 1548296 | tf_op jit(solution)/shard_map/ppermute | solution.py:23
  36.6 11.3 %collective-permute-start.16 = (bf16[96,2688]{1,0:T(8,128)(2,1)S(1)}, bf16[96,2688]{1,0:T(8,128)(2,1)S(1)}, u32[]{:S(2)}, u32[]{:S(2)}) collective-permute-start(bf16[96,2688]{1,0:T(8,128)(2,1)S(1)} %collective-permute-done.15.refs_1_), channel_id=1, source_target_pairs={{0,7},{1,0},{2,1},{3,2},{4,3},{5,4},{6,5},{7,6},{8,15},{9,8},{10,9... | collective-permute-start | bytes 1548296 | tf_op jit(solution)/shard_map/ppermute | solution.py:23
  40.0 38.1 %collective-permute-start.9 = (bf16[288,2688]{1,0:T(8,128)(2,1)}, bf16[288,2688]{1,0:T(8,128)(2,1)}, u32[]{:S(2)}, u32[]{:S(2)}) collective-permute-start(bf16[288,2688]{1,0:T(8,128)(2,1)} %get-tuple-element.270), channel_id=1, source_target_pairs={{0,8},{8,0},{1,9},{9,1},{2,10},{10,2},{3,11},{11,3},{4,12},{12,4},... | collective-permute-start | bytes 4644872 | tf_op jit(solution)/shard_map/ppermute | solution.py:18
  43.6 18.8 %collective-permute-start.24 = (bf16[192,2688]{1,0:T(8,128)(2,1)S(1)}, bf16[192,2688]{1,0:T(8,128)(2,1)S(1)}, u32[]{:S(2)}, u32[]{:S(2)}) collective-permute-start(bf16[192,2688]{1,0:T(8,128)(2,1)S(1)} %pad_maximum_fusion.3), channel_id=1, source_target_pairs={{0,8},{8,0},{1,9},{9,1},{2,10},{10,2},{3,11},{11,3},{4,12},{12,4},... | collective-permute-start | bytes 3096584 | tf_op jit(solution)/shard_map/ppermute | solution.py:18
  47.7 7.9 %collective-permute-start.14 = (bf16[48,2688]{1,0:T(8,128)(2,1)S(1)}, bf16[48,2688]{1,0:T(8,128)(2,1)S(1)}, u32[]{:S(2)}, u32[]{:S(2)}) collective-permute-start(bf16[48,2688]{1,0:T(8,128)(2,1)S(1)} %slice.159), channel_id=1, source_target_pairs={{0,1},{1,2},{2,3},{3,4},{4,5},{5,6},{6,7},{7,0},{8,9},{9,10},{10,1... | collective-permute-start | bytes 774152 | tf_op jit(solution)/shard_map/ppermute | solution.py:23
  48.0 42.4 %collective-permute-start.21 = (bf16[192,2688]{1,0:T(8,128)(2,1)S(1)}, bf16[192,2688]{1,0:T(8,128)(2,1)S(1)}, u32[]{:S(2)}, u32[]{:S(2)}) collective-permute-start(bf16[192,2688]{1,0:T(8,128)(2,1)S(1)} %pad_maximum_fusion.2), channel_id=1, source_target_pairs={{0,8},{8,0},{1,9},{9,1},{2,10},{10,2},{3,11},{11,3},{4,12},{12,4},... | collective-permute-start | bytes 3096584 | tf_op jit(solution)/shard_map/ppermute | solution.py:18
  52.2 9.0 %collective-permute-start.17 = (bf16[48,2688]{1,0:T(8,128)(2,1)S(1)}, bf16[48,2688]{1,0:T(8,128)(2,1)S(1)}, u32[]{:S(2)}, u32[]{:S(2)}) collective-permute-start(bf16[48,2688]{1,0:T(8,128)(2,1)S(1)} %slice.160), channel_id=1, source_target_pairs={{0,7},{1,0},{2,1},{3,2},{4,3},{5,4},{6,5},{7,6},{8,15},{9,8},{10,9... | collective-permute-start | bytes 774152 | tf_op jit(solution)/shard_map/ppermute | solution.py:23
  61.2 10.2 %collective-permute-start.18 = (bf16[96,2688]{1,0:T(8,128)(2,1)S(1)}, bf16[96,2688]{1,0:T(8,128)(2,1)S(1)}, u32[]{:S(2)}, u32[]{:S(2)}) collective-permute-start(bf16[96,2688]{1,0:T(8,128)(2,1)S(1)} %constant_dynamic-update-slice_fusion.10.refs_0_), channel_id=1, source_target_pairs={{0,8},{8,0},{1,9},{9,1},{2,10},{10,2},{3,11},{11,3},{4,12},{12,4},... | collective-permute-start | bytes 1548296 | tf_op jit(solution)/shard_map/ppermute | solution.py:18
  71.3 29.8 %collective-permute-start.25 = (bf16[192,2560]{1,0:T(8,128)(2,1)S(1)}, bf16[192,2560]{1,0:T(8,128)(2,1)S(1)}, u32[]{:S(2)}, u32[]{:S(2)}) collective-permute-start(bf16[192,2560]{1,0:T(8,128)(2,1)S(1)} %get-tuple-element.222), channel_id=1, source_target_pairs={{0,8},{8,0},{1,9},{9,1},{2,10},{10,2},{3,11},{11,3},{4,12},{12,4},... | collective-permute-start | bytes 2949128 | tf_op jit(solution)/shard_map/ppermute | solution.py:18
  77.6 22.1 %collective-permute-start.19 = (bf16[96,2560]{1,0:T(8,128)(2,1)S(1)}, bf16[96,2560]{1,0:T(8,128)(2,1)S(1)}, u32[]{:S(2)}, u32[]{:S(2)}) collective-permute-start(bf16[96,2560]{1,0:T(8,128)(2,1)S(1)} %get-tuple-element.218), channel_id=1, source_target_pairs={{0,8},{8,0},{1,9},{9,1},{2,10},{10,2},{3,11},{11,3},{4,12},{12,4},... | collective-permute-start | bytes 1474568 | tf_op jit(solution)/shard_map/ppermute | solution.py:18
  90.2 17.2 %collective-permute-start.10 = (bf16[288,2560]{1,0:T(8,128)(2,1)}, bf16[288,2560]{1,0:T(8,128)(2,1)S(1)}, u32[]{:S(2)}, u32[]{:S(2)}) collective-permute-start(bf16[288,2560]{1,0:T(8,128)(2,1)} %get-tuple-element.216), channel_id=1, source_target_pairs={{0,8},{8,0},{1,9},{9,1},{2,10},{10,2},{3,11},{11,3},{4,12},{12,4},... | collective-permute-start | bytes 4423688 | tf_op jit(solution)/shard_map/ppermute | solution.py:18
  99.2 9.7 %collective-permute-start.22 = (bf16[192,2560]{1,0:T(8,128)(2,1)S(1)}, bf16[192,2560]{1,0:T(8,128)(2,1)S(1)}, u32[]{:S(2)}, u32[]{:S(2)}) collective-permute-start(bf16[192,2560]{1,0:T(8,128)(2,1)S(1)} %get-tuple-element.220), channel_id=1, source_target_pairs={{0,8},{8,0},{1,9},{9,1},{2,10},{10,2},{3,11},{11,3},{4,12},{12,4},... | collective-permute-start | bytes 2949128 | tf_op jit(solution)/shard_map/ppermute | solution.py:18
  99.8 7.5 %collective-permute-start.20 = (bf16[48,2560]{1,0:T(8,128)(2,1)S(1)}, bf16[48,2560]{1,0:T(8,128)(2,1)S(1)}, u32[]{:S(2)}, u32[]{:S(2)}) collective-permute-start(bf16[48,2560]{1,0:T(8,128)(2,1)S(1)} %add_convert_fusion.14), channel_id=1, source_target_pairs={{0,16},{16,0},{1,17},{17,1},{2,18},{18,2},{3,19},{19,3},{4,20},{20... | collective-permute-start | bytes 737288 | tf_op jit(solution)/shard_map/ppermute | solution.py:18
  101.3 16.5 %collective-permute-start.26 = (bf16[96,2560]{1,0:T(8,128)(2,1)S(1)}, bf16[96,2560]{1,0:T(8,128)(2,1)S(1)}, u32[]{:S(2)}, u32[]{:S(2)}) collective-permute-start(bf16[96,2560]{1,0:T(8,128)(2,1)S(1)} %add_convert_fusion.5), channel_id=1, source_target_pairs={{0,16},{16,0},{1,17},{17,1},{2,18},{18,2},{3,19},{19,3},{4,20},{20... | collective-permute-start | bytes 1474568 | tf_op jit(solution)/shard_map/ppermute | solution.py:18
  107.6 36.8 %collective-permute-start.11 = (bf16[144,2560]{1,0:T(8,128)(2,1)S(1)}, bf16[144,2560]{1,0:T(8,128)(2,1)S(1)}, u32[]{:S(2)}, u32[]{:S(2)}) collective-permute-start(bf16[144,2560]{1,0:T(8,128)(2,1)S(1)} %add_convert_fusion.4), channel_id=1, source_target_pairs={{0,16},{16,0},{1,17},{17,1},{2,18},{18,2},{3,19},{19,3},{4,20},{20... | collective-permute-start | bytes 2211848 | tf_op jit(solution)/shard_map/ppermute | solution.py:18
  109.1 35.0 %collective-permute-start.23 = (bf16[96,2560]{1,0:T(8,128)(2,1)S(1)}, bf16[96,2560]{1,0:T(8,128)(2,1)S(1)}, u32[]{:S(2)}, u32[]{:S(2)}) collective-permute-start(bf16[96,2560]{1,0:T(8,128)(2,1)S(1)} %add_convert_fusion.6), channel_id=1, source_target_pairs={{0,16},{16,0},{1,17},{17,1},{2,18},{18,2},{3,19},{19,3},{4,20},{20... | collective-permute-start | bytes 1474568 | tf_op jit(solution)/shard_map/ppermute | solution.py:18
  147.8 8.7 %collective-permute-start = (bf16[48,2560]{1,0:T(8,128)(2,1)S(1)}, bf16[48,2560]{1,0:T(8,128)(2,1)S(1)}, u32[]{:S(2)}, u32[]{:S(2)}) collective-permute-start(bf16[48,2560]{1,0:T(8,128)(2,1)S(1)} %add_convert_fusion.20), channel_id=1, source_target_pairs={{0,1},{1,2},{2,3},{3,4},{4,5},{5,6},{6,7},{7,0},{8,9},{9,10},{10,1... | collective-permute-start | bytes 737288 | tf_op jit(solution)/shard_map/while/body/eval_jaxpr/ppermute | solution.py:23
  148.9 7.7 %collective-permute-start.1 = (bf16[48,2560]{1,0:T(8,128)(2,1)S(1)}, bf16[48,2560]{1,0:T(8,128)(2,1)S(1)}, u32[]{:S(2)}, u32[]{:S(2)}) collective-permute-start(bf16[48,2560]{1,0:T(8,128)(2,1)S(1)} %add_convert_fusion.21), channel_id=1, source_target_pairs={{0,7},{1,0},{2,1},{3,2},{4,3},{5,4},{6,5},{7,6},{8,15},{9,8},{10,9... | collective-permute-start | bytes 737288 | tf_op jit(solution)/shard_map/while/body/eval_jaxpr/ppermute | solution.py:23
  157.6 8.0 %collective-permute-start = (bf16[48,2560]{1,0:T(8,128)(2,1)S(1)}, bf16[48,2560]{1,0:T(8,128)(2,1)S(1)}, u32[]{:S(2)}, u32[]{:S(2)}) collective-permute-start(bf16[48,2560]{1,0:T(8,128)(2,1)S(1)} %add_convert_fusion.20), channel_id=1, source_target_pairs={{0,1},{1,2},{2,3},{3,4},{4,5},{5,6},{6,7},{7,0},{8,9},{9,10},{10,1... | collective-permute-start | bytes 737288 | tf_op jit(solution)/shard_map/while/body/eval_jaxpr/ppermute | solution.py:23
  161.1 5.5 %collective-permute-start.1 = (bf16[48,2560]{1,0:T(8,128)(2,1)S(1)}, bf16[48,2560]{1,0:T(8,128)(2,1)S(1)}, u32[]{:S(2)}, u32[]{:S(2)}) collective-permute-start(bf16[48,2560]{1,0:T(8,128)(2,1)S(1)} %add_convert_fusion.21), channel_id=1, source_target_pairs={{0,7},{1,0},{2,1},{3,2},{4,3},{5,4},{6,5},{7,6},{8,15},{9,8},{10,9... | collective-permute-start | bytes 737288 | tf_op jit(solution)/shard_map/while/body/eval_jaxpr/ppermute | solution.py:23
  167.6 6.3 %collective-permute-start = (bf16[48,2560]{1,0:T(8,128)(2,1)S(1)}, bf16[48,2560]{1,0:T(8,128)(2,1)S(1)}, u32[]{:S(2)}, u32[]{:S(2)}) collective-permute-start(bf16[48,2560]{1,0:T(8,128)(2,1)S(1)} %add_convert_fusion.20), channel_id=1, source_target_pairs={{0,1},{1,2},{2,3},{3,4},{4,5},{5,6},{6,7},{7,0},{8,9},{9,10},{10,1... | collective-permute-start | bytes 737288 | tf_op jit(solution)/shard_map/while/body/eval_jaxpr/ppermute | solution.py:23
  169.9 5.5 %collective-permute-start.1 = (bf16[48,2560]{1,0:T(8,128)(2,1)S(1)}, bf16[48,2560]{1,0:T(8,128)(2,1)S(1)}, u32[]{:S(2)}, u32[]{:S(2)}) collective-permute-start(bf16[48,2560]{1,0:T(8,128)(2,1)S(1)} %add_convert_fusion.21), channel_id=1, source_target_pairs={{0,7},{1,0},{2,1},{3,2},{4,3},{5,4},{6,5},{7,6},{8,15},{9,8},{10,9... | collective-permute-start | bytes 737288 | tf_op jit(solution)/shard_map/while/body/eval_jaxpr/ppermute | solution.py:23
  176.3 6.3 %collective-permute-start = (bf16[48,2560]{1,0:T(8,128)(2,1)S(1)}, bf16[48,2560]{1,0:T(8,128)(2,1)S(1)}, u32[]{:S(2)}, u32[]{:S(2)}) collective-permute-start(bf16[48,2560]{1,0:T(8,128)(2,1)S(1)} %add_convert_fusion.20), channel_id=1, source_target_pairs={{0,1},{1,2},{2,3},{3,4},{4,5},{5,6},{6,7},{7,0},{8,9},{9,10},{10,1... | collective-permute-start | bytes 737288 | tf_op jit(solution)/shard_map/while/body/eval_jaxpr/ppermute | solution.py:23
  178.9 5.1 %collective-permute-start.1 = (bf16[48,2560]{1,0:T(8,128)(2,1)S(1)}, bf16[48,2560]{1,0:T(8,128)(2,1)S(1)}, u32[]{:S(2)}, u32[]{:S(2)}) collective-permute-start(bf16[48,2560]{1,0:T(8,128)(2,1)S(1)} %add_convert_fusion.21), channel_id=1, source_target_pairs={{0,7},{1,0},{2,1},{3,2},{4,3},{5,4},{6,5},{7,6},{8,15},{9,8},{10,9... | collective-permute-start | bytes 737288 | tf_op jit(solution)/shard_map/while/body/eval_jaxpr/ppermute | solution.py:23
  185.6 6.6 %collective-permute-start.27 = (bf16[48,2560]{1,0:T(8,128)(2,1)S(1)}, bf16[48,2560]{1,0:T(8,128)(2,1)S(1)}, u32[]{:S(2)}, u32[]{:S(2)}) collective-permute-start(bf16[48,2560]{1,0:T(8,128)(2,1)S(1)} %fusion.10.refs_0_), channel_id=1, source_target_pairs={{0,1},{1,2},{2,3},{3,4},{4,5},{5,6},{6,7},{7,0},{8,9},{9,10},{10,1... | collective-permute-start | bytes 737288 | tf_op jit(solution)/shard_map/ppermute | solution.py:23
  192.2 8.6 %collective-permute-start.29 = (bf16[48,2560]{1,0:T(8,128)(2,1)S(1)}, bf16[48,2560]{1,0:T(8,128)(2,1)S(1)}, u32[]{:S(2)}, u32[]{:S(2)}) collective-permute-start(bf16[48,2560]{1,0:T(8,128)(2,1)S(1)} %collective-permute-done.27.refs_1_), channel_id=1, source_target_pairs={{0,1},{1,2},{2,3},{3,4},{4,5},{5,6},{6,7},{7,0},{8,9},{9,10},{10,1... | collective-permute-start | bytes 737288 | tf_op jit(solution)/shard_map/ppermute | solution.py:23
  192.7 8.0 %collective-permute-start.30 = (bf16[48,2560]{1,0:T(8,128)(2,1)S(1)}, bf16[48,2560]{1,0:T(8,128)(2,1)S(1)}, u32[]{:S(2)}, u32[]{:S(2)}) collective-permute-start(bf16[48,2560]{1,0:T(8,128)(2,1)S(1)} %collective-permute-done.28.refs_2_), channel_id=1, source_target_pairs={{0,7},{1,0},{2,1},{3,2},{4,3},{5,4},{6,5},{7,6},{8,15},{9,8},{10,9... | collective-permute-start | bytes 737288 | tf_op jit(solution)/shard_map/ppermute | solution.py:23
  200.8 10.4 %collective-permute-start.31 = (bf16[48,2560]{1,0:T(8,128)(2,1)S(1)}, bf16[48,2560]{1,0:T(8,128)(2,1)S(1)}, u32[]{:S(2)}, u32[]{:S(2)}) collective-permute-start(bf16[48,2560]{1,0:T(8,128)(2,1)S(1)} %collective-permute-done.29.refs_3_), channel_id=1, source_target_pairs={{0,1},{1,2},{2,3},{3,4},{4,5},{5,6},{6,7},{7,0},{8,9},{9,10},{10,1... | collective-permute-start | bytes 737288 | tf_op jit(solution)/shard_map/ppermute | solution.py:23
  200.8 10.5 %collective-permute-start.32 = (bf16[48,2560]{1,0:T(8,128)(2,1)S(1)}, bf16[48,2560]{1,0:T(8,128)(2,1)S(1)}, u32[]{:S(2)}, u32[]{:S(2)}) collective-permute-start(bf16[48,2560]{1,0:T(8,128)(2,1)S(1)} %collective-permute-done.30.refs_4_), channel_id=1, source_target_pairs={{0,7},{1,0},{2,1},{3,2},{4,3},{5,4},{6,5},{7,6},{8,15},{9,8},{10,9... | collective-permute-start | bytes 737288 | tf_op jit(solution)/shard_map/ppermute | solution.py:23
  209.8 5.6 %collective-permute-start.35 = (bf16[240,512]{1,0:T(8,128)(2,1)}, bf16[240,512]{1,0:T(8,128)(2,1)S(1)}, u32[]{:S(2)}, u32[]{:S(2)}) collective-permute-start(bf16[240,512]{1,0:T(8,128)(2,1)} %get-tuple-element.226), channel_id=1, source_target_pairs={{0,16},{16,0},{1,17},{17,1},{2,18},{18,2},{3,19},{19,3},{4,20},{20... | collective-permute-start | bytes 737288 | tf_op jit(solution)/shard_map/ppermute | solution.py:18
  211.2 18.1 %collective-permute-start.33 = (bf16[24,2560]{1,0:T(8,128)(2,1)S(1)}, bf16[24,2560]{1,0:T(8,128)(2,1)S(1)}, u32[]{:S(2)}, u32[]{:S(2)}) collective-permute-start(bf16[24,2560]{1,0:T(8,128)(2,1)S(1)} %slice.177), channel_id=1, source_target_pairs={{0,1},{1,2},{2,3},{3,4},{4,5},{5,6},{6,7},{7,0},{8,9},{9,10},{10,1... | collective-permute-start | bytes 368648 | tf_op jit(solution)/shard_map/ppermute | solution.py:23
  211.3 18.0 %collective-permute-start.34 = (bf16[24,2560]{1,0:T(8,128)(2,1)S(1)}, bf16[24,2560]{1,0:T(8,128)(2,1)S(1)}, u32[]{:S(2)}, u32[]{:S(2)}) collective-permute-start(bf16[24,2560]{1,0:T(8,128)(2,1)S(1)} %slice.178), channel_id=1, source_target_pairs={{0,7},{1,0},{2,1},{3,2},{4,3},{5,4},{6,5},{7,6},{8,15},{9,8},{10,9... | collective-permute-start | bytes 368648 | tf_op jit(solution)/shard_map/ppermute | solution.py:23
  235.1 5.3 %collective-permute-start.36 = (bf16[144,512]{1,0:T(8,128)(2,1)}, bf16[144,512]{1,0:T(8,128)(2,1)S(1)}, u32[]{:S(2)}, u32[]{:S(2)}) collective-permute-start(bf16[144,512]{1,0:T(8,128)(2,1)} %get-tuple-element.231), channel_id=1, source_target_pairs={{0,16},{16,0},{1,17},{17,1},{2,18},{18,2},{3,19},{19,3},{4,20},{20... | collective-permute-start | bytes 442376 | tf_op jit(solution)/shard_map/ppermute | solution.py:18
  248.4 8.4 %collective-permute-start.2 = (bf16[48,2560]{1,0:T(8,128)(2,1)S(1)}, bf16[48,2560]{1,0:T(8,128)(2,1)S(1)}, u32[]{:S(2)}, u32[]{:S(2)}) collective-permute-start(bf16[48,2560]{1,0:T(8,128)(2,1)S(1)} %add_convert_fusion.22), channel_id=1, source_target_pairs={{0,1},{1,2},{2,3},{3,4},{4,5},{5,6},{6,7},{7,0},{8,9},{9,10},{10,1... | collective-permute-start | bytes 737288 | tf_op jit(solution)/shard_map/while/body/eval_jaxpr/ppermute | solution.py:23
  248.6 8.3 %collective-permute-start.3 = (bf16[48,2560]{1,0:T(8,128)(2,1)S(1)}, bf16[48,2560]{1,0:T(8,128)(2,1)S(1)}, u32[]{:S(2)}, u32[]{:S(2)}) collective-permute-start(bf16[48,2560]{1,0:T(8,128)(2,1)S(1)} %add_convert_fusion.23), channel_id=1, source_target_pairs={{0,7},{1,0},{2,1},{3,2},{4,3},{5,4},{6,5},{7,6},{8,15},{9,8},{10,9... | collective-permute-start | bytes 737288 | tf_op jit(solution)/shard_map/while/body/eval_jaxpr/ppermute | solution.py:23
  257.0 7.6 %collective-permute-start.2 = (bf16[48,2560]{1,0:T(8,128)(2,1)S(1)}, bf16[48,2560]{1,0:T(8,128)(2,1)S(1)}, u32[]{:S(2)}, u32[]{:S(2)}) collective-permute-start(bf16[48,2560]{1,0:T(8,128)(2,1)S(1)} %add_convert_fusion.22), channel_id=1, source_target_pairs={{0,1},{1,2},{2,3},{3,4},{4,5},{5,6},{6,7},{7,0},{8,9},{9,10},{10,1... | collective-permute-start | bytes 737288 | tf_op jit(solution)/shard_map/while/body/eval_jaxpr/ppermute | solution.py:23
  257.1 7.4 %collective-permute-start.3 = (bf16[48,2560]{1,0:T(8,128)(2,1)S(1)}, bf16[48,2560]{1,0:T(8,128)(2,1)S(1)}, u32[]{:S(2)}, u32[]{:S(2)}) collective-permute-start(bf16[48,2560]{1,0:T(8,128)(2,1)S(1)} %add_convert_fusion.23), channel_id=1, source_target_pairs={{0,7},{1,0},{2,1},{3,2},{4,3},{5,4},{6,5},{7,6},{8,15},{9,8},{10,9... | collective-permute-start | bytes 737288 | tf_op jit(solution)/shard_map/while/body/eval_jaxpr/ppermute | solution.py:23
  264.6 6.7 %collective-permute-start.2 = (bf16[48,2560]{1,0:T(8,128)(2,1)S(1)}, bf16[48,2560]{1,0:T(8,128)(2,1)S(1)}, u32[]{:S(2)}, u32[]{:S(2)}) collective-permute-start(bf16[48,2560]{1,0:T(8,128)(2,1)S(1)} %add_convert_fusion.22), channel_id=1, source_target_pairs={{0,1},{1,2},{2,3},{3,4},{4,5},{5,6},{6,7},{7,0},{8,9},{9,10},{10,1... | collective-permute-start | bytes 737288 | tf_op jit(solution)/shard_map/while/body/eval_jaxpr/ppermute | solution.py:23
  264.8 6.6 %collective-permute-start.3 = (bf16[48,2560]{1,0:T(8,128)(2,1)S(1)}, bf16[48,2560]{1,0:T(8,128)(2,1)S(1)}, u32[]{:S(2)}, u32[]{:S(2)}) collective-permute-start(bf16[48,2560]{1,0:T(8,128)(2,1)S(1)} %add_convert_fusion.23), channel_id=1, source_target_pairs={{0,7},{1,0},{2,1},{3,2},{4,3},{5,4},{6,5},{7,6},{8,15},{9,8},{10,9... | collective-permute-start | bytes 737288 | tf_op jit(solution)/shard_map/while/body/eval_jaxpr/ppermute | solution.py:23
  271.4 6.3 %collective-permute-start.2 = (bf16[48,2560]{1,0:T(8,128)(2,1)S(1)}, bf16[48,2560]{1,0:T(8,128)(2,1)S(1)}, u32[]{:S(2)}, u32[]{:S(2)}) collective-permute-start(bf16[48,2560]{1,0:T(8,128)(2,1)S(1)} %add_convert_fusion.22), channel_id=1, source_target_pairs={{0,1},{1,2},{2,3},{3,4},{4,5},{5,6},{6,7},{7,0},{8,9},{9,10},{10,1... | collective-permute-start | bytes 737288 | tf_op jit(solution)/shard_map/while/body/eval_jaxpr/ppermute | solution.py:23
  271.6 6.2 %collective-permute-start.3 = (bf16[48,2560]{1,0:T(8,128)(2,1)S(1)}, bf16[48,2560]{1,0:T(8,128)(2,1)S(1)}, u32[]{:S(2)}, u32[]{:S(2)}) collective-permute-start(bf16[48,2560]{1,0:T(8,128)(2,1)S(1)} %add_convert_fusion.23), channel_id=1, source_target_pairs={{0,7},{1,0},{2,1},{3,2},{4,3},{5,4},{6,5},{7,6},{8,15},{9,8},{10,9... | collective-permute-start | bytes 737288 | tf_op jit(solution)/shard_map/while/body/eval_jaxpr/ppermute | solution.py:23
  (20 other events, 322.3 us)

commit v2 on v1

--- a/solution.py
+++ b/solution.py
@@ -224,7 +224,7 @@
             pltpu.SemaphoreType.DMA((n,)),
             pltpu.SemaphoreType.DMA((nk,)),
         ],
-        compiler_params=pltpu.CompilerParams(vmem_limit_bytes=58 * 2**20),
+        compiler_params=pltpu.CompilerParams(vmem_limit_bytes=16 * 2**20),
         cost_estimate=pl.CostEstimate(
             flops=2 * m * dim * cols, bytes_accessed=2 * dim * cols + 2 * m * dim, transcendentals=0
         ),
@@ -366,7 +366,8 @@
         ]
 
     up2, down2 = shift(up1, 1), shift(down1, -1)
-    own_terms, b1, a1 = experts([column, up1, down1])
+    (own_terms,) = experts([column])
+    b1, a1 = experts([up1, down1])
     up3, down3 = shift(up2, 1), shift(down2, -1)
     b2, a2 = experts([up2, down2])
     far_up, far_down = shift(up3[:rows], 1), shift(down3[rows:], -1)
@@ -389,15 +390,14 @@
         beside = swap(kv, "exp_0")
         return q, jnp.concatenate([kv, beside], 0)
 
-    half = rows // 2
     up1, down1 = shift(attn_in, 1), shift(attn_in, -1)
     up2, down2 = shift(up1, 1), shift(down1, -1)
     up3, down3 = shift(up2, 1), shift(down2, -1)
     q_a, kv_a = project([attn_in, up1, down1, up2, down2])
-    far = (shift(up3[:half], 1), shift(down3[half:], -1))
+    far = shift(up3, 1)
     kv_a = lax.all_gather(kv_a, "exp_1", axis=0, tiled=True)
     far, kv_a = tied(far, kv_a)
-    q_b, kv_b = project([up3, down3, jnp.concatenate(far, 0)])
+    q_b, kv_b = project([up3, down3, far])
     kvs = [kv_a, kv_b, swap(kv_b, "exp_1")]
     piece = attend_call([q_a, q_b], kvs, w_out, heads, rows)
     from_below, from_above = ring_scatter(

time: 282 us -> 255 us (0.904)
  waiting for transfers between devices: 111 us -> 96.6 us
  other arithmetic: 19.2 us -> 7.42 us
    ppermute x16 -> x19, waiting for transfers between devices: 46 us -> 31.3 us  [swap(): return lax.ppermute(value, axis, [(0, 1), (1, 0)])]
    convert_element_type x24 -> x25, other arithmetic: 9.74 us -> 2.09 us  [added(): return total.astype(jnp.bfloat16)]
    ppermute x34 -> x33, starting transfers between devices: 56.7 us -> 52.1 us  [shift(): return lax.ppermute(value, 'seq', [(i, (i + step) % n) for i in range(n)])]
    ppermute x16 -> x19, starting transfers between devices: 19.7 us -> 24.1 us  [swap(): return lax.ppermute(value, axis, [(0, 1), (1, 0)])]
    pallas_call x2, Pallas kernels: 10.9 us -> 7.6 us  [project_call(): pl.pallas_call(kernel, out_shape=[jax.ShapeDtypeStruct((m, width), jnp.bf...]
    pallas_call x4 -> x5, Pallas kernels: 36 us -> 38.2 us  [expert_call(): pl.pallas_call(kernel, out_shape=[jax.ShapeDtypeStruct((m1, dim), jnp.bfl...]
    ppermute x34 -> x33, waiting for transfers between devices: 65.3 us -> 65.4 us  [shift(): return lax.ppermute(value, 'seq', [(i, (i + step) % n) for i in range(n)])]
  transfers between devices with their start and end apart: 50 -> 52, of which waited for: 26 -> 22; matrix products, arithmetic and copies ran while one was open for 4% -> 1% of each run, Pallas kernels for 15% -> 17%
where the time goes in v2:
time: 255 us; the launch traced here: 252 us
  waiting for transfers between devices  96.6 us (38%)
  starting transfers between devices  76.2 us (30%)
  Pallas kernels  50 us (20%)
  blocking collectives  12.9 us (5%)
  local copies, waits for them, and re-layouts  8.06 us (3%)
  other arithmetic  7.42 us (3%)
    ppermute x33, waiting for transfers between devices, shift(): return lax.ppermute(value, 'seq', [(i, (i + step) % n) for i in range(n)])  65.4 us
    ppermute x33, starting transfers between devices, shift(): return lax.ppermute(value, 'seq', [(i, (i + step) % n) for i in range(n)])  52.1 us
    pallas_call x5, Pallas kernels, expert_call(): pl.pallas_call(kernel, out_shape=[jax.ShapeDtypeStruct((m1, dim), jnp.bfl...  38.2 us
    ppermute x19, waiting for transfers between devices, swap(): return lax.ppermute(value, axis, [(0, 1), (1, 0)])  31.3 us
    ppermute x19, starting transfers between devices, swap(): return lax.ppermute(value, axis, [(0, 1), (1, 0)])  24.1 us
    all_gather x1, blocking collectives, shards(): kv_a = lax.all_gather(kv_a, 'exp_1', axis=0, tiled=True)  12.9 us
    pallas_call x2, Pallas kernels, project_call(): pl.pallas_call(kernel, out_shape=[jax.ShapeDtypeStruct((m, width), jnp.bf...  7.6 us
    unnamed x42, local copies, waits for them, and re-layouts  6.32 us
  transfers between devices with their start and end apart: 52, of which 22 were waited for; matrix products, arithmetic and copies ran while one was open for 1% of the time, Pallas kernels for 17%

profile of v2, /device:TPU:1, one launch (start us, length us, event | category | flops | bytes accessed | tf_op | source)
XLA Modules:
  0.0 252.4 jit_solution(2562490750215877335)
XLA Ops:
  3.7 2.2 collective-permute-start.4
  7.6 3.9 %collective-permute-start.13 = (bf16[48,2688]{1,0:T(8,128)(2,1)S(1)}, bf16[48,2688]{1,0:T(8,128)(2,1)S(1)}, u32[]{:S(2)}, u32[]{:S(2)}) collective-permute-start(bf16[48,2688]{1,0:T(8,128)(2,1)S(1)} %pad_maximum_fusion.9), channel_id=1, source_target_pairs={{0,7},{1,0},{2,1},{3,2},{4,3},{5,4},{6,5},{7,6},{8,15},{9,8},{10,9... | collective-permute-start | bytes 774152 | tf_op jit(solution)/shard_map/ppermute | solution.py:23
  11.5 1.9 collective-permute-start.5
  15.0 3.9 %collective-permute-start.14 = (bf16[48,2688]{1,0:T(8,128)(2,1)S(1)}, bf16[48,2688]{1,0:T(8,128)(2,1)S(1)}, u32[]{:S(2)}, u32[]{:S(2)}) collective-permute-start(bf16[48,2688]{1,0:T(8,128)(2,1)S(1)} %collective-permute-done.4), channel_id=1, source_target_pairs={{0,7},{1,0},{2,1},{3,2},{4,3},{5,4},{6,5},{7,6},{8,15},{9,8},{10,9... | collective-permute-start | bytes 774152 | tf_op jit(solution)/shard_map/ppermute | solution.py:23
  19.7 5.8 %collective-permute-done.9 = bf16[48,2688]{1,0:T(8,128)(2,1)S(1)} collective-permute-done((bf16[48,2688]{1,0:T(8,128)(2,1)S(1)}, bf16[48,2688]{1,0:T(8,128)(2,1)S(1)}, u32[]{:S(2)}, u32[]{:S(2)}) %collective-permute-start.9) | collective-permute-done | bytes 258080 | tf_op jit(solution)/shard_map/ppermute | solution.py:23
  27.7 2.7 %collective-permute-start.15 = (bf16[96,2688]{1,0:T(8,128)(2,1)S(1)}, bf16[96,2688]{1,0:T(8,128)(2,1)S(1)}, u32[]{:S(2)}, u32[]{:S(2)}) collective-permute-start(bf16[96,2688]{1,0:T(8,128)(2,1)S(1)} %constant_dynamic-update-slice_fusion.2.refs_1_), channel_id=1, source_target_pairs={{0,7},{1,0},{2,1},{3,2},{4,3},{5,4},{6,5},{7,6},{8,15},{9,8},{10,9... | collective-permute-start | bytes 1548296 | tf_op jit(solution)/shard_map/ppermute | solution.py:23
  30.4 6.1 %expert.5 = (bf16[96,2560]{1,0:T(8,128)(2,1)S(1)}, bf16[96,2560]{1,0:T(8,128)(2,1)S(1)}) custom-call(s32[1]{0:T(128)} %bitcast.me_ref, bf16[96,2688]{1,0:T(8,128)(2,1)S(1)} %pad_maximum_fusion.7.refs_0_, bf16[96,2688]{1,0:T(8,128)(2,1)S(1)} %collective-permute-done.5.refs_1_, bf16[4,224,2560]{2,1,0:T(8,128)(2,1)} %bitcast.24, bf16[2,224,2560]{2,1,0:T(8,128)(2,1)} %bitcast.29), custom_call_target="tpu_custom_call" | custom-call | flops 1321205760 | bytes 8847360 | tf_op jit(solution)/shard_map/expert/pallas_call | solution.py:139
  37.8 2.5 collective-permute-done.10.refs_0_
  42.5 3.4 %collective-permute-start.16 = (bf16[96,2688]{1,0:T(8,128)(2,1)S(1)}, bf16[96,2688]{1,0:T(8,128)(2,1)S(1)}, u32[]{:S(2)}, u32[]{:S(2)}) collective-permute-start(bf16[96,2688]{1,0:T(8,128)(2,1)S(1)} %collective-permute-done.15.refs_1_), channel_id=1, source_target_pairs={{0,7},{1,0},{2,1},{3,2},{4,3},{5,4},{6,5},{7,6},{8,15},{9,8},{10,9... | collective-permute-start | bytes 1548296 | tf_op jit(solution)/shard_map/ppermute | solution.py:23
  45.9 7.4 %collective-permute-done.11.refs_0_ = bf16[96,2688]{1,0:T(8,128)(2,1)S(1)} collective-permute-done((bf16[96,2688]{1,0:T(8,128)(2,1)S(1)}, bf16[96,2688]{1,0:T(8,128)(2,1)S(1)}, u32[]{:S(2)}, u32[]{:S(2)}) %collective-permute-start.11) | collective-permute-done | bytes 516128 | tf_op jit(solution)/shard_map/ppermute | solution.py:23
  55.1 8.2 %expert.9 = (bf16[192,2560]{1,0:T(8,128)(2,1)S(1)}, bf16[192,2560]{1,0:T(8,128)(2,1)S(1)}) custom-call(s32[1]{0:T(128)} %bitcast.me_ref, bf16[96,2688]{1,0:T(8,128)(2,1)} %constant_dynamic-update-slice_fusion.refs_0_, bf16[96,2688]{1,0:T(8,128)(2,1)S(1)} %constant_dynamic-update-slice_fusion.2.refs_1_, ...), custom_call_target="tpu_custom_call" | custom-call | flops 2642411520 | bytes 10813440 | tf_op jit(solution)/shard_map/expert/pallas_call | solution.py:139
  63.3 2.7 %collective-permute-start.28 = (bf16[192,2560]{1,0:T(8,128)(2,1)S(1)}, bf16[192,2560]{1,0:T(8,128)(2,1)S(1)}, u32[]{:S(2)}, u32[]{:S(2)}) collective-permute-start(bf16[192,2560]{1,0:T(8,128)(2,1)S(1)} %get-tuple-element.225), channel_id=1, source_target_pairs={{0,8},{8,0},{1,9},{9,1},{2,10},{10,2},{3,11},{11,3},{4,12},{12,4},... | collective-permute-start | bytes 2949128 | tf_op jit(solution)/shard_map/ppermute | solution.py:18
  66.0 3.0 %collective-permute-start.17 = (bf16[48,2688]{1,0:T(8,128)(2,1)S(1)}, bf16[48,2688]{1,0:T(8,128)(2,1)S(1)}, u32[]{:S(2)}, u32[]{:S(2)}) collective-permute-start(bf16[48,2688]{1,0:T(8,128)(2,1)S(1)} %slice.155), channel_id=1, source_target_pairs={{0,7},{1,0},{2,1},{3,2},{4,3},{5,4},{6,5},{7,6},{8,15},{9,8},{10,9... | collective-permute-start | bytes 774152 | tf_op jit(solution)/shard_map/ppermute | solution.py:23
  69.1 5.5 %collective-permute-done.17 = bf16[48,2688]{1,0:T(8,128)(2,1)S(1)} collective-permute-done((bf16[48,2688]{1,0:T(8,128)(2,1)S(1)}, bf16[48,2688]{1,0:T(8,128)(2,1)S(1)}, u32[]{:S(2)}, u32[]{:S(2)}) %collective-permute-start.17) | collective-permute-done | bytes 258080 | tf_op jit(solution)/shard_map/ppermute | solution.py:23
  75.8 8.9 %expert.8 = (bf16[192,2560]{1,0:T(8,128)(2,1)S(1)}, bf16[192,2560]{1,0:T(8,128)(2,1)S(1)}) custom-call(s32[1]{0:T(128)} %bitcast.me_ref, bf16[96,2688]{1,0:T(8,128)(2,1)S(1)} %collective-permute-done.10.refs_0_, bf16[96,2688]{1,0:T(8,128)(2,1)S(1)} %collective-permute-done.15.refs_1_, bf16[192,2688]{1,0:T(8,128)(2,1)S(1)} %collective-permute-done.24.refs_2_, ...), custom_call_target="tpu_custom_call" | custom-call | flops 2642411520 | bytes 10813440 | tf_op jit(solution)/shard_map/expert/pallas_call | solution.py:139
  85.2 6.1 %expert.6 = (bf16[96,2560]{1,0:T(8,128)(2,1)S(1)}, bf16[96,2560]{1,0:T(8,128)(2,1)S(1)}) custom-call(s32[1]{0:T(128)} %bitcast.me_ref, bf16[96,2688]{1,0:T(8,128)(2,1)S(1)} %constant_dynamic-update-slice_fusion.4.refs_0_, bf16[96,2688]{1,0:T(8,128)(2,1)S(1)} %collective-permute-done.18.refs_1_, bf16[4,224,2560]{2,1,0:T(8,128)(2,1)} %bitcast.27, ...), custom_call_target="tpu_custom_call" | custom-call | flops 1321205760 | bytes 8847360 | tf_op jit(solution)/shard_map/expert/pallas_call | solution.py:139
  91.9 8.9 %expert.7 = (bf16[192,2560]{1,0:T(8,128)(2,1)S(1)}, bf16[192,2560]{1,0:T(8,128)(2,1)S(1)}) custom-call(s32[1]{0:T(128)} %bitcast.me_ref, bf16[96,2688]{1,0:T(8,128)(2,1)S(1)} %collective-permute-done.11.refs_0_, bf16[96,2688]{1,0:T(8,128)(2,1)S(1)} %collective-permute-done.16.refs_1_, bf16[192,2688]{1,0:T(8,128)(2,1)S(1)} %collective-permute-done.21.refs_2_, ...), custom_call_target="tpu_custom_call" | custom-call | flops 2642411520 | bytes 10813440 | tf_op jit(solution)/shard_map/expert/pallas_call | solution.py:139
  104.6 5.1 %collective-permute-done.20 = bf16[48,2560]{1,0:T(8,128)(2,1)S(1)} collective-permute-done((bf16[48,2560]{1,0:T(8,128)(2,1)S(1)}, bf16[48,2560]{1,0:T(8,128)(2,1)S(1)}, u32[]{:S(2)}, u32[]{:S(2)}) %collective-permute-start.20) | collective-permute-done | bytes 245792 | tf_op jit(solution)/shard_map/ppermute | solution.py:18
  111.0 9.3 %collective-permute-done.26 = bf16[96,2560]{1,0:T(8,128)(2,1)S(1)} collective-permute-done((bf16[96,2560]{1,0:T(8,128)(2,1)S(1)}, bf16[96,2560]{1,0:T(8,128)(2,1)S(1)}, u32[]{:S(2)}, u32[]{:S(2)}) %collective-permute-start.26) | collective-permute-done | bytes 491552 | tf_op jit(solution)/shard_map/ppermute | solution.py:18
  120.5 10.4 %collective-permute-done.23 = bf16[96,2560]{1,0:T(8,128)(2,1)S(1)} collective-permute-done((bf16[96,2560]{1,0:T(8,128)(2,1)S(1)}, bf16[96,2560]{1,0:T(8,128)(2,1)S(1)}, u32[]{:S(2)}, u32[]{:S(2)}) %collective-permute-start.23) | collective-permute-done | bytes 491552 | tf_op jit(solution)/shard_map/ppermute | solution.py:18
  132.6 29.8 %while.30 = (s32[]{:T(128)}, bf16[48,2560]{1,0:T(8,128)(2,1)S(1)}, bf16[48,2560]{1,0:T(8,128)(2,1)S(1)}, bf16[192,2560]{1,0:T(8,128)(2,1)S(1)}, bf16[192,2560]{1...) while((s32[]{:T(128)}, bf16[48,2560]{1,0:T(8,128)(2,1)S(1)}, ...), condition=%wide.region_2.3_spmd, body=%wide.region_1.2_spmd.sunk | while | flops 983046 | bytes 3440867 | solution.py:54
  132.8 3.4 %collective-permute-start.1 = (bf16[48,2560]{1,0:T(8,128)(2,1)S(1)}, bf16[48,2560]{1,0:T(8,128)(2,1)S(1)}, u32[]{:S(2)}, u32[]{:S(2)}) collective-permute-start(bf16[48,2560]{1,0:T(8,128)(2,1)S(1)} %add_convert_fusion.22), channel_id=1, source_target_pairs={{0,7},{1,0},{2,1},{3,2},{4,3},{5,4},{6,5},{7,6},{8,15},{9,8},{10,9... | collective-permute-start | bytes 737288 | tf_op jit(solution)/shard_map/while/body/eval_jaxpr/ppermute | solution.py:23
  136.2 5.2 %collective-permute-done = bf16[48,2560]{1,0:T(8,128)(2,1)S(1)} collective-permute-done((bf16[48,2560]{1,0:T(8,128)(2,1)S(1)}, bf16[48,2560]{1,0:T(8,128)(2,1)S(1)}, u32[]{:S(2)}, u32[]{:S(2)}) %collective-permute-start) | collective-permute-done | bytes 245792 | tf_op jit(solution)/shard_map/while/body/eval_jaxpr/ppermute | solution.py:23
  144.3 4.3 %collective-permute-done = bf16[48,2560]{1,0:T(8,128)(2,1)S(1)} collective-permute-done((bf16[48,2560]{1,0:T(8,128)(2,1)S(1)}, bf16[48,2560]{1,0:T(8,128)(2,1)S(1)}, u32[]{:S(2)}, u32[]{:S(2)}) %collective-permute-start) | collective-permute-done | bytes 245792 | tf_op jit(solution)/shard_map/while/body/eval_jaxpr/ppermute | solution.py:23
  149.9 1.7 collective-permute-start.1
  151.7 3.4 %collective-permute-done = bf16[48,2560]{1,0:T(8,128)(2,1)S(1)} collective-permute-done((bf16[48,2560]{1,0:T(8,128)(2,1)S(1)}, bf16[48,2560]{1,0:T(8,128)(2,1)S(1)}, u32[]{:S(2)}, u32[]{:S(2)}) %collective-permute-start) | collective-permute-done | bytes 245792 | tf_op jit(solution)/shard_map/while/body/eval_jaxpr/ppermute | solution.py:23
  155.2 2.0 collective-permute-start
  158.2 3.4 %collective-permute-done = bf16[48,2560]{1,0:T(8,128)(2,1)S(1)} collective-permute-done((bf16[48,2560]{1,0:T(8,128)(2,1)S(1)}, bf16[48,2560]{1,0:T(8,128)(2,1)S(1)}, u32[]{:S(2)}, u32[]{:S(2)}) %collective-permute-start) | collective-permute-done | bytes 245792 | tf_op jit(solution)/shard_map/while/body/eval_jaxpr/ppermute | solution.py:23
  166.8 3.6 %collective-permute-done.30.refs_1_ = bf16[48,2560]{1,0:T(8,128)(2,1)S(1)} collective-permute-done((bf16[48,2560]{1,0:T(8,128)(2,1)S(1)}, bf16[48,2560]{1,0:T(8,128)(2,1)S(1)}, u32[]{:S(2)}, u32[]{:S(2)}) %collective-permute-start.30) | collective-permute-done | bytes 245792 | tf_op jit(solution)/shard_map/ppermute | solution.py:23
  170.6 2.4 collective-permute-start.33
  173.1 5.8 %collective-permute-done.32.refs_3_ = bf16[48,2560]{1,0:T(8,128)(2,1)S(1)} collective-permute-done((bf16[48,2560]{1,0:T(8,128)(2,1)S(1)}, bf16[48,2560]{1,0:T(8,128)(2,1)S(1)}, u32[]{:S(2)}, u32[]{:S(2)}) %collective-permute-start.32) | collective-permute-done | bytes 245792 | tf_op jit(solution)/shard_map/ppermute | solution.py:23
  178.9 2.1 copy-done
  181.0 4.3 %project.2 = (bf16[240,256]{1,0:T(8,128)(2,1)S(1)}, bf16[240,512]{1,0:T(8,128)(2,1)S(1)}) custom-call(bf16[48,2560]{1,0:T(8,128)(2,1)S(1)} %fusion.10.refs_0_, bf16[48,2560]{1,0:T(8,128)(2,1)S(1)} %collective-permute-done.30.refs_1_, bf16[48,2560]{1,0:T(8,128)(2,1)S(1)} %collective-permute-done.31.refs_2_, ...), custom_call_target="tpu_custom_call" | custom-call | flops 943718400 | bytes 5160960 | tf_op jit(solution)/shard_map/project/pallas_call | solution.py:212
  186.3 3.0 %collective-permute-start.35 = (bf16[48,2560]{1,0:T(8,128)(2,1)S(1)}, bf16[48,2560]{1,0:T(8,128)(2,1)S(1)}, u32[]{:S(2)}, u32[]{:S(2)}) collective-permute-start(bf16[48,2560]{1,0:T(8,128)(2,1)S(1)} %collective-permute-done.33.refs_4_), channel_id=1, source_target_pairs={{0,7},{1,0},{2,1},{3,2},{4,3},{5,4},{6,5},{7,6},{8,15},{9,8},{10,9... | collective-permute-start | bytes 737288 | tf_op jit(solution)/shard_map/ppermute | solution.py:23
  190.5 12.9 %all_gather.3.refs_2_ = bf16[960,512]{1,0:T(8,128)(2,1)S(1)} all-gather(bf16[480,512]{1,0:T(8,128)(2,1)S(1)} %pad_maximum_fusion.8), channel_id=1, replica_groups=mesh['set'=8,'exp_0'=2,'exp_1'=2,'seq'=8] {'exp_1'}, dimensions={0}, use_global_device_ids=true | all-gather | bytes 1474560 | tf_op jit(solution)/shard_map/all_gather | solution.py:398
  203.4 3.3 %project.3 = (bf16[144,256]{1,0:T(8,128)(2,1)S(1)}, bf16[144,512]{1,0:T(8,128)(2,1)S(1)}) custom-call(bf16[48,2560]{1,0:T(8,128)(2,1)S(1)} %collective-permute-done.34.refs_0_, bf16[48,2560]{1,0:T(8,128)(2,1)S(1)} %collective-permute-done.35.refs_1_, bf16[48,2560]{1,0:T(8,128)(2,1)S(1)} %collective-permute-done.36.refs_2_, ...), custom_call_target="tpu_custom_call" | custom-call | flops 566231040 | bytes 4669440 | tf_op jit(solution)/shard_map/project/pallas_call | solution.py:212
  207.7 3.1 %collective-permute-done.38 = bf16[144,512]{1,0:T(8,128)(2,1)S(1)} collective-permute-done((bf16[144,512]{1,0:T(8,128)(2,1)S(1)}, bf16[144,512]{1,0:T(8,128)(2,1)S(1)}, u32[]{:S(2)}, u32[]{:S(2)}) %collective-permute-start.38) | collective-permute-done | bytes 147488 | tf_op jit(solution)/shard_map/ppermute | solution.py:18
  210.8 4.9 %collective-permute-start.39 = (bf16[288,512]{1,0:T(8,128)(2,1)S(1)}, bf16[288,512]{1,0:T(8,128)(2,1)S(1)}, u32[]{:S(2)}, u32[]{:S(2)}) collective-permute-start(bf16[288,512]{1,0:T(8,128)(2,1)S(1)} %constant_dynamic-update-slice_fusion.6.refs_3_), channel_id=1, source_target_pairs={{0,8},{8,0},{1,9},{9,1},{2,10},{10,2},{3,11},{11,3},{4,12},{12,4},... | collective-permute-start | bytes 884744 | tf_op jit(solution)/shard_map/ppermute | solution.py:18
  216.9 4.2 %attend.1 = (bf16[48,2560]{1,0:T(8,128)(2,1)S(1)}, bf16[48,2560]{1,0:T(8,128)(2,1)S(1)}, bf16[48,2560]{1,0:T(8,128)(2,1)S(1)}, bf16[48,2560]{1,0:T(8,128)(2,1)S(...) custom-call(bf16[240,256]{1,0:T(8,128)(2,1)S(1)} %get-tuple-element., ...), custom_call_target="tpu_custom_call" | custom-call | flops 1107296256 | bytes 4849664 | tf_op jit(solution)/shard_map/attend/pallas_call | solution.py:300
  222.1 29.5 %while.31 = (s32[]{:T(128)}, bf16[48,2560]{1,0:T(8,128)(2,1)S(1)}, bf16[48,2560]{1,0:T(8,128)(2,1)S(1)}, bf16[192,2560]{1,0:T(8,128)(2,1)S(1)}, bf16[192,2560]{1...) while((s32[]{:T(128)}, bf16[48,2560]{1,0:T(8,128)(2,1)S(1)}, ...), condition=%wide.region_5.6_spmd, body=%wide.region_4.5_spmd.sunk | while | flops 983046 | bytes 3440867 | solution.py:54
  222.4 2.7 %collective-permute-start.3 = (bf16[48,2560]{1,0:T(8,128)(2,1)S(1)}, bf16[48,2560]{1,0:T(8,128)(2,1)S(1)}, u32[]{:S(2)}, u32[]{:S(2)}) collective-permute-start(bf16[48,2560]{1,0:T(8,128)(2,1)S(1)} %add_convert_fusion.24), channel_id=1, source_target_pairs={{0,7},{1,0},{2,1},{3,2},{4,3},{5,4},{6,5},{7,6},{8,15},{9,8},{10,9... | collective-permute-start | bytes 737288 | tf_op jit(solution)/shard_map/while/body/eval_jaxpr/ppermute | solution.py:23
  225.1 5.6 %collective-permute-done.2 = bf16[48,2560]{1,0:T(8,128)(2,1)S(1)} collective-permute-done((bf16[48,2560]{1,0:T(8,128)(2,1)S(1)}, bf16[48,2560]{1,0:T(8,128)(2,1)S(1)}, u32[]{:S(2)}, u32[]{:S(2)}) %collective-permute-start.2) | collective-permute-done | bytes 245792 | tf_op jit(solution)/shard_map/while/body/eval_jaxpr/ppermute | solution.py:23
  230.9 2.7 %collective-permute-start.3 = (bf16[48,2560]{1,0:T(8,128)(2,1)S(1)}, bf16[48,2560]{1,0:T(8,128)(2,1)S(1)}, u32[]{:S(2)}, u32[]{:S(2)}) collective-permute-start(bf16[48,2560]{1,0:T(8,128)(2,1)S(1)} %add_convert_fusion.24), channel_id=1, source_target_pairs={{0,7},{1,0},{2,1},{3,2},{4,3},{5,4},{6,5},{7,6},{8,15},{9,8},{10,9... | collective-permute-start | bytes 737288 | tf_op jit(solution)/shard_map/while/body/eval_jaxpr/ppermute | solution.py:23
  233.6 4.7 %collective-permute-done.2 = bf16[48,2560]{1,0:T(8,128)(2,1)S(1)} collective-permute-done((bf16[48,2560]{1,0:T(8,128)(2,1)S(1)}, bf16[48,2560]{1,0:T(8,128)(2,1)S(1)}, u32[]{:S(2)}, u32[]{:S(2)}) %collective-permute-start.2) | collective-permute-done | bytes 245792 | tf_op jit(solution)/shard_map/while/body/eval_jaxpr/ppermute | solution.py:23
  238.6 2.7 %collective-permute-start.3 = (bf16[48,2560]{1,0:T(8,128)(2,1)S(1)}, bf16[48,2560]{1,0:T(8,128)(2,1)S(1)}, u32[]{:S(2)}, u32[]{:S(2)}) collective-permute-start(bf16[48,2560]{1,0:T(8,128)(2,1)S(1)} %add_convert_fusion.24), channel_id=1, source_target_pairs={{0,7},{1,0},{2,1},{3,2},{4,3},{5,4},{6,5},{7,6},{8,15},{9,8},{10,9... | collective-permute-start | bytes 737288 | tf_op jit(solution)/shard_map/while/body/eval_jaxpr/ppermute | solution.py:23
  241.3 3.9 %collective-permute-done.2 = bf16[48,2560]{1,0:T(8,128)(2,1)S(1)} collective-permute-done((bf16[48,2560]{1,0:T(8,128)(2,1)S(1)}, bf16[48,2560]{1,0:T(8,128)(2,1)S(1)}, u32[]{:S(2)}, u32[]{:S(2)}) %collective-permute-start.2) | collective-permute-done | bytes 245792 | tf_op jit(solution)/shard_map/while/body/eval_jaxpr/ppermute | solution.py:23
  245.5 2.6 %collective-permute-start.3 = (bf16[48,2560]{1,0:T(8,128)(2,1)S(1)}, bf16[48,2560]{1,0:T(8,128)(2,1)S(1)}, u32[]{:S(2)}, u32[]{:S(2)}) collective-permute-start(bf16[48,2560]{1,0:T(8,128)(2,1)S(1)} %add_convert_fusion.24), channel_id=1, source_target_pairs={{0,7},{1,0},{2,1},{3,2},{4,3},{5,4},{6,5},{7,6},{8,15},{9,8},{10,9... | collective-permute-start | bytes 737288 | tf_op jit(solution)/shard_map/while/body/eval_jaxpr/ppermute | solution.py:23
  248.2 3.4 %collective-permute-done.2 = bf16[48,2560]{1,0:T(8,128)(2,1)S(1)} collective-permute-done((bf16[48,2560]{1,0:T(8,128)(2,1)S(1)}, bf16[48,2560]{1,0:T(8,128)(2,1)S(1)}, u32[]{:S(2)}, u32[]{:S(2)}) %collective-permute-start.2) | collective-permute-done | bytes 245792 | tf_op jit(solution)/shard_map/while/body/eval_jaxpr/ppermute | solution.py:23
  (163 shorter events, 41.7 us)
Async XLA Ops:
  3.7 7.8 %collective-permute-start.4 = (bf16[48,2688]{1,0:T(8,128)(2,1)S(1)}, bf16[48,2688]{1,0:T(8,128)(2,1)S(1)}, u32[]{:S(2)}, u32[]{:S(2)}) collective-permute-start(bf16[48,2688]{1,0:T(8,128)(2,1)S(1)} %pad_maximum_fusion.9), channel_id=1, source_target_pairs={{0,16},{16,0},{1,17},{17,1},{2,18},{18,2},{3,19},{19,3},{4,20},{20... | collective-permute-start | bytes 774152 | tf_op jit(solution)/shard_map/ppermute | solution.py:18
  5.9 13.0 %collective-permute-start.8 = (bf16[48,2688]{1,0:T(8,128)(2,1)S(1)}, bf16[48,2688]{1,0:T(8,128)(2,1)S(1)}, u32[]{:S(2)}, u32[]{:S(2)}) collective-permute-start(bf16[48,2688]{1,0:T(8,128)(2,1)S(1)} %pad_maximum_fusion.9), channel_id=1, source_target_pairs={{0,1},{1,2},{2,3},{3,4},{4,5},{5,6},{6,7},{7,0},{8,9},{9,10},{10,1... | collective-permute-start | bytes 774152 | tf_op jit(solution)/shard_map/ppermute | solution.py:23
  7.6 18.7 %collective-permute-start.13 = (bf16[48,2688]{1,0:T(8,128)(2,1)S(1)}, bf16[48,2688]{1,0:T(8,128)(2,1)S(1)}, u32[]{:S(2)}, u32[]{:S(2)}) collective-permute-start(bf16[48,2688]{1,0:T(8,128)(2,1)S(1)} %pad_maximum_fusion.9), channel_id=1, source_target_pairs={{0,7},{1,0},{2,1},{3,2},{4,3},{5,4},{6,5},{7,6},{8,15},{9,8},{10,9... | collective-permute-start | bytes 774152 | tf_op jit(solution)/shard_map/ppermute | solution.py:23
  11.5 18.8 %collective-permute-start.5 = (bf16[96,2688]{1,0:T(8,128)(2,1)S(1)}, bf16[96,2688]{1,0:T(8,128)(2,1)S(1)}, u32[]{:S(2)}, u32[]{:S(2)}) collective-permute-start(bf16[96,2688]{1,0:T(8,128)(2,1)S(1)} %pad_maximum_fusion.7.refs_0_), channel_id=1, source_target_pairs={{0,8},{8,0},{1,9},{9,1},{2,10},{10,2},{3,11},{11,3},{4,12},{12,4},... | collective-permute-start | bytes 1548296 | tf_op jit(solution)/shard_map/ppermute | solution.py:18
  13.5 12.0 %collective-permute-start.9 = (bf16[48,2688]{1,0:T(8,128)(2,1)S(1)}, bf16[48,2688]{1,0:T(8,128)(2,1)S(1)}, u32[]{:S(2)}, u32[]{:S(2)}) collective-permute-start(bf16[48,2688]{1,0:T(8,128)(2,1)S(1)} %collective-permute-done.4), channel_id=1, source_target_pairs={{0,1},{1,2},{2,3},{3,4},{4,5},{5,6},{6,7},{7,0},{8,9},{9,10},{10,1... | collective-permute-start | bytes 774152 | tf_op jit(solution)/shard_map/ppermute | solution.py:23
  15.0 11.3 %collective-permute-start.14 = (bf16[48,2688]{1,0:T(8,128)(2,1)S(1)}, bf16[48,2688]{1,0:T(8,128)(2,1)S(1)}, u32[]{:S(2)}, u32[]{:S(2)}) collective-permute-start(bf16[48,2688]{1,0:T(8,128)(2,1)S(1)} %collective-permute-done.4), channel_id=1, source_target_pairs={{0,7},{1,0},{2,1},{3,2},{4,3},{5,4},{6,5},{7,6},{8,15},{9,8},{10,9... | collective-permute-start | bytes 774152 | tf_op jit(solution)/shard_map/ppermute | solution.py:23
  26.2 14.1 %collective-permute-start.10 = (bf16[96,2688]{1,0:T(8,128)(2,1)}, bf16[96,2688]{1,0:T(8,128)(2,1)S(1)}, u32[]{:S(2)}, u32[]{:S(2)}) collective-permute-start(bf16[96,2688]{1,0:T(8,128)(2,1)} %constant_dynamic-update-slice_fusion.refs_0_), channel_id=1, source_target_pairs={{0,1},{1,2},{2,3},{3,4},{4,5},{5,6},{6,7},{7,0},{8,9},{9,10},{10,1... | collective-permute-start | bytes 1548296 | tf_op jit(solution)/shard_map/ppermute | solution.py:23
  27.7 14.4 %collective-permute-start.15 = (bf16[96,2688]{1,0:T(8,128)(2,1)S(1)}, bf16[96,2688]{1,0:T(8,128)(2,1)S(1)}, u32[]{:S(2)}, u32[]{:S(2)}) collective-permute-start(bf16[96,2688]{1,0:T(8,128)(2,1)S(1)} %constant_dynamic-update-slice_fusion.2.refs_1_), channel_id=1, source_target_pairs={{0,7},{1,0},{2,1},{3,2},{4,3},{5,4},{6,5},{7,6},{8,15},{9,8},{10,9... | collective-permute-start | bytes 1548296 | tf_op jit(solution)/shard_map/ppermute | solution.py:23
  36.5 16.9 %collective-permute-start.6 = (bf16[96,2560]{1,0:T(8,128)(2,1)S(1)}, bf16[96,2560]{1,0:T(8,128)(2,1)S(1)}, u32[]{:S(2)}, u32[]{:S(2)}) collective-permute-start(bf16[96,2560]{1,0:T(8,128)(2,1)S(1)} %get-tuple-element.217), channel_id=1, source_target_pairs={{0,8},{8,0},{1,9},{9,1},{2,10},{10,2},{3,11},{11,3},{4,12},{12,4},... | collective-permute-start | bytes 1474568 | tf_op jit(solution)/shard_map/ppermute | solution.py:18
  40.3 13.0 %collective-permute-start.11 = (bf16[96,2688]{1,0:T(8,128)(2,1)S(1)}, bf16[96,2688]{1,0:T(8,128)(2,1)S(1)}, u32[]{:S(2)}, u32[]{:S(2)}) collective-permute-start(bf16[96,2688]{1,0:T(8,128)(2,1)S(1)} %collective-permute-done.10.refs_0_), channel_id=1, source_target_pairs={{0,1},{1,2},{2,3},{3,4},{4,5},{5,6},{6,7},{7,0},{8,9},{9,10},{10,1... | collective-permute-start | bytes 1548296 | tf_op jit(solution)/shard_map/ppermute | solution.py:23
  40.4 14.7 %collective-permute-start.27 = (bf16[192,2688]{1,0:T(8,128)(2,1)S(1)}, bf16[192,2688]{1,0:T(8,128)(2,1)S(1)}, u32[]{:S(2)}, u32[]{:S(2)}) collective-permute-start(bf16[192,2688]{1,0:T(8,128)(2,1)S(1)} %pad_maximum_fusion.4), channel_id=1, source_target_pairs={{0,8},{8,0},{1,9},{9,1},{2,10},{10,2},{3,11},{11,3},{4,12},{12,4},... | collective-permute-start | bytes 3096584 | tf_op jit(solution)/shard_map/ppermute | solution.py:18
  42.1 33.7 %collective-permute-start.24 = (bf16[192,2688]{1,0:T(8,128)(2,1)S(1)}, bf16[192,2688]{1,0:T(8,128)(2,1)S(1)}, u32[]{:S(2)}, u32[]{:S(2)}) collective-permute-start(bf16[192,2688]{1,0:T(8,128)(2,1)S(1)} %pad_maximum_fusion.3), channel_id=1, source_target_pairs={{0,8},{8,0},{1,9},{9,1},{2,10},{10,2},{3,11},{11,3},{4,12},{12,4},... | collective-permute-start | bytes 3096584 | tf_op jit(solution)/shard_map/ppermute | solution.py:18
  42.5 23.6 %collective-permute-start.16 = (bf16[96,2688]{1,0:T(8,128)(2,1)S(1)}, bf16[96,2688]{1,0:T(8,128)(2,1)S(1)}, u32[]{:S(2)}, u32[]{:S(2)}) collective-permute-start(bf16[96,2688]{1,0:T(8,128)(2,1)S(1)} %collective-permute-done.15.refs_1_), channel_id=1, source_target_pairs={{0,7},{1,0},{2,1},{3,2},{4,3},{5,4},{6,5},{7,6},{8,15},{9,8},{10,9... | collective-permute-start | bytes 1548296 | tf_op jit(solution)/shard_map/ppermute | solution.py:23
  53.3 15.7 %collective-permute-start.12 = (bf16[48,2688]{1,0:T(8,128)(2,1)S(1)}, bf16[48,2688]{1,0:T(8,128)(2,1)S(1)}, u32[]{:S(2)}, u32[]{:S(2)}) collective-permute-start(bf16[48,2688]{1,0:T(8,128)(2,1)S(1)} %slice.154), channel_id=1, source_target_pairs={{0,1},{1,2},{2,3},{3,4},{4,5},{5,6},{6,7},{7,0},{8,9},{9,10},{10,1... | collective-permute-start | bytes 774152 | tf_op jit(solution)/shard_map/ppermute | solution.py:23
  53.5 78.3 %collective-permute-start.7 = (bf16[48,2560]{1,0:T(8,128)(2,1)S(1)}, bf16[48,2560]{1,0:T(8,128)(2,1)S(1)}, u32[]{:S(2)}, u32[]{:S(2)}) collective-permute-start(bf16[48,2560]{1,0:T(8,128)(2,1)S(1)} %add_convert_fusion.15), channel_id=1, source_target_pairs={{0,16},{16,0},{1,17},{17,1},{2,18},{18,2},{3,19},{19,3},{4,20},{20... | collective-permute-start | bytes 737288 | tf_op jit(solution)/shard_map/ppermute | solution.py:18
  63.3 28.2 %collective-permute-start.28 = (bf16[192,2560]{1,0:T(8,128)(2,1)S(1)}, bf16[192,2560]{1,0:T(8,128)(2,1)S(1)}, u32[]{:S(2)}, u32[]{:S(2)}) collective-permute-start(bf16[192,2560]{1,0:T(8,128)(2,1)S(1)} %get-tuple-element.225), channel_id=1, source_target_pairs={{0,8},{8,0},{1,9},{9,1},{2,10},{10,2},{3,11},{11,3},{4,12},{12,4},... | collective-permute-start | bytes 2949128 | tf_op jit(solution)/shard_map/ppermute | solution.py:18
  66.0 8.6 %collective-permute-start.17 = (bf16[48,2688]{1,0:T(8,128)(2,1)S(1)}, bf16[48,2688]{1,0:T(8,128)(2,1)S(1)}, u32[]{:S(2)}, u32[]{:S(2)}) collective-permute-start(bf16[48,2688]{1,0:T(8,128)(2,1)S(1)} %slice.155), channel_id=1, source_target_pairs={{0,7},{1,0},{2,1},{3,2},{4,3},{5,4},{6,5},{7,6},{8,15},{9,8},{10,9... | collective-permute-start | bytes 774152 | tf_op jit(solution)/shard_map/ppermute | solution.py:23
  74.6 10.6 %collective-permute-start.18 = (bf16[96,2688]{1,0:T(8,128)(2,1)S(1)}, bf16[96,2688]{1,0:T(8,128)(2,1)S(1)}, u32[]{:S(2)}, u32[]{:S(2)}) collective-permute-start(bf16[96,2688]{1,0:T(8,128)(2,1)S(1)} %constant_dynamic-update-slice_fusion.4.refs_0_), channel_id=1, source_target_pairs={{0,8},{8,0},{1,9},{9,1},{2,10},{10,2},{3,11},{11,3},{4,12},{12,4},... | collective-permute-start | bytes 1548296 | tf_op jit(solution)/shard_map/ppermute | solution.py:18
  75.7 16.2 %collective-permute-start.21 = (bf16[192,2688]{1,0:T(8,128)(2,1)S(1)}, bf16[192,2688]{1,0:T(8,128)(2,1)S(1)}, u32[]{:S(2)}, u32[]{:S(2)}) collective-permute-start(bf16[192,2688]{1,0:T(8,128)(2,1)S(1)} %pad_maximum_fusion.2), channel_id=1, source_target_pairs={{0,8},{8,0},{1,9},{9,1},{2,10},{10,2},{3,11},{11,3},{4,12},{12,4},... | collective-permute-start | bytes 3096584 | tf_op jit(solution)/shard_map/ppermute | solution.py:18
  84.7 19.5 %collective-permute-start.25 = (bf16[192,2560]{1,0:T(8,128)(2,1)S(1)}, bf16[192,2560]{1,0:T(8,128)(2,1)S(1)}, u32[]{:S(2)}, u32[]{:S(2)}) collective-permute-start(bf16[192,2560]{1,0:T(8,128)(2,1)S(1)} %get-tuple-element.223), channel_id=1, source_target_pairs={{0,8},{8,0},{1,9},{9,1},{2,10},{10,2},{3,11},{11,3},{4,12},{12,4},... | collective-permute-start | bytes 2949128 | tf_op jit(solution)/shard_map/ppermute | solution.py:18
  91.3 10.3 %collective-permute-start.19 = (bf16[96,2560]{1,0:T(8,128)(2,1)S(1)}, bf16[96,2560]{1,0:T(8,128)(2,1)S(1)}, u32[]{:S(2)}, u32[]{:S(2)}) collective-permute-start(bf16[96,2560]{1,0:T(8,128)(2,1)S(1)} %get-tuple-element.219), channel_id=1, source_target_pairs={{0,8},{8,0},{1,9},{9,1},{2,10},{10,2},{3,11},{11,3},{4,12},{12,4},... | collective-permute-start | bytes 1474568 | tf_op jit(solution)/shard_map/ppermute | solution.py:18
  91.6 12.4 %collective-permute-start.29 = (bf16[96,2560]{1,0:T(8,128)(2,1)S(1)}, bf16[96,2560]{1,0:T(8,128)(2,1)S(1)}, u32[]{:S(2)}, u32[]{:S(2)}) collective-permute-start(bf16[96,2560]{1,0:T(8,128)(2,1)S(1)} %add_convert_fusion.4), channel_id=1, source_target_pairs={{0,16},{16,0},{1,17},{17,1},{2,18},{18,2},{3,19},{19,3},{4,20},{20... | collective-permute-start | bytes 1474568 | tf_op jit(solution)/shard_map/ppermute | solution.py:18
  100.8 9.1 %collective-permute-start.22 = (bf16[192,2560]{1,0:T(8,128)(2,1)S(1)}, bf16[192,2560]{1,0:T(8,128)(2,1)S(1)}, u32[]{:S(2)}, u32[]{:S(2)}) collective-permute-start(bf16[192,2560]{1,0:T(8,128)(2,1)S(1)} %get-tuple-element.221), channel_id=1, source_target_pairs={{0,8},{8,0},{1,9},{9,1},{2,10},{10,2},{3,11},{11,3},{4,12},{12,4},... | collective-permute-start | bytes 2949128 | tf_op jit(solution)/shard_map/ppermute | solution.py:18
  101.7 8.1 %collective-permute-start.20 = (bf16[48,2560]{1,0:T(8,128)(2,1)S(1)}, bf16[48,2560]{1,0:T(8,128)(2,1)S(1)}, u32[]{:S(2)}, u32[]{:S(2)}) collective-permute-start(bf16[48,2560]{1,0:T(8,128)(2,1)S(1)} %add_convert_fusion.14), channel_id=1, source_target_pairs={{0,16},{16,0},{1,17},{17,1},{2,18},{18,2},{3,19},{19,3},{4,20},{20... | collective-permute-start | bytes 737288 | tf_op jit(solution)/shard_map/ppermute | solution.py:18
  104.3 15.9 %collective-permute-start.26 = (bf16[96,2560]{1,0:T(8,128)(2,1)S(1)}, bf16[96,2560]{1,0:T(8,128)(2,1)S(1)}, u32[]{:S(2)}, u32[]{:S(2)}) collective-permute-start(bf16[96,2560]{1,0:T(8,128)(2,1)S(1)} %add_convert_fusion.5), channel_id=1, source_target_pairs={{0,16},{16,0},{1,17},{17,1},{2,18},{18,2},{3,19},{19,3},{4,20},{20... | collective-permute-start | bytes 1474568 | tf_op jit(solution)/shard_map/ppermute | solution.py:18
  110.0 20.8 %collective-permute-start.23 = (bf16[96,2560]{1,0:T(8,128)(2,1)S(1)}, bf16[96,2560]{1,0:T(8,128)(2,1)S(1)}, u32[]{:S(2)}, u32[]{:S(2)}) collective-permute-start(bf16[96,2560]{1,0:T(8,128)(2,1)S(1)} %add_convert_fusion.6), channel_id=1, source_target_pairs={{0,16},{16,0},{1,17},{17,1},{2,18},{18,2},{3,19},{19,3},{4,20},{20... | collective-permute-start | bytes 1474568 | tf_op jit(solution)/shard_map/ppermute | solution.py:18
  132.6 8.8 %collective-permute-start = (bf16[48,2560]{1,0:T(8,128)(2,1)S(1)}, bf16[48,2560]{1,0:T(8,128)(2,1)S(1)}, u32[]{:S(2)}, u32[]{:S(2)}) collective-permute-start(bf16[48,2560]{1,0:T(8,128)(2,1)S(1)} %add_convert_fusion.21), channel_id=1, source_target_pairs={{0,1},{1,2},{2,3},{3,4},{4,5},{5,6},{6,7},{7,0},{8,9},{9,10},{10,1... | collective-permute-start | bytes 737288 | tf_op jit(solution)/shard_map/while/body/eval_jaxpr/ppermute | solution.py:23
  132.8 8.6 %collective-permute-start.1 = (bf16[48,2560]{1,0:T(8,128)(2,1)S(1)}, bf16[48,2560]{1,0:T(8,128)(2,1)S(1)}, u32[]{:S(2)}, u32[]{:S(2)}) collective-permute-start(bf16[48,2560]{1,0:T(8,128)(2,1)S(1)} %add_convert_fusion.22), channel_id=1, source_target_pairs={{0,7},{1,0},{2,1},{3,2},{4,3},{5,4},{6,5},{7,6},{8,15},{9,8},{10,9... | collective-permute-start | bytes 737288 | tf_op jit(solution)/shard_map/while/body/eval_jaxpr/ppermute | solution.py:23
  141.5 7.2 %collective-permute-start = (bf16[48,2560]{1,0:T(8,128)(2,1)S(1)}, bf16[48,2560]{1,0:T(8,128)(2,1)S(1)}, u32[]{:S(2)}, u32[]{:S(2)}) collective-permute-start(bf16[48,2560]{1,0:T(8,128)(2,1)S(1)} %add_convert_fusion.21), channel_id=1, source_target_pairs={{0,1},{1,2},{2,3},{3,4},{4,5},{5,6},{6,7},{7,0},{8,9},{9,10},{10,1... | collective-permute-start | bytes 737288 | tf_op jit(solution)/shard_map/while/body/eval_jaxpr/ppermute | solution.py:23
  143.1 5.6 %collective-permute-start.1 = (bf16[48,2560]{1,0:T(8,128)(2,1)S(1)}, bf16[48,2560]{1,0:T(8,128)(2,1)S(1)}, u32[]{:S(2)}, u32[]{:S(2)}) collective-permute-start(bf16[48,2560]{1,0:T(8,128)(2,1)S(1)} %add_convert_fusion.22), channel_id=1, source_target_pairs={{0,7},{1,0},{2,1},{3,2},{4,3},{5,4},{6,5},{7,6},{8,15},{9,8},{10,9... | collective-permute-start | bytes 737288 | tf_op jit(solution)/shard_map/while/body/eval_jaxpr/ppermute | solution.py:23
  148.8 6.3 %collective-permute-start = (bf16[48,2560]{1,0:T(8,128)(2,1)S(1)}, bf16[48,2560]{1,0:T(8,128)(2,1)S(1)}, u32[]{:S(2)}, u32[]{:S(2)}) collective-permute-start(bf16[48,2560]{1,0:T(8,128)(2,1)S(1)} %add_convert_fusion.21), channel_id=1, source_target_pairs={{0,1},{1,2},{2,3},{3,4},{4,5},{5,6},{6,7},{7,0},{8,9},{9,10},{10,1... | collective-permute-start | bytes 737288 | tf_op jit(solution)/shard_map/while/body/eval_jaxpr/ppermute | solution.py:23
  149.9 5.2 %collective-permute-start.1 = (bf16[48,2560]{1,0:T(8,128)(2,1)S(1)}, bf16[48,2560]{1,0:T(8,128)(2,1)S(1)}, u32[]{:S(2)}, u32[]{:S(2)}) collective-permute-start(bf16[48,2560]{1,0:T(8,128)(2,1)S(1)} %add_convert_fusion.22), channel_id=1, source_target_pairs={{0,7},{1,0},{2,1},{3,2},{4,3},{5,4},{6,5},{7,6},{8,15},{9,8},{10,9... | collective-permute-start | bytes 737288 | tf_op jit(solution)/shard_map/while/body/eval_jaxpr/ppermute | solution.py:23
  155.2 6.5 %collective-permute-start = (bf16[48,2560]{1,0:T(8,128)(2,1)S(1)}, bf16[48,2560]{1,0:T(8,128)(2,1)S(1)}, u32[]{:S(2)}, u32[]{:S(2)}) collective-permute-start(bf16[48,2560]{1,0:T(8,128)(2,1)S(1)} %add_convert_fusion.21), channel_id=1, source_target_pairs={{0,1},{1,2},{2,3},{3,4},{4,5},{5,6},{6,7},{7,0},{8,9},{9,10},{10,1... | collective-permute-start | bytes 737288 | tf_op jit(solution)/shard_map/while/body/eval_jaxpr/ppermute | solution.py:23
  164.1 6.3 %collective-permute-start.30 = (bf16[48,2560]{1,0:T(8,128)(2,1)S(1)}, bf16[48,2560]{1,0:T(8,128)(2,1)S(1)}, u32[]{:S(2)}, u32[]{:S(2)}) collective-permute-start(bf16[48,2560]{1,0:T(8,128)(2,1)S(1)} %fusion.10.refs_0_), channel_id=1, source_target_pairs={{0,1},{1,2},{2,3},{3,4},{4,5},{5,6},{6,7},{7,0},{8,9},{9,10},{10,1... | collective-permute-start | bytes 737288 | tf_op jit(solution)/shard_map/ppermute | solution.py:23
  170.4 8.5 %collective-permute-start.32 = (bf16[48,2560]{1,0:T(8,128)(2,1)S(1)}, bf16[48,2560]{1,0:T(8,128)(2,1)S(1)}, u32[]{:S(2)}, u32[]{:S(2)}) collective-permute-start(bf16[48,2560]{1,0:T(8,128)(2,1)S(1)} %collective-permute-done.30.refs_1_), channel_id=1, source_target_pairs={{0,1},{1,2},{2,3},{3,4},{4,5},{5,6},{6,7},{7,0},{8,9},{9,10},{10,1... | collective-permute-start | bytes 737288 | tf_op jit(solution)/shard_map/ppermute | solution.py:23
  170.6 8.2 %collective-permute-start.33 = (bf16[48,2560]{1,0:T(8,128)(2,1)S(1)}, bf16[48,2560]{1,0:T(8,128)(2,1)S(1)}, u32[]{:S(2)}, u32[]{:S(2)}) collective-permute-start(bf16[48,2560]{1,0:T(8,128)(2,1)S(1)} %collective-permute-done.31.refs_2_), channel_id=1, source_target_pairs={{0,7},{1,0},{2,1},{3,2},{4,3},{5,4},{6,5},{7,6},{8,15},{9,8},{10,9... | collective-permute-start | bytes 737288 | tf_op jit(solution)/shard_map/ppermute | solution.py:23
  178.9 10.5 %collective-permute-start.34 = (bf16[48,2560]{1,0:T(8,128)(2,1)S(1)}, bf16[48,2560]{1,0:T(8,128)(2,1)S(1)}, u32[]{:S(2)}, u32[]{:S(2)}) collective-permute-start(bf16[48,2560]{1,0:T(8,128)(2,1)S(1)} %collective-permute-done.32.refs_3_), channel_id=1, source_target_pairs={{0,1},{1,2},{2,3},{3,4},{4,5},{5,6},{6,7},{7,0},{8,9},{9,10},{10,1... | collective-permute-start | bytes 737288 | tf_op jit(solution)/shard_map/ppermute | solution.py:23
  186.3 17.1 %collective-permute-start.35 = (bf16[48,2560]{1,0:T(8,128)(2,1)S(1)}, bf16[48,2560]{1,0:T(8,128)(2,1)S(1)}, u32[]{:S(2)}, u32[]{:S(2)}) collective-permute-start(bf16[48,2560]{1,0:T(8,128)(2,1)S(1)} %collective-permute-done.33.refs_4_), channel_id=1, source_target_pairs={{0,7},{1,0},{2,1},{3,2},{4,3},{5,4},{6,5},{7,6},{8,15},{9,8},{10,9... | collective-permute-start | bytes 737288 | tf_op jit(solution)/shard_map/ppermute | solution.py:23
  189.3 14.1 %collective-permute-start.36 = (bf16[48,2560]{1,0:T(8,128)(2,1)S(1)}, bf16[48,2560]{1,0:T(8,128)(2,1)S(1)}, u32[]{:S(2)}, u32[]{:S(2)}) collective-permute-start(bf16[48,2560]{1,0:T(8,128)(2,1)S(1)} %collective-permute-done.34.refs_0_), channel_id=1, source_target_pairs={{0,1},{1,2},{2,3},{3,4},{4,5},{5,6},{6,7},{7,0},{8,9},{9,10},{10,1... | collective-permute-start | bytes 737288 | tf_op jit(solution)/shard_map/ppermute | solution.py:23
  210.8 6.1 %collective-permute-start.39 = (bf16[288,512]{1,0:T(8,128)(2,1)S(1)}, bf16[288,512]{1,0:T(8,128)(2,1)S(1)}, u32[]{:S(2)}, u32[]{:S(2)}) collective-permute-start(bf16[288,512]{1,0:T(8,128)(2,1)S(1)} %constant_dynamic-update-slice_fusion.6.refs_3_), channel_id=1, source_target_pairs={{0,8},{8,0},{1,9},{9,1},{2,10},{10,2},{3,11},{11,3},{4,12},{12,4},... | collective-permute-start | bytes 884744 | tf_op jit(solution)/shard_map/ppermute | solution.py:18
  222.2 8.5 %collective-permute-start.2 = (bf16[48,2560]{1,0:T(8,128)(2,1)S(1)}, bf16[48,2560]{1,0:T(8,128)(2,1)S(1)}, u32[]{:S(2)}, u32[]{:S(2)}) collective-permute-start(bf16[48,2560]{1,0:T(8,128)(2,1)S(1)} %add_convert_fusion.23), channel_id=1, source_target_pairs={{0,1},{1,2},{2,3},{3,4},{4,5},{5,6},{6,7},{7,0},{8,9},{9,10},{10,1... | collective-permute-start | bytes 737288 | tf_op jit(solution)/shard_map/while/body/eval_jaxpr/ppermute | solution.py:23
  222.4 8.3 %collective-permute-start.3 = (bf16[48,2560]{1,0:T(8,128)(2,1)S(1)}, bf16[48,2560]{1,0:T(8,128)(2,1)S(1)}, u32[]{:S(2)}, u32[]{:S(2)}) collective-permute-start(bf16[48,2560]{1,0:T(8,128)(2,1)S(1)} %add_convert_fusion.24), channel_id=1, source_target_pairs={{0,7},{1,0},{2,1},{3,2},{4,3},{5,4},{6,5},{7,6},{8,15},{9,8},{10,9... | collective-permute-start | bytes 737288 | tf_op jit(solution)/shard_map/while/body/eval_jaxpr/ppermute | solution.py:23
  230.7 7.6 %collective-permute-start.2 = (bf16[48,2560]{1,0:T(8,128)(2,1)S(1)}, bf16[48,2560]{1,0:T(8,128)(2,1)S(1)}, u32[]{:S(2)}, u32[]{:S(2)}) collective-permute-start(bf16[48,2560]{1,0:T(8,128)(2,1)S(1)} %add_convert_fusion.23), channel_id=1, source_target_pairs={{0,1},{1,2},{2,3},{3,4},{4,5},{5,6},{6,7},{7,0},{8,9},{9,10},{10,1... | collective-permute-start | bytes 737288 | tf_op jit(solution)/shard_map/while/body/eval_jaxpr/ppermute | solution.py:23
  230.9 7.5 %collective-permute-start.3 = (bf16[48,2560]{1,0:T(8,128)(2,1)S(1)}, bf16[48,2560]{1,0:T(8,128)(2,1)S(1)}, u32[]{:S(2)}, u32[]{:S(2)}) collective-permute-start(bf16[48,2560]{1,0:T(8,128)(2,1)S(1)} %add_convert_fusion.24), channel_id=1, source_target_pairs={{0,7},{1,0},{2,1},{3,2},{4,3},{5,4},{6,5},{7,6},{8,15},{9,8},{10,9... | collective-permute-start | bytes 737288 | tf_op jit(solution)/shard_map/while/body/eval_jaxpr/ppermute | solution.py:23
  238.4 6.8 %collective-permute-start.2 = (bf16[48,2560]{1,0:T(8,128)(2,1)S(1)}, bf16[48,2560]{1,0:T(8,128)(2,1)S(1)}, u32[]{:S(2)}, u32[]{:S(2)}) collective-permute-start(bf16[48,2560]{1,0:T(8,128)(2,1)S(1)} %add_convert_fusion.23), channel_id=1, source_target_pairs={{0,1},{1,2},{2,3},{3,4},{4,5},{5,6},{6,7},{7,0},{8,9},{9,10},{10,1... | collective-permute-start | bytes 737288 | tf_op jit(solution)/shard_map/while/body/eval_jaxpr/ppermute | solution.py:23
  238.6 6.6 %collective-permute-start.3 = (bf16[48,2560]{1,0:T(8,128)(2,1)S(1)}, bf16[48,2560]{1,0:T(8,128)(2,1)S(1)}, u32[]{:S(2)}, u32[]{:S(2)}) collective-permute-start(bf16[48,2560]{1,0:T(8,128)(2,1)S(1)} %add_convert_fusion.24), channel_id=1, source_target_pairs={{0,7},{1,0},{2,1},{3,2},{4,3},{5,4},{6,5},{7,6},{8,15},{9,8},{10,9... | collective-permute-start | bytes 737288 | tf_op jit(solution)/shard_map/while/body/eval_jaxpr/ppermute | solution.py:23
  245.3 6.3 %collective-permute-start.2 = (bf16[48,2560]{1,0:T(8,128)(2,1)S(1)}, bf16[48,2560]{1,0:T(8,128)(2,1)S(1)}, u32[]{:S(2)}, u32[]{:S(2)}) collective-permute-start(bf16[48,2560]{1,0:T(8,128)(2,1)S(1)} %add_convert_fusion.23), channel_id=1, source_target_pairs={{0,1},{1,2},{2,3},{3,4},{4,5},{5,6},{6,7},{7,0},{8,9},{9,10},{10,1... | collective-permute-start | bytes 737288 | tf_op jit(solution)/shard_map/while/body/eval_jaxpr/ppermute | solution.py:23
  245.5 6.1 %collective-permute-start.3 = (bf16[48,2560]{1,0:T(8,128)(2,1)S(1)}, bf16[48,2560]{1,0:T(8,128)(2,1)S(1)}, u32[]{:S(2)}, u32[]{:S(2)}) collective-permute-start(bf16[48,2560]{1,0:T(8,128)(2,1)S(1)} %add_convert_fusion.24), channel_id=1, source_target_pairs={{0,7},{1,0},{2,1},{3,2},{4,3},{5,4},{6,5},{7,6},{8,15},{9,8},{10,9... | collective-permute-start | bytes 737288 | tf_op jit(solution)/shard_map/while/body/eval_jaxpr/ppermute | solution.py:23
  (23 other events, 213.8 us)

commit v3 on v2

--- a/solution.py
+++ b/solution.py
@@ -393,11 +393,11 @@
     up1, down1 = shift(attn_in, 1), shift(attn_in, -1)
     up2, down2 = shift(up1, 1), shift(down1, -1)
     up3, down3 = shift(up2, 1), shift(down2, -1)
-    q_a, kv_a = project([attn_in, up1, down1, up2, down2])
+    q_a, kv_a = project([attn_in, up1, down1])
+    kv_a = lax.all_gather(kv_a, "exp_1", axis=0, tiled=True)
+    (up3, down3), kv_a = tied((up3, down3), kv_a)
     far = shift(up3, 1)
-    kv_a = lax.all_gather(kv_a, "exp_1", axis=0, tiled=True)
-    far, kv_a = tied(far, kv_a)
-    q_b, kv_b = project([up3, down3, far])
+    q_b, kv_b = project([up2, down2, up3, down3, far])
     kvs = [kv_a, kv_b, swap(kv_b, "exp_1")]
     piece = attend_call([q_a, q_b], kvs, w_out, heads, rows)
     from_below, from_above = ring_scatter(

time: 255 us -> 256 us (level)
  transfers between devices with their start and end apart: 52 -> 52, of which waited for: 22 -> 22; matrix products, arithmetic and copies ran while one was open for 1% -> 1% of each run, Pallas kernels for 17% -> 16%
where the time goes in v3:
time: 256 us; the launch traced here: 253 us
  waiting for transfers between devices  98.8 us (39%)
  starting transfers between devices  74.9 us (29%)
  Pallas kernels  50.3 us (20%)
  blocking collectives  12.3 us (5%)
  local copies, waits for them, and re-layouts  8.07 us (3%)
  other arithmetic  7.42 us (3%)
    ppermute x33, waiting for transfers between devices, shift(): return lax.ppermute(value, 'seq', [(i, (i + step) % n) for i in range(n)])  66.8 us
    ppermute x33, starting transfers between devices, shift(): return lax.ppermute(value, 'seq', [(i, (i + step) % n) for i in range(n)])  51.8 us
    pallas_call x5, Pallas kernels, expert_call(): pl.pallas_call(kernel, out_shape=[jax.ShapeDtypeStruct((m1, dim), jnp.bfl...  38.2 us
    ppermute x19, waiting for transfers between devices, swap(): return lax.ppermute(value, axis, [(0, 1), (1, 0)])  32 us
    ppermute x19, starting transfers between devices, swap(): return lax.ppermute(value, axis, [(0, 1), (1, 0)])  23 us
    all_gather x1, blocking collectives, shards(): kv_a = lax.all_gather(kv_a, 'exp_1', axis=0, tiled=True)  12.3 us
    pallas_call x2, Pallas kernels, project_call(): pl.pallas_call(kernel, out_shape=[jax.ShapeDtypeStruct((m, width), jnp.bf...  7.58 us
    unnamed x42, local copies, waits for them, and re-layouts  6.33 us
  transfers between devices with their start and end apart: 52, of which 22 were waited for; matrix products, arithmetic and copies ran while one was open for 1% of the time, Pallas kernels for 16%

profile of v3, /device:TPU:1, one launch (start us, length us, event | category | flops | bytes accessed | tf_op | source)
XLA Modules:
  0.0 253.0 jit_solution(1214400272933702279)
XLA Ops:
  3.7 2.2 collective-permute-start.4
  7.6 3.9 %collective-permute-start.13 = (bf16[48,2688]{1,0:T(8,128)(2,1)S(1)}, bf16[48,2688]{1,0:T(8,128)(2,1)S(1)}, u32[]{:S(2)}, u32[]{:S(2)}) collective-permute-start(bf16[48,2688]{1,0:T(8,128)(2,1)S(1)} %pad_maximum_fusion.9), channel_id=1, source_target_pairs={{0,7},{1,0},{2,1},{3,2},{4,3},{5,4},{6,5},{7,6},{8,15},{9,8},{10,9... | collective-permute-start | bytes 774152 | tf_op jit(solution)/shard_map/ppermute | solution.py:23
  11.5 1.9 collective-permute-start.5
  15.0 3.9 %collective-permute-start.14 = (bf16[48,2688]{1,0:T(8,128)(2,1)S(1)}, bf16[48,2688]{1,0:T(8,128)(2,1)S(1)}, u32[]{:S(2)}, u32[]{:S(2)}) collective-permute-start(bf16[48,2688]{1,0:T(8,128)(2,1)S(1)} %collective-permute-done.4), channel_id=1, source_target_pairs={{0,7},{1,0},{2,1},{3,2},{4,3},{5,4},{6,5},{7,6},{8,15},{9,8},{10,9... | collective-permute-start | bytes 774152 | tf_op jit(solution)/shard_map/ppermute | solution.py:23
  19.7 5.8 %collective-permute-done.9 = bf16[48,2688]{1,0:T(8,128)(2,1)S(1)} collective-permute-done((bf16[48,2688]{1,0:T(8,128)(2,1)S(1)}, bf16[48,2688]{1,0:T(8,128)(2,1)S(1)}, u32[]{:S(2)}, u32[]{:S(2)}) %collective-permute-start.9) | collective-permute-done | bytes 258080 | tf_op jit(solution)/shard_map/ppermute | solution.py:23
  27.7 2.7 %collective-permute-start.15 = (bf16[96,2688]{1,0:T(8,128)(2,1)S(1)}, bf16[96,2688]{1,0:T(8,128)(2,1)S(1)}, u32[]{:S(2)}, u32[]{:S(2)}) collective-permute-start(bf16[96,2688]{1,0:T(8,128)(2,1)S(1)} %constant_dynamic-update-slice_fusion.2.refs_1_), channel_id=1, source_target_pairs={{0,7},{1,0},{2,1},{3,2},{4,3},{5,4},{6,5},{7,6},{8,15},{9,8},{10,9... | collective-permute-start | bytes 1548296 | tf_op jit(solution)/shard_map/ppermute | solution.py:23
  30.4 6.1 %expert.5 = (bf16[96,2560]{1,0:T(8,128)(2,1)S(1)}, bf16[96,2560]{1,0:T(8,128)(2,1)S(1)}) custom-call(s32[1]{0:T(128)} %bitcast.me_ref, bf16[96,2688]{1,0:T(8,128)(2,1)S(1)} %pad_maximum_fusion.7.refs_0_, bf16[96,2688]{1,0:T(8,128)(2,1)S(1)} %collective-permute-done.5.refs_1_, bf16[4,224,2560]{2,1,0:T(8,128)(2,1)} %bitcast.24, bf16[2,224,2560]{2,1,0:T(8,128)(2,1)} %bitcast.29), custom_call_target="tpu_custom_call" | custom-call | flops 1321205760 | bytes 8847360 | tf_op jit(solution)/shard_map/expert/pallas_call | solution.py:139
  37.8 2.5 collective-permute-done.10.refs_0_
  42.5 3.4 %collective-permute-start.16 = (bf16[96,2688]{1,0:T(8,128)(2,1)S(1)}, bf16[96,2688]{1,0:T(8,128)(2,1)S(1)}, u32[]{:S(2)}, u32[]{:S(2)}) collective-permute-start(bf16[96,2688]{1,0:T(8,128)(2,1)S(1)} %collective-permute-done.15.refs_1_), channel_id=1, source_target_pairs={{0,7},{1,0},{2,1},{3,2},{4,3},{5,4},{6,5},{7,6},{8,15},{9,8},{10,9... | collective-permute-start | bytes 1548296 | tf_op jit(solution)/shard_map/ppermute | solution.py:23
  45.9 7.4 %collective-permute-done.11.refs_0_ = bf16[96,2688]{1,0:T(8,128)(2,1)S(1)} collective-permute-done((bf16[96,2688]{1,0:T(8,128)(2,1)S(1)}, bf16[96,2688]{1,0:T(8,128)(2,1)S(1)}, u32[]{:S(2)}, u32[]{:S(2)}) %collective-permute-start.11) | collective-permute-done | bytes 516128 | tf_op jit(solution)/shard_map/ppermute | solution.py:23
  55.1 8.2 %expert.9 = (bf16[192,2560]{1,0:T(8,128)(2,1)S(1)}, bf16[192,2560]{1,0:T(8,128)(2,1)S(1)}) custom-call(s32[1]{0:T(128)} %bitcast.me_ref, bf16[96,2688]{1,0:T(8,128)(2,1)} %constant_dynamic-update-slice_fusion.refs_0_, bf16[96,2688]{1,0:T(8,128)(2,1)S(1)} %constant_dynamic-update-slice_fusion.2.refs_1_, ...), custom_call_target="tpu_custom_call" | custom-call | flops 2642411520 | bytes 10813440 | tf_op jit(solution)/shard_map/expert/pallas_call | solution.py:139
  63.3 2.7 %collective-permute-start.28 = (bf16[192,2560]{1,0:T(8,128)(2,1)S(1)}, bf16[192,2560]{1,0:T(8,128)(2,1)S(1)}, u32[]{:S(2)}, u32[]{:S(2)}) collective-permute-start(bf16[192,2560]{1,0:T(8,128)(2,1)S(1)} %get-tuple-element.226), channel_id=1, source_target_pairs={{0,8},{8,0},{1,9},{9,1},{2,10},{10,2},{3,11},{11,3},{4,12},{12,4},... | collective-permute-start | bytes 2949128 | tf_op jit(solution)/shard_map/ppermute | solution.py:18
  66.0 3.0 %collective-permute-start.17 = (bf16[48,2688]{1,0:T(8,128)(2,1)S(1)}, bf16[48,2688]{1,0:T(8,128)(2,1)S(1)}, u32[]{:S(2)}, u32[]{:S(2)}) collective-permute-start(bf16[48,2688]{1,0:T(8,128)(2,1)S(1)} %slice.155), channel_id=1, source_target_pairs={{0,7},{1,0},{2,1},{3,2},{4,3},{5,4},{6,5},{7,6},{8,15},{9,8},{10,9... | collective-permute-start | bytes 774152 | tf_op jit(solution)/shard_map/ppermute | solution.py:23
  69.1 5.5 %collective-permute-done.17 = bf16[48,2688]{1,0:T(8,128)(2,1)S(1)} collective-permute-done((bf16[48,2688]{1,0:T(8,128)(2,1)S(1)}, bf16[48,2688]{1,0:T(8,128)(2,1)S(1)}, u32[]{:S(2)}, u32[]{:S(2)}) %collective-permute-start.17) | collective-permute-done | bytes 258080 | tf_op jit(solution)/shard_map/ppermute | solution.py:23
  75.8 8.9 %expert.8 = (bf16[192,2560]{1,0:T(8,128)(2,1)S(1)}, bf16[192,2560]{1,0:T(8,128)(2,1)S(1)}) custom-call(s32[1]{0:T(128)} %bitcast.me_ref, bf16[96,2688]{1,0:T(8,128)(2,1)S(1)} %collective-permute-done.10.refs_0_, bf16[96,2688]{1,0:T(8,128)(2,1)S(1)} %collective-permute-done.15.refs_1_, bf16[192,2688]{1,0:T(8,128)(2,1)S(1)} %collective-permute-done.24.refs_2_, ...), custom_call_target="tpu_custom_call" | custom-call | flops 2642411520 | bytes 10813440 | tf_op jit(solution)/shard_map/expert/pallas_call | solution.py:139
  85.2 6.1 %expert.6 = (bf16[96,2560]{1,0:T(8,128)(2,1)S(1)}, bf16[96,2560]{1,0:T(8,128)(2,1)S(1)}) custom-call(s32[1]{0:T(128)} %bitcast.me_ref, bf16[96,2688]{1,0:T(8,128)(2,1)S(1)} %constant_dynamic-update-slice_fusion.4.refs_0_, bf16[96,2688]{1,0:T(8,128)(2,1)S(1)} %collective-permute-done.18.refs_1_, bf16[4,224,2560]{2,1,0:T(8,128)(2,1)} %bitcast.27, ...), custom_call_target="tpu_custom_call" | custom-call | flops 1321205760 | bytes 8847360 | tf_op jit(solution)/shard_map/expert/pallas_call | solution.py:139
  91.9 8.9 %expert.7 = (bf16[192,2560]{1,0:T(8,128)(2,1)S(1)}, bf16[192,2560]{1,0:T(8,128)(2,1)S(1)}) custom-call(s32[1]{0:T(128)} %bitcast.me_ref, bf16[96,2688]{1,0:T(8,128)(2,1)S(1)} %collective-permute-done.11.refs_0_, bf16[96,2688]{1,0:T(8,128)(2,1)S(1)} %collective-permute-done.16.refs_1_, bf16[192,2688]{1,0:T(8,128)(2,1)S(1)} %collective-permute-done.21.refs_2_, ...), custom_call_target="tpu_custom_call" | custom-call | flops 2642411520 | bytes 10813440 | tf_op jit(solution)/shard_map/expert/pallas_call | solution.py:139
  104.6 5.1 %collective-permute-done.20 = bf16[48,2560]{1,0:T(8,128)(2,1)S(1)} collective-permute-done((bf16[48,2560]{1,0:T(8,128)(2,1)S(1)}, bf16[48,2560]{1,0:T(8,128)(2,1)S(1)}, u32[]{:S(2)}, u32[]{:S(2)}) %collective-permute-start.20) | collective-permute-done | bytes 245792 | tf_op jit(solution)/shard_map/ppermute | solution.py:18
  111.0 9.3 %collective-permute-done.26 = bf16[96,2560]{1,0:T(8,128)(2,1)S(1)} collective-permute-done((bf16[96,2560]{1,0:T(8,128)(2,1)S(1)}, bf16[96,2560]{1,0:T(8,128)(2,1)S(1)}, u32[]{:S(2)}, u32[]{:S(2)}) %collective-permute-start.26) | collective-permute-done | bytes 491552 | tf_op jit(solution)/shard_map/ppermute | solution.py:18
  120.5 10.4 %collective-permute-done.23 = bf16[96,2560]{1,0:T(8,128)(2,1)S(1)} collective-permute-done((bf16[96,2560]{1,0:T(8,128)(2,1)S(1)}, bf16[96,2560]{1,0:T(8,128)(2,1)S(1)}, u32[]{:S(2)}, u32[]{:S(2)}) %collective-permute-start.23) | collective-permute-done | bytes 491552 | tf_op jit(solution)/shard_map/ppermute | solution.py:18
  132.6 29.8 %while.30 = (s32[]{:T(128)}, bf16[48,2560]{1,0:T(8,128)(2,1)S(1)}, bf16[48,2560]{1,0:T(8,128)(2,1)S(1)}, bf16[192,2560]{1,0:T(8,128)(2,1)S(1)}, bf16[192,2560]{1...) while((s32[]{:T(128)}, bf16[48,2560]{1,0:T(8,128)(2,1)S(1)}, ...), condition=%wide.region_2.3_spmd, body=%wide.region_1.2_spmd.sunk | while | flops 983046 | bytes 3440867 | solution.py:54
  132.8 3.4 %collective-permute-start.1 = (bf16[48,2560]{1,0:T(8,128)(2,1)S(1)}, bf16[48,2560]{1,0:T(8,128)(2,1)S(1)}, u32[]{:S(2)}, u32[]{:S(2)}) collective-permute-start(bf16[48,2560]{1,0:T(8,128)(2,1)S(1)} %add_convert_fusion.22), channel_id=1, source_target_pairs={{0,7},{1,0},{2,1},{3,2},{4,3},{5,4},{6,5},{7,6},{8,15},{9,8},{10,9... | collective-permute-start | bytes 737288 | tf_op jit(solution)/shard_map/while/body/eval_jaxpr/ppermute | solution.py:23
  136.2 5.2 %collective-permute-done = bf16[48,2560]{1,0:T(8,128)(2,1)S(1)} collective-permute-done((bf16[48,2560]{1,0:T(8,128)(2,1)S(1)}, bf16[48,2560]{1,0:T(8,128)(2,1)S(1)}, u32[]{:S(2)}, u32[]{:S(2)}) %collective-permute-start) | collective-permute-done | bytes 245792 | tf_op jit(solution)/shard_map/while/body/eval_jaxpr/ppermute | solution.py:23
  144.3 4.3 %collective-permute-done = bf16[48,2560]{1,0:T(8,128)(2,1)S(1)} collective-permute-done((bf16[48,2560]{1,0:T(8,128)(2,1)S(1)}, bf16[48,2560]{1,0:T(8,128)(2,1)S(1)}, u32[]{:S(2)}, u32[]{:S(2)}) %collective-permute-start) | collective-permute-done | bytes 245792 | tf_op jit(solution)/shard_map/while/body/eval_jaxpr/ppermute | solution.py:23
  149.9 1.7 collective-permute-start.1
  151.7 3.4 %collective-permute-done = bf16[48,2560]{1,0:T(8,128)(2,1)S(1)} collective-permute-done((bf16[48,2560]{1,0:T(8,128)(2,1)S(1)}, bf16[48,2560]{1,0:T(8,128)(2,1)S(1)}, u32[]{:S(2)}, u32[]{:S(2)}) %collective-permute-start) | collective-permute-done | bytes 245792 | tf_op jit(solution)/shard_map/while/body/eval_jaxpr/ppermute | solution.py:23
  155.2 2.0 collective-permute-start
  158.2 3.4 %collective-permute-done = bf16[48,2560]{1,0:T(8,128)(2,1)S(1)} collective-permute-done((bf16[48,2560]{1,0:T(8,128)(2,1)S(1)}, bf16[48,2560]{1,0:T(8,128)(2,1)S(1)}, u32[]{:S(2)}, u32[]{:S(2)}) %collective-permute-start) | collective-permute-done | bytes 245792 | tf_op jit(solution)/shard_map/while/body/eval_jaxpr/ppermute | solution.py:23
  166.8 3.6 %collective-permute-done.30.refs_1_ = bf16[48,2560]{1,0:T(8,128)(2,1)S(1)} collective-permute-done((bf16[48,2560]{1,0:T(8,128)(2,1)S(1)}, bf16[48,2560]{1,0:T(8,128)(2,1)S(1)}, u32[]{:S(2)}, u32[]{:S(2)}) %collective-permute-start.30) | collective-permute-done | bytes 245792 | tf_op jit(solution)/shard_map/ppermute | solution.py:23
  170.6 2.4 collective-permute-start.33
  173.1 2.1 copy-done
  175.2 3.2 %project.2 = (bf16[144,256]{1,0:T(8,128)(2,1)S(1)}, bf16[144,512]{1,0:T(8,128)(2,1)S(1)}) custom-call(bf16[48,2560]{1,0:T(8,128)(2,1)S(1)} %fusion.10.refs_0_, bf16[48,2560]{1,0:T(8,128)(2,1)S(1)} %collective-permute-done.30.refs_1_, bf16[48,2560]{1,0:T(8,128)(2,1)S(1)} %collective-permute-done.31.refs_2_, bf16[3,2560,256]{2,1,0:T(8,128)(2,1)S(1)} %bitcast.18, ...), custom_call_target="tpu_custom_call" | custom-call | flops 566231040 | bytes 4669440 | tf_op jit(solution)/shard_map/project/pallas_call | solution.py:212
  179.6 2.7 %collective-permute-start.35 = (bf16[48,2560]{1,0:T(8,128)(2,1)S(1)}, bf16[48,2560]{1,0:T(8,128)(2,1)S(1)}, u32[]{:S(2)}, u32[]{:S(2)}) collective-permute-start(bf16[48,2560]{1,0:T(8,128)(2,1)S(1)} %collective-permute-done.33.refs_1_), channel_id=1, source_target_pairs={{0,7},{1,0},{2,1},{3,2},{4,3},{5,4},{6,5},{7,6},{8,15},{9,8},{10,9... | collective-permute-start | bytes 737288 | tf_op jit(solution)/shard_map/ppermute | solution.py:23
  182.9 12.3 %all_gather.3.refs_2_ = bf16[576,512]{1,0:T(8,128)(2,1)S(1)} all-gather(bf16[288,512]{1,0:T(8,128)(2,1)S(1)} %pad_maximum_fusion.8), channel_id=1, replica_groups=mesh['set'=8,'exp_0'=2,'exp_1'=2,'seq'=8] {'exp_1'}, dimensions={0}, use_global_device_ids=true | all-gather | bytes 884736 | tf_op jit(solution)/shard_map/all_gather | solution.py:397
  195.3 7.3 %collective-permute-done.37.refs_4_ = bf16[48,2560]{1,0:T(8,128)(2,1)S(1)} collective-permute-done((bf16[48,2560]{1,0:T(8,128)(2,1)S(1)}, bf16[48,2560]{1,0:T(8,128)(2,1)S(1)}, u32[]{:S(2)}, u32[]{:S(2)}) %collective-permute-start.37) | collective-permute-done | bytes 245792 | tf_op jit(solution)/shard_map/ppermute | solution.py:23
  202.6 4.3 %project.3 = (bf16[240,256]{1,0:T(8,128)(2,1)S(1)}, bf16[240,512]{1,0:T(8,128)(2,1)S(1)}) custom-call(bf16[48,2560]{1,0:T(8,128)(2,1)S(1)} %collective-permute-done.32.refs_0_, bf16[48,2560]{1,0:T(8,128)(2,1)S(1)} %collective-permute-done.33.refs_1_, bf16[48,2560]{1,0:T(8,128)(2,1)S(1)} %collective-permute-done.34.refs_2_, ...), custom_call_target="tpu_custom_call" | custom-call | flops 943718400 | bytes 5160960 | tf_op jit(solution)/shard_map/project/pallas_call | solution.py:212
  207.9 4.1 %collective-permute-done.38 = bf16[240,512]{1,0:T(8,128)(2,1)S(1)} collective-permute-done((bf16[240,512]{1,0:T(8,128)(2,1)S(1)}, bf16[240,512]{1,0:T(8,128)(2,1)S(1)}, u32[]{:S(2)}, u32[]{:S(2)}) %collective-permute-start.38) | collective-permute-done | bytes 245792 | tf_op jit(solution)/shard_map/ppermute | solution.py:18
  212.1 3.7 %collective-permute-start.39 = (bf16[480,512]{1,0:T(8,128)(2,1)S(1)}, bf16[480,512]{1,0:T(8,128)(2,1)S(1)}, u32[]{:S(2)}, u32[]{:S(2)}) collective-permute-start(bf16[480,512]{1,0:T(8,128)(2,1)S(1)} %constant_dynamic-update-slice_fusion.6.refs_3_), channel_id=1, source_target_pairs={{0,8},{8,0},{1,9},{9,1},{2,10},{10,2},{3,11},{11,3},{4,12},{12,4},... | collective-permute-start | bytes 1474568 | tf_op jit(solution)/shard_map/ppermute | solution.py:18
  217.3 4.6 %attend.1 = (bf16[48,2560]{1,0:T(8,128)(2,1)S(1)}, bf16[48,2560]{1,0:T(8,128)(2,1)S(1)}, bf16[48,2560]{1,0:T(8,128)(2,1)S(1)}, bf16[48,2560]{1,0:T(8,128)(2,1)S(...) custom-call(bf16[144,256]{1,0:T(8,128)(2,1)S(1)} %get-tuple-element., ...), custom_call_target="tpu_custom_call" | custom-call | flops 1107296256 | bytes 4849664 | tf_op jit(solution)/shard_map/attend/pallas_call | solution.py:300
  222.9 29.3 %while.31 = (s32[]{:T(128)}, bf16[48,2560]{1,0:T(8,128)(2,1)S(1)}, bf16[48,2560]{1,0:T(8,128)(2,1)S(1)}, bf16[192,2560]{1,0:T(8,128)(2,1)S(1)}, bf16[192,2560]{1...) while((s32[]{:T(128)}, bf16[48,2560]{1,0:T(8,128)(2,1)S(1)}, ...), condition=%wide.region_5.6_spmd, body=%wide.region_4.5_spmd.sunk | while | flops 983046 | bytes 3440867 | solution.py:54
  223.1 2.7 %collective-permute-start.3 = (bf16[48,2560]{1,0:T(8,128)(2,1)S(1)}, bf16[48,2560]{1,0:T(8,128)(2,1)S(1)}, u32[]{:S(2)}, u32[]{:S(2)}) collective-permute-start(bf16[48,2560]{1,0:T(8,128)(2,1)S(1)} %add_convert_fusion.24), channel_id=1, source_target_pairs={{0,7},{1,0},{2,1},{3,2},{4,3},{5,4},{6,5},{7,6},{8,15},{9,8},{10,9... | collective-permute-start | bytes 737288 | tf_op jit(solution)/shard_map/while/body/eval_jaxpr/ppermute | solution.py:23
  225.8 5.5 %collective-permute-done.2 = bf16[48,2560]{1,0:T(8,128)(2,1)S(1)} collective-permute-done((bf16[48,2560]{1,0:T(8,128)(2,1)S(1)}, bf16[48,2560]{1,0:T(8,128)(2,1)S(1)}, u32[]{:S(2)}, u32[]{:S(2)}) %collective-permute-start.2) | collective-permute-done | bytes 245792 | tf_op jit(solution)/shard_map/while/body/eval_jaxpr/ppermute | solution.py:23
  231.6 2.7 %collective-permute-start.3 = (bf16[48,2560]{1,0:T(8,128)(2,1)S(1)}, bf16[48,2560]{1,0:T(8,128)(2,1)S(1)}, u32[]{:S(2)}, u32[]{:S(2)}) collective-permute-start(bf16[48,2560]{1,0:T(8,128)(2,1)S(1)} %add_convert_fusion.24), channel_id=1, source_target_pairs={{0,7},{1,0},{2,1},{3,2},{4,3},{5,4},{6,5},{7,6},{8,15},{9,8},{10,9... | collective-permute-start | bytes 737288 | tf_op jit(solution)/shard_map/while/body/eval_jaxpr/ppermute | solution.py:23
  234.3 4.7 %collective-permute-done.2 = bf16[48,2560]{1,0:T(8,128)(2,1)S(1)} collective-permute-done((bf16[48,2560]{1,0:T(8,128)(2,1)S(1)}, bf16[48,2560]{1,0:T(8,128)(2,1)S(1)}, u32[]{:S(2)}, u32[]{:S(2)}) %collective-permute-start.2) | collective-permute-done | bytes 245792 | tf_op jit(solution)/shard_map/while/body/eval_jaxpr/ppermute | solution.py:23
  239.2 2.7 %collective-permute-start.3 = (bf16[48,2560]{1,0:T(8,128)(2,1)S(1)}, bf16[48,2560]{1,0:T(8,128)(2,1)S(1)}, u32[]{:S(2)}, u32[]{:S(2)}) collective-permute-start(bf16[48,2560]{1,0:T(8,128)(2,1)S(1)} %add_convert_fusion.24), channel_id=1, source_target_pairs={{0,7},{1,0},{2,1},{3,2},{4,3},{5,4},{6,5},{7,6},{8,15},{9,8},{10,9... | collective-permute-start | bytes 737288 | tf_op jit(solution)/shard_map/while/body/eval_jaxpr/ppermute | solution.py:23
  242.0 3.8 %collective-permute-done.2 = bf16[48,2560]{1,0:T(8,128)(2,1)S(1)} collective-permute-done((bf16[48,2560]{1,0:T(8,128)(2,1)S(1)}, bf16[48,2560]{1,0:T(8,128)(2,1)S(1)}, u32[]{:S(2)}, u32[]{:S(2)}) %collective-permute-start.2) | collective-permute-done | bytes 245792 | tf_op jit(solution)/shard_map/while/body/eval_jaxpr/ppermute | solution.py:23
  246.0 2.7 %collective-permute-start.3 = (bf16[48,2560]{1,0:T(8,128)(2,1)S(1)}, bf16[48,2560]{1,0:T(8,128)(2,1)S(1)}, u32[]{:S(2)}, u32[]{:S(2)}) collective-permute-start(bf16[48,2560]{1,0:T(8,128)(2,1)S(1)} %add_convert_fusion.24), channel_id=1, source_target_pairs={{0,7},{1,0},{2,1},{3,2},{4,3},{5,4},{6,5},{7,6},{8,15},{9,8},{10,9... | collective-permute-start | bytes 737288 | tf_op jit(solution)/shard_map/while/body/eval_jaxpr/ppermute | solution.py:23
  248.7 3.4 %collective-permute-done.2 = bf16[48,2560]{1,0:T(8,128)(2,1)S(1)} collective-permute-done((bf16[48,2560]{1,0:T(8,128)(2,1)S(1)}, bf16[48,2560]{1,0:T(8,128)(2,1)S(1)}, u32[]{:S(2)}, u32[]{:S(2)}) %collective-permute-start.2) | collective-permute-done | bytes 245792 | tf_op jit(solution)/shard_map/while/body/eval_jaxpr/ppermute | solution.py:23
  (163 shorter events, 41.5 us)
Async XLA Ops:
  3.7 7.8 %collective-permute-start.4 = (bf16[48,2688]{1,0:T(8,128)(2,1)S(1)}, bf16[48,2688]{1,0:T(8,128)(2,1)S(1)}, u32[]{:S(2)}, u32[]{:S(2)}) collective-permute-start(bf16[48,2688]{1,0:T(8,128)(2,1)S(1)} %pad_maximum_fusion.9), channel_id=1, source_target_pairs={{0,16},{16,0},{1,17},{17,1},{2,18},{18,2},{3,19},{19,3},{4,20},{20... | collective-permute-start | bytes 774152 | tf_op jit(solution)/shard_map/ppermute | solution.py:18
  5.9 13.0 %collective-permute-start.8 = (bf16[48,2688]{1,0:T(8,128)(2,1)S(1)}, bf16[48,2688]{1,0:T(8,128)(2,1)S(1)}, u32[]{:S(2)}, u32[]{:S(2)}) collective-permute-start(bf16[48,2688]{1,0:T(8,128)(2,1)S(1)} %pad_maximum_fusion.9), channel_id=1, source_target_pairs={{0,1},{1,2},{2,3},{3,4},{4,5},{5,6},{6,7},{7,0},{8,9},{9,10},{10,1... | collective-permute-start | bytes 774152 | tf_op jit(solution)/shard_map/ppermute | solution.py:23
  7.6 18.7 %collective-permute-start.13 = (bf16[48,2688]{1,0:T(8,128)(2,1)S(1)}, bf16[48,2688]{1,0:T(8,128)(2,1)S(1)}, u32[]{:S(2)}, u32[]{:S(2)}) collective-permute-start(bf16[48,2688]{1,0:T(8,128)(2,1)S(1)} %pad_maximum_fusion.9), channel_id=1, source_target_pairs={{0,7},{1,0},{2,1},{3,2},{4,3},{5,4},{6,5},{7,6},{8,15},{9,8},{10,9... | collective-permute-start | bytes 774152 | tf_op jit(solution)/shard_map/ppermute | solution.py:23
  11.5 18.8 %collective-permute-start.5 = (bf16[96,2688]{1,0:T(8,128)(2,1)S(1)}, bf16[96,2688]{1,0:T(8,128)(2,1)S(1)}, u32[]{:S(2)}, u32[]{:S(2)}) collective-permute-start(bf16[96,2688]{1,0:T(8,128)(2,1)S(1)} %pad_maximum_fusion.7.refs_0_), channel_id=1, source_target_pairs={{0,8},{8,0},{1,9},{9,1},{2,10},{10,2},{3,11},{11,3},{4,12},{12,4},... | collective-permute-start | bytes 1548296 | tf_op jit(solution)/shard_map/ppermute | solution.py:18
  13.5 12.0 %collective-permute-start.9 = (bf16[48,2688]{1,0:T(8,128)(2,1)S(1)}, bf16[48,2688]{1,0:T(8,128)(2,1)S(1)}, u32[]{:S(2)}, u32[]{:S(2)}) collective-permute-start(bf16[48,2688]{1,0:T(8,128)(2,1)S(1)} %collective-permute-done.4), channel_id=1, source_target_pairs={{0,1},{1,2},{2,3},{3,4},{4,5},{5,6},{6,7},{7,0},{8,9},{9,10},{10,1... | collective-permute-start | bytes 774152 | tf_op jit(solution)/shard_map/ppermute | solution.py:23
  15.0 11.3 %collective-permute-start.14 = (bf16[48,2688]{1,0:T(8,128)(2,1)S(1)}, bf16[48,2688]{1,0:T(8,128)(2,1)S(1)}, u32[]{:S(2)}, u32[]{:S(2)}) collective-permute-start(bf16[48,2688]{1,0:T(8,128)(2,1)S(1)} %collective-permute-done.4), channel_id=1, source_target_pairs={{0,7},{1,0},{2,1},{3,2},{4,3},{5,4},{6,5},{7,6},{8,15},{9,8},{10,9... | collective-permute-start | bytes 774152 | tf_op jit(solution)/shard_map/ppermute | solution.py:23
  26.2 14.1 %collective-permute-start.10 = (bf16[96,2688]{1,0:T(8,128)(2,1)}, bf16[96,2688]{1,0:T(8,128)(2,1)S(1)}, u32[]{:S(2)}, u32[]{:S(2)}) collective-permute-start(bf16[96,2688]{1,0:T(8,128)(2,1)} %constant_dynamic-update-slice_fusion.refs_0_), channel_id=1, source_target_pairs={{0,1},{1,2},{2,3},{3,4},{4,5},{5,6},{6,7},{7,0},{8,9},{9,10},{10,1... | collective-permute-start | bytes 1548296 | tf_op jit(solution)/shard_map/ppermute | solution.py:23
  27.7 14.4 %collective-permute-start.15 = (bf16[96,2688]{1,0:T(8,128)(2,1)S(1)}, bf16[96,2688]{1,0:T(8,128)(2,1)S(1)}, u32[]{:S(2)}, u32[]{:S(2)}) collective-permute-start(bf16[96,2688]{1,0:T(8,128)(2,1)S(1)} %constant_dynamic-update-slice_fusion.2.refs_1_), channel_id=1, source_target_pairs={{0,7},{1,0},{2,1},{3,2},{4,3},{5,4},{6,5},{7,6},{8,15},{9,8},{10,9... | collective-permute-start | bytes 1548296 | tf_op jit(solution)/shard_map/ppermute | solution.py:23
  36.5 16.9 %collective-permute-start.6 = (bf16[96,2560]{1,0:T(8,128)(2,1)S(1)}, bf16[96,2560]{1,0:T(8,128)(2,1)S(1)}, u32[]{:S(2)}, u32[]{:S(2)}) collective-permute-start(bf16[96,2560]{1,0:T(8,128)(2,1)S(1)} %get-tuple-element.218), channel_id=1, source_target_pairs={{0,8},{8,0},{1,9},{9,1},{2,10},{10,2},{3,11},{11,3},{4,12},{12,4},... | collective-permute-start | bytes 1474568 | tf_op jit(solution)/shard_map/ppermute | solution.py:18
  40.3 13.0 %collective-permute-start.11 = (bf16[96,2688]{1,0:T(8,128)(2,1)S(1)}, bf16[96,2688]{1,0:T(8,128)(2,1)S(1)}, u32[]{:S(2)}, u32[]{:S(2)}) collective-permute-start(bf16[96,2688]{1,0:T(8,128)(2,1)S(1)} %collective-permute-done.10.refs_0_), channel_id=1, source_target_pairs={{0,1},{1,2},{2,3},{3,4},{4,5},{5,6},{6,7},{7,0},{8,9},{9,10},{10,1... | collective-permute-start | bytes 1548296 | tf_op jit(solution)/shard_map/ppermute | solution.py:23
  40.4 14.7 %collective-permute-start.27 = (bf16[192,2688]{1,0:T(8,128)(2,1)S(1)}, bf16[192,2688]{1,0:T(8,128)(2,1)S(1)}, u32[]{:S(2)}, u32[]{:S(2)}) collective-permute-start(bf16[192,2688]{1,0:T(8,128)(2,1)S(1)} %pad_maximum_fusion.4), channel_id=1, source_target_pairs={{0,8},{8,0},{1,9},{9,1},{2,10},{10,2},{3,11},{11,3},{4,12},{12,4},... | collective-permute-start | bytes 3096584 | tf_op jit(solution)/shard_map/ppermute | solution.py:18
  42.1 33.7 %collective-permute-start.24 = (bf16[192,2688]{1,0:T(8,128)(2,1)S(1)}, bf16[192,2688]{1,0:T(8,128)(2,1)S(1)}, u32[]{:S(2)}, u32[]{:S(2)}) collective-permute-start(bf16[192,2688]{1,0:T(8,128)(2,1)S(1)} %pad_maximum_fusion.3), channel_id=1, source_target_pairs={{0,8},{8,0},{1,9},{9,1},{2,10},{10,2},{3,11},{11,3},{4,12},{12,4},... | collective-permute-start | bytes 3096584 | tf_op jit(solution)/shard_map/ppermute | solution.py:18
  42.5 23.6 %collective-permute-start.16 = (bf16[96,2688]{1,0:T(8,128)(2,1)S(1)}, bf16[96,2688]{1,0:T(8,128)(2,1)S(1)}, u32[]{:S(2)}, u32[]{:S(2)}) collective-permute-start(bf16[96,2688]{1,0:T(8,128)(2,1)S(1)} %collective-permute-done.15.refs_1_), channel_id=1, source_target_pairs={{0,7},{1,0},{2,1},{3,2},{4,3},{5,4},{6,5},{7,6},{8,15},{9,8},{10,9... | collective-permute-start | bytes 1548296 | tf_op jit(solution)/shard_map/ppermute | solution.py:23
  53.3 15.7 %collective-permute-start.12 = (bf16[48,2688]{1,0:T(8,128)(2,1)S(1)}, bf16[48,2688]{1,0:T(8,128)(2,1)S(1)}, u32[]{:S(2)}, u32[]{:S(2)}) collective-permute-start(bf16[48,2688]{1,0:T(8,128)(2,1)S(1)} %slice.154), channel_id=1, source_target_pairs={{0,1},{1,2},{2,3},{3,4},{4,5},{5,6},{6,7},{7,0},{8,9},{9,10},{10,1... | collective-permute-start | bytes 774152 | tf_op jit(solution)/shard_map/ppermute | solution.py:23
  53.5 78.3 %collective-permute-start.7 = (bf16[48,2560]{1,0:T(8,128)(2,1)S(1)}, bf16[48,2560]{1,0:T(8,128)(2,1)S(1)}, u32[]{:S(2)}, u32[]{:S(2)}) collective-permute-start(bf16[48,2560]{1,0:T(8,128)(2,1)S(1)} %add_convert_fusion.15), channel_id=1, source_target_pairs={{0,16},{16,0},{1,17},{17,1},{2,18},{18,2},{3,19},{19,3},{4,20},{20... | collective-permute-start | bytes 737288 | tf_op jit(solution)/shard_map/ppermute | solution.py:18
  63.3 28.2 %collective-permute-start.28 = (bf16[192,2560]{1,0:T(8,128)(2,1)S(1)}, bf16[192,2560]{1,0:T(8,128)(2,1)S(1)}, u32[]{:S(2)}, u32[]{:S(2)}) collective-permute-start(bf16[192,2560]{1,0:T(8,128)(2,1)S(1)} %get-tuple-element.226), channel_id=1, source_target_pairs={{0,8},{8,0},{1,9},{9,1},{2,10},{10,2},{3,11},{11,3},{4,12},{12,4},... | collective-permute-start | bytes 2949128 | tf_op jit(solution)/shard_map/ppermute | solution.py:18
  66.0 8.6 %collective-permute-start.17 = (bf16[48,2688]{1,0:T(8,128)(2,1)S(1)}, bf16[48,2688]{1,0:T(8,128)(2,1)S(1)}, u32[]{:S(2)}, u32[]{:S(2)}) collective-permute-start(bf16[48,2688]{1,0:T(8,128)(2,1)S(1)} %slice.155), channel_id=1, source_target_pairs={{0,7},{1,0},{2,1},{3,2},{4,3},{5,4},{6,5},{7,6},{8,15},{9,8},{10,9... | collective-permute-start | bytes 774152 | tf_op jit(solution)/shard_map/ppermute | solution.py:23
  74.6 10.6 %collective-permute-start.18 = (bf16[96,2688]{1,0:T(8,128)(2,1)S(1)}, bf16[96,2688]{1,0:T(8,128)(2,1)S(1)}, u32[]{:S(2)}, u32[]{:S(2)}) collective-permute-start(bf16[96,2688]{1,0:T(8,128)(2,1)S(1)} %constant_dynamic-update-slice_fusion.4.refs_0_), channel_id=1, source_target_pairs={{0,8},{8,0},{1,9},{9,1},{2,10},{10,2},{3,11},{11,3},{4,12},{12,4},... | collective-permute-start | bytes 1548296 | tf_op jit(solution)/shard_map/ppermute | solution.py:18
  75.7 16.2 %collective-permute-start.21 = (bf16[192,2688]{1,0:T(8,128)(2,1)S(1)}, bf16[192,2688]{1,0:T(8,128)(2,1)S(1)}, u32[]{:S(2)}, u32[]{:S(2)}) collective-permute-start(bf16[192,2688]{1,0:T(8,128)(2,1)S(1)} %pad_maximum_fusion.2), channel_id=1, source_target_pairs={{0,8},{8,0},{1,9},{9,1},{2,10},{10,2},{3,11},{11,3},{4,12},{12,4},... | collective-permute-start | bytes 3096584 | tf_op jit(solution)/shard_map/ppermute | solution.py:18
  84.7 19.5 %collective-permute-start.25 = (bf16[192,2560]{1,0:T(8,128)(2,1)S(1)}, bf16[192,2560]{1,0:T(8,128)(2,1)S(1)}, u32[]{:S(2)}, u32[]{:S(2)}) collective-permute-start(bf16[192,2560]{1,0:T(8,128)(2,1)S(1)} %get-tuple-element.224), channel_id=1, source_target_pairs={{0,8},{8,0},{1,9},{9,1},{2,10},{10,2},{3,11},{11,3},{4,12},{12,4},... | collective-permute-start | bytes 2949128 | tf_op jit(solution)/shard_map/ppermute | solution.py:18
  91.3 10.3 %collective-permute-start.19 = (bf16[96,2560]{1,0:T(8,128)(2,1)S(1)}, bf16[96,2560]{1,0:T(8,128)(2,1)S(1)}, u32[]{:S(2)}, u32[]{:S(2)}) collective-permute-start(bf16[96,2560]{1,0:T(8,128)(2,1)S(1)} %get-tuple-element.220), channel_id=1, source_target_pairs={{0,8},{8,0},{1,9},{9,1},{2,10},{10,2},{3,11},{11,3},{4,12},{12,4},... | collective-permute-start | bytes 1474568 | tf_op jit(solution)/shard_map/ppermute | solution.py:18
  91.6 12.4 %collective-permute-start.29 = (bf16[96,2560]{1,0:T(8,128)(2,1)S(1)}, bf16[96,2560]{1,0:T(8,128)(2,1)S(1)}, u32[]{:S(2)}, u32[]{:S(2)}) collective-permute-start(bf16[96,2560]{1,0:T(8,128)(2,1)S(1)} %add_convert_fusion.4), channel_id=1, source_target_pairs={{0,16},{16,0},{1,17},{17,1},{2,18},{18,2},{3,19},{19,3},{4,20},{20... | collective-permute-start | bytes 1474568 | tf_op jit(solution)/shard_map/ppermute | solution.py:18
  100.8 9.1 %collective-permute-start.22 = (bf16[192,2560]{1,0:T(8,128)(2,1)S(1)}, bf16[192,2560]{1,0:T(8,128)(2,1)S(1)}, u32[]{:S(2)}, u32[]{:S(2)}) collective-permute-start(bf16[192,2560]{1,0:T(8,128)(2,1)S(1)} %get-tuple-element.222), channel_id=1, source_target_pairs={{0,8},{8,0},{1,9},{9,1},{2,10},{10,2},{3,11},{11,3},{4,12},{12,4},... | collective-permute-start | bytes 2949128 | tf_op jit(solution)/shard_map/ppermute | solution.py:18
  101.7 8.1 %collective-permute-start.20 = (bf16[48,2560]{1,0:T(8,128)(2,1)S(1)}, bf16[48,2560]{1,0:T(8,128)(2,1)S(1)}, u32[]{:S(2)}, u32[]{:S(2)}) collective-permute-start(bf16[48,2560]{1,0:T(8,128)(2,1)S(1)} %add_convert_fusion.14), channel_id=1, source_target_pairs={{0,16},{16,0},{1,17},{17,1},{2,18},{18,2},{3,19},{19,3},{4,20},{20... | collective-permute-start | bytes 737288 | tf_op jit(solution)/shard_map/ppermute | solution.py:18
  104.3 15.9 %collective-permute-start.26 = (bf16[96,2560]{1,0:T(8,128)(2,1)S(1)}, bf16[96,2560]{1,0:T(8,128)(2,1)S(1)}, u32[]{:S(2)}, u32[]{:S(2)}) collective-permute-start(bf16[96,2560]{1,0:T(8,128)(2,1)S(1)} %add_convert_fusion.5), channel_id=1, source_target_pairs={{0,16},{16,0},{1,17},{17,1},{2,18},{18,2},{3,19},{19,3},{4,20},{20... | collective-permute-start | bytes 1474568 | tf_op jit(solution)/shard_map/ppermute | solution.py:18
  110.0 20.8 %collective-permute-start.23 = (bf16[96,2560]{1,0:T(8,128)(2,1)S(1)}, bf16[96,2560]{1,0:T(8,128)(2,1)S(1)}, u32[]{:S(2)}, u32[]{:S(2)}) collective-permute-start(bf16[96,2560]{1,0:T(8,128)(2,1)S(1)} %add_convert_fusion.6), channel_id=1, source_target_pairs={{0,16},{16,0},{1,17},{17,1},{2,18},{18,2},{3,19},{19,3},{4,20},{20... | collective-permute-start | bytes 1474568 | tf_op jit(solution)/shard_map/ppermute | solution.py:18
  132.6 8.8 %collective-permute-start = (bf16[48,2560]{1,0:T(8,128)(2,1)S(1)}, bf16[48,2560]{1,0:T(8,128)(2,1)S(1)}, u32[]{:S(2)}, u32[]{:S(2)}) collective-permute-start(bf16[48,2560]{1,0:T(8,128)(2,1)S(1)} %add_convert_fusion.21), channel_id=1, source_target_pairs={{0,1},{1,2},{2,3},{3,4},{4,5},{5,6},{6,7},{7,0},{8,9},{9,10},{10,1... | collective-permute-start | bytes 737288 | tf_op jit(solution)/shard_map/while/body/eval_jaxpr/ppermute | solution.py:23
  132.8 8.6 %collective-permute-start.1 = (bf16[48,2560]{1,0:T(8,128)(2,1)S(1)}, bf16[48,2560]{1,0:T(8,128)(2,1)S(1)}, u32[]{:S(2)}, u32[]{:S(2)}) collective-permute-start(bf16[48,2560]{1,0:T(8,128)(2,1)S(1)} %add_convert_fusion.22), channel_id=1, source_target_pairs={{0,7},{1,0},{2,1},{3,2},{4,3},{5,4},{6,5},{7,6},{8,15},{9,8},{10,9... | collective-permute-start | bytes 737288 | tf_op jit(solution)/shard_map/while/body/eval_jaxpr/ppermute | solution.py:23
  141.5 7.2 %collective-permute-start = (bf16[48,2560]{1,0:T(8,128)(2,1)S(1)}, bf16[48,2560]{1,0:T(8,128)(2,1)S(1)}, u32[]{:S(2)}, u32[]{:S(2)}) collective-permute-start(bf16[48,2560]{1,0:T(8,128)(2,1)S(1)} %add_convert_fusion.21), channel_id=1, source_target_pairs={{0,1},{1,2},{2,3},{3,4},{4,5},{5,6},{6,7},{7,0},{8,9},{9,10},{10,1... | collective-permute-start | bytes 737288 | tf_op jit(solution)/shard_map/while/body/eval_jaxpr/ppermute | solution.py:23
  143.1 5.6 %collective-permute-start.1 = (bf16[48,2560]{1,0:T(8,128)(2,1)S(1)}, bf16[48,2560]{1,0:T(8,128)(2,1)S(1)}, u32[]{:S(2)}, u32[]{:S(2)}) collective-permute-start(bf16[48,2560]{1,0:T(8,128)(2,1)S(1)} %add_convert_fusion.22), channel_id=1, source_target_pairs={{0,7},{1,0},{2,1},{3,2},{4,3},{5,4},{6,5},{7,6},{8,15},{9,8},{10,9... | collective-permute-start | bytes 737288 | tf_op jit(solution)/shard_map/while/body/eval_jaxpr/ppermute | solution.py:23
  148.8 6.3 %collective-permute-start = (bf16[48,2560]{1,0:T(8,128)(2,1)S(1)}, bf16[48,2560]{1,0:T(8,128)(2,1)S(1)}, u32[]{:S(2)}, u32[]{:S(2)}) collective-permute-start(bf16[48,2560]{1,0:T(8,128)(2,1)S(1)} %add_convert_fusion.21), channel_id=1, source_target_pairs={{0,1},{1,2},{2,3},{3,4},{4,5},{5,6},{6,7},{7,0},{8,9},{9,10},{10,1... | collective-permute-start | bytes 737288 | tf_op jit(solution)/shard_map/while/body/eval_jaxpr/ppermute | solution.py:23
  149.9 5.2 %collective-permute-start.1 = (bf16[48,2560]{1,0:T(8,128)(2,1)S(1)}, bf16[48,2560]{1,0:T(8,128)(2,1)S(1)}, u32[]{:S(2)}, u32[]{:S(2)}) collective-permute-start(bf16[48,2560]{1,0:T(8,128)(2,1)S(1)} %add_convert_fusion.22), channel_id=1, source_target_pairs={{0,7},{1,0},{2,1},{3,2},{4,3},{5,4},{6,5},{7,6},{8,15},{9,8},{10,9... | collective-permute-start | bytes 737288 | tf_op jit(solution)/shard_map/while/body/eval_jaxpr/ppermute | solution.py:23
  155.2 6.5 %collective-permute-start = (bf16[48,2560]{1,0:T(8,128)(2,1)S(1)}, bf16[48,2560]{1,0:T(8,128)(2,1)S(1)}, u32[]{:S(2)}, u32[]{:S(2)}) collective-permute-start(bf16[48,2560]{1,0:T(8,128)(2,1)S(1)} %add_convert_fusion.21), channel_id=1, source_target_pairs={{0,1},{1,2},{2,3},{3,4},{4,5},{5,6},{6,7},{7,0},{8,9},{9,10},{10,1... | collective-permute-start | bytes 737288 | tf_op jit(solution)/shard_map/while/body/eval_jaxpr/ppermute | solution.py:23
  164.1 6.3 %collective-permute-start.30 = (bf16[48,2560]{1,0:T(8,128)(2,1)S(1)}, bf16[48,2560]{1,0:T(8,128)(2,1)S(1)}, u32[]{:S(2)}, u32[]{:S(2)}) collective-permute-start(bf16[48,2560]{1,0:T(8,128)(2,1)S(1)} %fusion.10.refs_0_), channel_id=1, source_target_pairs={{0,1},{1,2},{2,3},{3,4},{4,5},{5,6},{6,7},{7,0},{8,9},{9,10},{10,1... | collective-permute-start | bytes 737288 | tf_op jit(solution)/shard_map/ppermute | solution.py:23
  170.4 9.2 %collective-permute-start.32 = (bf16[48,2560]{1,0:T(8,128)(2,1)S(1)}, bf16[48,2560]{1,0:T(8,128)(2,1)S(1)}, u32[]{:S(2)}, u32[]{:S(2)}) collective-permute-start(bf16[48,2560]{1,0:T(8,128)(2,1)S(1)} %collective-permute-done.30.refs_1_), channel_id=1, source_target_pairs={{0,1},{1,2},{2,3},{3,4},{4,5},{5,6},{6,7},{7,0},{8,9},{9,10},{10,1... | collective-permute-start | bytes 737288 | tf_op jit(solution)/shard_map/ppermute | solution.py:23
  170.6 8.9 %collective-permute-start.33 = (bf16[48,2560]{1,0:T(8,128)(2,1)S(1)}, bf16[48,2560]{1,0:T(8,128)(2,1)S(1)}, u32[]{:S(2)}, u32[]{:S(2)}) collective-permute-start(bf16[48,2560]{1,0:T(8,128)(2,1)S(1)} %collective-permute-done.31.refs_2_), channel_id=1, source_target_pairs={{0,7},{1,0},{2,1},{3,2},{4,3},{5,4},{6,5},{7,6},{8,15},{9,8},{10,9... | collective-permute-start | bytes 737288 | tf_op jit(solution)/shard_map/ppermute | solution.py:23
  179.6 15.6 %collective-permute-start.34 = (bf16[48,2560]{1,0:T(8,128)(2,1)S(1)}, bf16[48,2560]{1,0:T(8,128)(2,1)S(1)}, u32[]{:S(2)}, u32[]{:S(2)}) collective-permute-start(bf16[48,2560]{1,0:T(8,128)(2,1)S(1)} %collective-permute-done.32.refs_0_), channel_id=1, source_target_pairs={{0,1},{1,2},{2,3},{3,4},{4,5},{5,6},{6,7},{7,0},{8,9},{9,10},{10,1... | collective-permute-start | bytes 737288 | tf_op jit(solution)/shard_map/ppermute | solution.py:23
  179.6 15.6 %collective-permute-start.35 = (bf16[48,2560]{1,0:T(8,128)(2,1)S(1)}, bf16[48,2560]{1,0:T(8,128)(2,1)S(1)}, u32[]{:S(2)}, u32[]{:S(2)}) collective-permute-start(bf16[48,2560]{1,0:T(8,128)(2,1)S(1)} %collective-permute-done.33.refs_1_), channel_id=1, source_target_pairs={{0,7},{1,0},{2,1},{3,2},{4,3},{5,4},{6,5},{7,6},{8,15},{9,8},{10,9... | collective-permute-start | bytes 737288 | tf_op jit(solution)/shard_map/ppermute | solution.py:23
  195.2 7.4 %collective-permute-start.37 = (bf16[48,2560]{1,0:T(8,128)(2,1)S(1)}, bf16[48,2560]{1,0:T(8,128)(2,1)S(1)}, u32[]{:S(2)}, u32[]{:S(2)}) collective-permute-start(bf16[48,2560]{1,0:T(8,128)(2,1)S(1)} %collective-permute-done.34.refs_2_), channel_id=1, source_target_pairs={{0,1},{1,2},{2,3},{3,4},{4,5},{5,6},{6,7},{7,0},{8,9},{9,10},{10,1... | collective-permute-start | bytes 737288 | tf_op jit(solution)/shard_map/ppermute | solution.py:23
  212.1 5.2 %collective-permute-start.39 = (bf16[480,512]{1,0:T(8,128)(2,1)S(1)}, bf16[480,512]{1,0:T(8,128)(2,1)S(1)}, u32[]{:S(2)}, u32[]{:S(2)}) collective-permute-start(bf16[480,512]{1,0:T(8,128)(2,1)S(1)} %constant_dynamic-update-slice_fusion.6.refs_3_), channel_id=1, source_target_pairs={{0,8},{8,0},{1,9},{9,1},{2,10},{10,2},{3,11},{11,3},{4,12},{12,4},... | collective-permute-start | bytes 1474568 | tf_op jit(solution)/shard_map/ppermute | solution.py:18
  222.9 8.4 %collective-permute-start.2 = (bf16[48,2560]{1,0:T(8,128)(2,1)S(1)}, bf16[48,2560]{1,0:T(8,128)(2,1)S(1)}, u32[]{:S(2)}, u32[]{:S(2)}) collective-permute-start(bf16[48,2560]{1,0:T(8,128)(2,1)S(1)} %add_convert_fusion.23), channel_id=1, source_target_pairs={{0,1},{1,2},{2,3},{3,4},{4,5},{5,6},{6,7},{7,0},{8,9},{9,10},{10,1... | collective-permute-start | bytes 737288 | tf_op jit(solution)/shard_map/while/body/eval_jaxpr/ppermute | solution.py:23
  223.1 8.3 %collective-permute-start.3 = (bf16[48,2560]{1,0:T(8,128)(2,1)S(1)}, bf16[48,2560]{1,0:T(8,128)(2,1)S(1)}, u32[]{:S(2)}, u32[]{:S(2)}) collective-permute-start(bf16[48,2560]{1,0:T(8,128)(2,1)S(1)} %add_convert_fusion.24), channel_id=1, source_target_pairs={{0,7},{1,0},{2,1},{3,2},{4,3},{5,4},{6,5},{7,6},{8,15},{9,8},{10,9... | collective-permute-start | bytes 737288 | tf_op jit(solution)/shard_map/while/body/eval_jaxpr/ppermute | solution.py:23
  231.4 7.6 %collective-permute-start.2 = (bf16[48,2560]{1,0:T(8,128)(2,1)S(1)}, bf16[48,2560]{1,0:T(8,128)(2,1)S(1)}, u32[]{:S(2)}, u32[]{:S(2)}) collective-permute-start(bf16[48,2560]{1,0:T(8,128)(2,1)S(1)} %add_convert_fusion.23), channel_id=1, source_target_pairs={{0,1},{1,2},{2,3},{3,4},{4,5},{5,6},{6,7},{7,0},{8,9},{9,10},{10,1... | collective-permute-start | bytes 737288 | tf_op jit(solution)/shard_map/while/body/eval_jaxpr/ppermute | solution.py:23
  231.6 7.4 %collective-permute-start.3 = (bf16[48,2560]{1,0:T(8,128)(2,1)S(1)}, bf16[48,2560]{1,0:T(8,128)(2,1)S(1)}, u32[]{:S(2)}, u32[]{:S(2)}) collective-permute-start(bf16[48,2560]{1,0:T(8,128)(2,1)S(1)} %add_convert_fusion.24), channel_id=1, source_target_pairs={{0,7},{1,0},{2,1},{3,2},{4,3},{5,4},{6,5},{7,6},{8,15},{9,8},{10,9... | collective-permute-start | bytes 737288 | tf_op jit(solution)/shard_map/while/body/eval_jaxpr/ppermute | solution.py:23
  239.1 6.7 %collective-permute-start.2 = (bf16[48,2560]{1,0:T(8,128)(2,1)S(1)}, bf16[48,2560]{1,0:T(8,128)(2,1)S(1)}, u32[]{:S(2)}, u32[]{:S(2)}) collective-permute-start(bf16[48,2560]{1,0:T(8,128)(2,1)S(1)} %add_convert_fusion.23), channel_id=1, source_target_pairs={{0,1},{1,2},{2,3},{3,4},{4,5},{5,6},{6,7},{7,0},{8,9},{9,10},{10,1... | collective-permute-start | bytes 737288 | tf_op jit(solution)/shard_map/while/body/eval_jaxpr/ppermute | solution.py:23
  239.2 6.6 %collective-permute-start.3 = (bf16[48,2560]{1,0:T(8,128)(2,1)S(1)}, bf16[48,2560]{1,0:T(8,128)(2,1)S(1)}, u32[]{:S(2)}, u32[]{:S(2)}) collective-permute-start(bf16[48,2560]{1,0:T(8,128)(2,1)S(1)} %add_convert_fusion.24), channel_id=1, source_target_pairs={{0,7},{1,0},{2,1},{3,2},{4,3},{5,4},{6,5},{7,6},{8,15},{9,8},{10,9... | collective-permute-start | bytes 737288 | tf_op jit(solution)/shard_map/while/body/eval_jaxpr/ppermute | solution.py:23
  245.8 6.3 %collective-permute-start.2 = (bf16[48,2560]{1,0:T(8,128)(2,1)S(1)}, bf16[48,2560]{1,0:T(8,128)(2,1)S(1)}, u32[]{:S(2)}, u32[]{:S(2)}) collective-permute-start(bf16[48,2560]{1,0:T(8,128)(2,1)S(1)} %add_convert_fusion.23), channel_id=1, source_target_pairs={{0,1},{1,2},{2,3},{3,4},{4,5},{5,6},{6,7},{7,0},{8,9},{9,10},{10,1... | collective-permute-start | bytes 737288 | tf_op jit(solution)/shard_map/while/body/eval_jaxpr/ppermute | solution.py:23
  246.0 6.2 %collective-permute-start.3 = (bf16[48,2560]{1,0:T(8,128)(2,1)S(1)}, bf16[48,2560]{1,0:T(8,128)(2,1)S(1)}, u32[]{:S(2)}, u32[]{:S(2)}) collective-permute-start(bf16[48,2560]{1,0:T(8,128)(2,1)S(1)} %add_convert_fusion.24), channel_id=1, source_target_pairs={{0,7},{1,0},{2,1},{3,2},{4,3},{5,4},{6,5},{7,6},{8,15},{9,8},{10,9... | collective-permute-start | bytes 737288 | tf_op jit(solution)/shard_map/while/body/eval_jaxpr/ppermute | solution.py:23
  (23 other events, 209.4 us)
